TPU v7x, 128 devices: a whole 4x4x4 slice. The times are simulated.
128 devices in a mesh: grp: 4 (over z), feat: 32 (over x, y, core).
Axes of the slice: x: 4, y: 4, z: 4, core: 2. Of those that a mesh axis runs over, the one named last changes fastest.
Arguments:
- features: bfloat16 [4, 768, 768, 128], P('grp', None, 'feat'), may hold values from -6 to 6
- adj_tiles: bfloat16 [4, 384, 128, 128], P('grp'), may hold values from -0.4375 to 0.4375
- tile_rows: int32 [4, 384], P('grp'), may hold values from 0 to 255, as said below
- tile_cols: int32 [4, 384], P('grp'), may hold values from 0 to 767
- self_blocks: int32 [4, 256], P('grp'), may hold values from 0 to 767, as said below
- weight: bfloat16 [1536, 1024], replicated, may hold values from -0.15625 to 0.15625
- proj_bias: float32 [1024], replicated, may hold values from -0.5 to 0.5
- cotangent: bfloat16 [4, 32768, 1024], P('grp', 'feat'), may hold values from -0.015625 to 0.015625
Outputs:
- hidden: bfloat16 [4, 32768, 1024], P('grp', 'feat')
- weight_grad: float32 [1536, 1024], P('feat')
Inputs may be any that keep to these rules, and one draw needn't show every extreme that they name: `tile_rows`: within each minibatch the row blocks are in nondecreasing order and every row block 0 to 255 has at least one tile. `self_blocks`: within each minibatch the blocks are distinct.
All inputs are finite; a program needn't handle non-finite values.
Results may differ from a plain program's by a relative error of at most 0.0038.
Values may be sent and summed in bfloat16 or wider, within the bound.
No kernel may reach another device: no remote copies, remote signals or barrier semaphores. Data moves between devices by JAX's collectives and lax.ppermute only.
A program may use at most 128 MiB of HBM per device.

v0:
```python
import jax
import jax.numpy as jnp
from jax import lax
from jax.sharding import PartitionSpec as P


def elu_act(value):
    return jnp.where(value > 0, value, jnp.expm1(jnp.minimum(value, 0.0)))


def per_device(
    features, adj_tiles, tile_rows, tile_cols, self_blocks, weight, proj_bias, cotangent
):
    local_blocks = features[0]
    col_count = local_blocks.shape[1]
    tile_side = local_blocks.shape[2]
    tile_count = adj_tiles.shape[1]
    block_count = self_blocks.shape[1]
    picked = jnp.take(local_blocks, tile_cols[0], axis=0)
    contrib = jnp.einsum("tfs,tds->tfd", picked, adj_tiles[0], preferred_element_type=jnp.float32)
    onehot = (tile_rows[0][None, :] == jnp.arange(block_count, dtype=jnp.int32)[:, None]).astype(
        jnp.float32
    )
    summed = jnp.dot(
        onehot, contrib.reshape(tile_count, col_count * tile_side), precision=lax.Precision.HIGHEST
    )
    aggregate = summed.reshape(block_count, col_count, tile_side).astype(jnp.bfloat16)
    self_feat = jnp.take(local_blocks, self_blocks[0], axis=0)
    stacked = jnp.stack([self_feat, aggregate], axis=1)
    owned = lax.all_to_all(stacked, "feat", split_axis=0, concat_axis=2, tiled=True)
    own_blocks = owned.shape[0]
    combined = owned.reshape(own_blocks, 2 * owned.shape[2], tile_side)
    preact = jnp.einsum("rcd,ch->rdh", combined, weight, preferred_element_type=jnp.float32)
    preact = preact.reshape(own_blocks * tile_side, weight.shape[1]) + proj_bias
    hidden = elu_act(preact).astype(jnp.bfloat16)
    pre_grad = (cotangent[0].astype(jnp.float32) * jnp.exp(jnp.minimum(preact, 0.0))).astype(
        jnp.bfloat16
    )
    grad_rows3 = pre_grad.reshape(own_blocks, tile_side, weight.shape[1])
    row_share = combined.shape[1] // lax.axis_size("feat")
    partial_grad = jnp.einsum(
        "rcd,rdh->ch", combined, grad_rows3, preferred_element_type=jnp.float32
    )
    totals = lax.psum(partial_grad, ("grp", "feat"))
    weight_grad = lax.dynamic_slice_in_dim(totals, lax.axis_index("feat") * row_share, row_share, 0)
    return (hidden[None], weight_grad)


def solution(mesh):
    return jax.shard_map(
        per_device,
        mesh=mesh,
        in_specs=(
            P("grp", None, "feat", None),
            P("grp", None, None, None),
            P("grp", None),
            P("grp", None),
            P("grp", None),
            P(),
            P(),
            P("grp", "feat", None),
        ),
        out_specs=(P("grp", "feat", None), P("feat", None)),
        check_vma=False,
    )
```

profile of v0, /device:TPU:0, one launch (start us, length us, event | category | flops | bytes accessed | tf_op | source)
XLA Modules:
  0.0 285.6 jit_solution(16939328353353296432)
XLA Ops:
  7.2 0.0 copy-start
  7.2 0.0 all-reduce.2.cloned.1.call-start
  7.2 0.8 fusion.12
  8.1 0.7 reduce.1
  8.8 4.9 %gather_fusion.1 = bf16[384,24,128]{2,1,0:T(8,128)(2,1)} fusion(bf16[768,24,128]{2,1,0:T(8,128)(2,1)} %bitcast.51, s32[1024]{0:T(1024)S(1)} %pad_clamp_fusion), kind=kCustom, calls=%fused_computation.1 | custom fusion | bytes 4720128 | tf_op jit(solution)/shard_map/jit(_take)/gather | solution.py:19
  13.7 14.1 %fusion = f32[384,24,128]{2,1,0:T(8,128)} fusion(bf16[1,384,128,128]{3,2,1,0:T(8,128)(2,1)} %param.9, bf16[384,24,128]{2,1,0:T(8,128)(2,1)} %gather_fusion.1, pred[384]{0:T(512)(128)(4,1)S(1)} %compare_and_fusion), kind=kOutput, calls=%fused_computation.2 | convolution fusion | flops 303169536 | bytes 19661184 | tf_op jit(solution)/shard_map/tfs,tds->tfd/dot_general | solution.py:20
  27.8 5.5 %copy.24 = f32[48,8,24,128]{3,1,2,0:T(8,128)} copy(f32[48,8,24,128]{3,2,1,0:T(8,128)} %bitcast.47) | data formatting | bytes 9437184
  33.3 0.0 copy-start.3
  33.3 0.0 copy-start.4
  33.3 6.1 %copy.17 = f32[3072,384]{1,0:T(8,128)} copy(f32[3072,384]{0,1:T(8,128)} %bitcast.46) | data formatting | bytes 9437184 | tf_op jit(solution)/shard_map/dot_general | solution.py:24
  39.4 0.0 copy-done.3
  39.4 0.0 copy-done.4
  39.4 4.4 %gather_fusion = bf16[256,24,128]{2,1,0:T(8,128)(2,1)} fusion(bf16[768,24,128]{2,1,0:T(8,128)(2,1)} %bitcast.52, s32[1024]{0:T(1024)S(1)} %pad_clamp_fusion.1), kind=kCustom, calls=%fused_computation | custom fusion | bytes 3146752 | tf_op jit(solution)/shard_map/jit(_take)/gather | solution.py:28
  43.8 0.0 copy-start.2
  43.8 5.4 %fusion.7 = bf16[256,1,24,128]{3,0,2,1:T(8,128)(2,1)S(1)} fusion(f32[24,128,384]{2,1,0:T(8,128)} %bitcast.45, s32[384]{0:T(512)S(1)} %reduce), kind=kOutput, calls=%fused_computation.16 | convolution fusion | flops 3624763392 | bytes 6292992 | tf_op jit(solution)/shard_map/dot_general | solution.py:24
  49.2 0.0 copy-done.2
  49.2 0.3 bitcast_select_fusion
  49.5 0.3 pad_maximum_fusion
  49.8 2.0 copy.18
  51.8 46.5 %all_to_all.15 = bf16[256,2,24,128]{3,2,1,0:T(8,128)(2,1)S(1)} all-to-all(bf16[256,2,24,128]{3,2,1,0:T(8,128)(2,1)S(1)} %copy.18), channel_id=1, replica_groups=mesh['grp'=4,'feat'=32] {'feat'}, dimensions={0} | all-to-all | bytes 6291456 | tf_op jit(solution)/shard_map/all_to_all | solution.py:30
  98.3 2.5 copy.19
  100.8 0.0 copy-start.5
  100.8 4.7 %copy.20 = bf16[8,128,1536]{2,1,0:T(8,128)(2,1)} copy(bf16[8,128,1536]{1,2,0:T(8,128)(2,1)} %bitcast.48) | data formatting | bytes 6291456 | tf_op jit(solution)/shard_map/rcd,ch->rdh/dot_general | solution.py:33
  105.5 0.0 copy-done
  105.5 0.0 copy-done.5
  105.5 0.0 copy-start.1
  105.5 8.5 %fusion.3 = (bf16[1024,1024]{1,0:T(8,128)(2,1)S(1)}, bf16[1,1024,1024]{2,1,0:T(8,128)(2,1)}) fusion(bf16[1,1024,1024]{2,1,0:T(8,128)(2,1)} %param.15, f32[1024]{0:T(1024)S(1)} %copy-done.5, bf16[1024,1536]{1,0:T(8,128)(2,1)} %bitcast.53, bf16[1536,1024]{1,0:T(8,128)(2,1)S(1)} %copy-done), kind=kOutput, calls=%fused_computation.9 | convolution fusion | flops 3229614080 | bytes 12587008 | tf_op jit(solution)/shard_map/rcd,ch->rdh/dot_general | solution.py:33
  114.0 0.0 copy-done.1
  114.0 5.2 %convolution_bitcast_fusion = f32[1536,1024]{1,0:T(8,128)} fusion(bf16[8,1536,128]{2,1,0:T(8,128)(2,1)S(1)} %bitcast.49, bf16[8,128,1024]{2,1,0:T(8,128)(2,1)S(1)} %bitcast.56), kind=kOutput, calls=%fused_computation.6 | convolution fusion | flops 3221225472 | bytes 11534336 | tf_op jit(solution)/shard_map/rcd,rdh->ch/dot_general | solution.py:41
  119.2 0.0 all-reduce.2.cloned.1.call-update
  119.3 157.8 %all-reduce.2.cloned.1.call-done = f32[1536,1024]{1,0:T(8,128)} async-done(((f32[1536,1024]{1,0:T(8,128)}), f32[1536,1024]{1,0:T(8,128)}) %all-reduce.2.cloned.1.call-update) | async-done | bytes 6291472 | tf_op jit(solution)/shard_map/psum | solution.py:44
  277.1 1.6 constant_dynamic-slice_fusion
  (6 shorter events, 0.1 us)
Async XLA Ops:
  7.2 98.3 %copy-start = (bf16[1536,1024]{1,0:T(8,128)(2,1)S(1)}, bf16[1536,1024]{1,0:T(8,128)(2,1)}, u32[]{:S(2)}) copy-start(bf16[1536,1024]{1,0:T(8,128)(2,1)} %param.13) | copy-start | bytes 9437188
  7.2 269.9 %all-reduce.2.cloned.1.call-start = ((), (), s32[]{:S(2)}) async-start(), calls=%async_computation.1 | async-start | bytes 12582912 | tf_op jit(solution)/shard_map/psum | solution.py:44
  33.3 6.1 %copy-start.3 = (s32[1,384]{1,0:T(1,128)S(1)}, s32[1,384]{1,0:T(1,128)}, u32[]{:S(2)}) copy-start(s32[1,384]{1,0:T(1,128)} %param.10) | copy-start | bytes 4612
  33.3 6.1 %copy-start.4 = (s32[1,256]{1,0:T(1,128)S(1)}, s32[1,256]{1,0:T(1,128)}, u32[]{:S(2)}) copy-start(s32[1,256]{1,0:T(1,128)} %param.12) | copy-start | bytes 3076
  43.8 5.4 %copy-start.2 = (bf16[256,24,128]{2,1,0:T(8,128)(2,1)S(1)}, bf16[256,24,128]{2,1,0:T(8,128)(2,1)}, u32[]{:S(2)}) copy-start(bf16[256,24,128]{2,1,0:T(8,128)(2,1)} %gather_fusion) | copy-start | bytes 4718596
  100.8 4.7 %copy-start.5 = (f32[1024]{0:T(1024)S(1)}, f32[1024]{0:T(1024)}, u32[]{:S(2)}) copy-start(f32[1024]{0:T(1024)} %param.14) | copy-start | bytes 12292
  105.5 8.5 %copy-start.1 = (bf16[32,8,2,24,128]{4,3,0,2,1:T(8,128)(2,1)S(1)}, bf16[32,8,2,24,128]{4,3,0,2,1:T(8,128)(2,1)}, u32[]{:S(2)}) copy-start(bf16[32,8,2,24,128]{4,3,0,2,1:T(8,128)(2,1)} %copy.19) | copy-start | bytes 9437188
Sparse Core Ops, SparseCore 0:
  119.4 157.6 all-reduce.1
where the time goes:
time: 286 us
  waiting for transfers between devices  158 us (55%)
  blocking collectives  46.5 us (16%)
  matrix products  33.2 us (12%)
  local copies, waits for them, and re-layouts  31.7 us (11%)
  between operations  14.1 us (5%)
    psum x1, waiting for transfers between devices, per_device(): totals = lax.psum(partial_grad, ('grp', 'feat'))  158 us
    all_to_all x1, blocking collectives, per_device(): lax.all_to_all(stacked, 'feat', split_axis=0, concat_axis=2, tiled=True)  46.5 us
    dot_general x1, matrix products, per_device(): jnp.einsum('tfs,tds->tfd', picked, adj_tiles[0], preferred_element_type=j...  14.1 us
    dot_general x1, matrix products, per_device(): jnp.einsum('rcd,ch->rdh', combined, weight, preferred_element_type=jnp.fl...  8.52 us
    dot_general x1, local copies, waits for them, and re-layouts, per_device(): jnp.dot(onehot, contrib.reshape(tile_count, col_count * tile_side), preci...  6.06 us
  transfers between devices with their start and end apart: 1, of which 1 were waited for; matrix products, arithmetic and copies ran while one was open for 0% of the time, Pallas kernels for 0%

commit v1 on v0

v1 whole, which is shorter than its diff:
```python
import functools

import jax
import jax.numpy as jnp
from jax import lax
from jax.experimental import pallas as pl
from jax.experimental.pallas import tpu as pltpu
from jax.sharding import Mesh, PartitionSpec as P

BF = jnp.bfloat16
F32 = jnp.float32
VMEM_LIMIT = 56 << 20


def gather_body(blocks_ref, feat_ref, out_ref, sem):
    count = out_ref.shape[0]

    def start(r, carry):
        pltpu.make_async_copy(feat_ref.at[blocks_ref[r]], out_ref.at[r], sem).start()
        return carry

    lax.fori_loop(0, count, start, 0, unroll=8)
    pltpu.make_async_copy(feat_ref.at[pl.ds(0, count)], out_ref, sem).wait()


def gather_self(blocks, feat):
    count = blocks.shape[0]
    return pl.pallas_call(
        gather_body,
        out_shape=jax.ShapeDtypeStruct((count,) + feat.shape[1:], feat.dtype),
        grid_spec=pltpu.PrefetchScalarGridSpec(
            num_scalar_prefetch=1,
            grid=(1,),
            in_specs=[pl.BlockSpec(memory_space=pl.ANY)],
            out_specs=pl.BlockSpec((count,) + feat.shape[1:], lambda i, b: (0, 0, 0)),
            scratch_shapes=[pltpu.SemaphoreType.DMA(())],
        ),
        compiler_params=pltpu.CompilerParams(vmem_limit_bytes=VMEM_LIMIT),
        name="gather_self",
    )(blocks, feat)


def aggregate_body(unroll, rows_ref, cols_ref, feat_ref, adj_ref, out_ref, acc_ref, part_ref):
    step = pl.program_id(0)
    tiles = adj_ref.shape[0]
    base = step * tiles

    @pl.when(step == 0)
    def _():
        acc_ref[...] = jnp.zeros_like(acc_ref)

    def multiply(k, carry):
        for u in range(unroll):
            local = k * unroll + u
            part_ref[local] = lax.dot_general(
                feat_ref[cols_ref[base + local]],
                adj_ref[local],
                (((1,), (1,)), ((), ())),
                preferred_element_type=F32,
            )
        return carry

    lax.fori_loop(0, tiles // unroll, multiply, 0)

    def add(k, acc):
        for u in range(unroll):
            local = k * unroll + u
            tile = base + local
            row = rows_ref[tile]
            same = jnp.logical_and(tile > 0, rows_ref[jnp.maximum(tile - 1, 0)] == row)
            keep = jnp.where(same, 1.0, 0.0).astype(F32)
            acc = part_ref[local] + acc * keep
            out_ref[row] = acc.astype(BF)
        return acc

    acc_ref[...] = lax.fori_loop(0, tiles // unroll, add, acc_ref[...])


def aggregate_tiles(rows, cols, feat, adj, nrb, steps=8, unroll=12):
    count, side, _ = adj.shape
    width = feat.shape[1]
    return pl.pallas_call(
        functools.partial(aggregate_body, unroll),
        out_shape=jax.ShapeDtypeStruct((nrb, width, side), BF),
        grid_spec=pltpu.PrefetchScalarGridSpec(
            num_scalar_prefetch=2,
            grid=(steps,),
            in_specs=[
                pl.BlockSpec(feat.shape, lambda i, a, b: (0, 0, 0), pipeline_mode=pl.Buffered(1)),
                pl.BlockSpec((count // steps, side, side), lambda i, a, b: (i, 0, 0)),
            ],
            out_specs=pl.BlockSpec((nrb, width, side), lambda i, a, b: (0, 0, 0)),
            scratch_shapes=[
                pltpu.VMEM((width, side), F32),
                pltpu.VMEM((count // steps, width, side), F32),
            ],
        ),
        compiler_params=pltpu.CompilerParams(
            vmem_limit_bytes=VMEM_LIMIT, dimension_semantics=("arbitrary",)
        ),
        name="aggregate_tiles",
    )(rows, cols, feat, adj)


def dense_body(
    core_ref, self_ref, agg_ref, weight_ref, bias_ref, cot_ref, hidden_ref, send_ref, keep_ref,
    comb_ref, grad_ref
):
    sources, own, width, side = self_ref.shape
    half = sources * width
    for r in range(own):
        cols = pl.ds(r * side, side)
        comb_ref[0:half, cols] = self_ref[:, r].reshape(half, side)
        comb_ref[half:, cols] = agg_ref[:, r].reshape(half, side)
    chunk = 4 * side
    for m in range(own // 4):
        rows = pl.ds(m * chunk, chunk)
        pre = lax.dot_general(
            comb_ref[:, rows], weight_ref[...], (((0,), (0,)), ((), ())), preferred_element_type=F32
        )
        pre = pre + bias_ref[...]
        decay = jnp.exp(jnp.minimum(pre, 0.0))
        hidden_ref[rows, :] = jnp.where(pre > 0, pre, decay - 1.0).astype(BF)
        grad_ref[rows, :] = (cot_ref[rows, :].astype(F32) * decay).astype(BF)
    core = core_ref[0]
    blocks, share, hid = send_ref.shape
    for dest, out_ref in ((1 - core, send_ref), (core, keep_ref)):
        for b in range(0, blocks, 4):
            lhs = jnp.concatenate(
                [comb_ref[pl.ds(pl.multiple_of((2 * (b + i) + dest) * share, share), share), :] for i in range(4)],
                axis=0,
            )
            part = jnp.dot(lhs, grad_ref[...], preferred_element_type=F32)
            out_ref[b:b + 4] = part.reshape(4, share, hid).astype(out_ref.dtype)


def dense_layer(core, own_self, own_agg, weight, bias, cot):
    nodes, hid = cot.shape
    channels = weight.shape[0]
    share = channels // 32
    return pl.pallas_call(
        dense_body,
        out_shape=(
            jax.ShapeDtypeStruct((nodes, hid), BF),
            jax.ShapeDtypeStruct((16, share, hid), BF),
            jax.ShapeDtypeStruct((16, share, hid), F32),
        ),
        in_specs=[pl.BlockSpec(memory_space=pltpu.SMEM)] + [pl.BlockSpec(memory_space=pltpu.VMEM)] * 5,
        out_specs=(pl.BlockSpec(memory_space=pltpu.VMEM),) * 3,
        scratch_shapes=[pltpu.VMEM((channels, nodes), BF), pltpu.VMEM((nodes, hid), BF)],
        compiler_params=pltpu.CompilerParams(vmem_limit_bytes=VMEM_LIMIT),
        name="dense_layer",
    )(core, own_self, own_agg, weight, bias, cot)


FEAT = ("x", "y", "core")


def per_device(
    features, adj_tiles, tile_rows, tile_cols, self_blocks, weight, proj_bias, cotangent
):
    feat = features[0]
    width, side = feat.shape[1:]
    nrb = self_blocks.shape[1]
    mine = gather_self(self_blocks[0], feat)
    own_self = lax.all_to_all(mine, FEAT, 0, 0, tiled=True)
    agg = aggregate_tiles(tile_rows[0], tile_cols[0], feat, adj_tiles[0], nrb)
    own_agg = lax.all_to_all(agg, FEAT, 0, 0, tiled=True)
    shape = (32, nrb // 32, width, side)
    core = lax.axis_index("core").astype(jnp.int32).reshape(1)
    hidden, send, keep = dense_layer(
        core, own_self.reshape(shape), own_agg.reshape(shape), weight, proj_bias[None], cotangent[0]
    )
    other = lax.ppermute(send, "core", [(0, 1), (1, 0)])
    pair = (keep + other.astype(F32)).astype(BF)
    pieces = lax.all_to_all(pair, ("x", "y"), 0, 0, tiled=True)
    part = jnp.sum(pieces.astype(F32), axis=0)
    totals = lax.all_gather(part, "grp", axis=0)
    return hidden[None], jnp.sum(totals, axis=0)


def solution(mesh):
    names = ("grp", "x", "y", "core")
    fine = Mesh(mesh.devices.reshape(4, 4, 4, 2), names)
    return jax.shard_map(
        per_device,
        mesh=fine,
        in_specs=(
            P("grp", None, FEAT, None),
            P("grp", None, None, None),
            P("grp", None),
            P("grp", None),
            P("grp", None),
            P(),
            P(),
            P("grp", FEAT, None),
        ),
        out_specs=(P("grp", FEAT, None), P(FEAT, None)),
        check_vma=False,
    )
```

time: 286 us -> 142 us (0.50)
  waiting for transfers between devices: 158 us -> 46.1 us
  Pallas kernels: 0 us -> 33.7 us
  matrix products: 33.2 us -> 0 us
  local copies, waits for them, and re-layouts: 31.7 us -> 2.31 us
  between operations: 14.1 us -> 0.67 us
  starting transfers between devices: 0.04 us -> 11.4 us
  blocking collectives: 46.5 us -> 41.2 us
  other arithmetic: 2.21 us -> 6.07 us
    psum x1 -> x0, waiting for transfers between devices: 158 us -> none  [per_device(): totals = lax.psum(partial_grad, ('grp', 'feat'))]
    all_to_all x0 -> x2, waiting for transfers between devices: none -> 42.5 us  [the longest x1 23.1 us: per_device(): own_self = lax.all_to_all(mine, FEAT, 0, 0, tiled=True)]
    pallas_call x0 -> x3, Pallas kernels: none -> 33.7 us  [the longest x1 16.7 us: aggregate_tiles(): pl.pallas_call(functools.partial(aggregate_body, unroll), out_shape=jax.S...]
    dot_general x4 -> x0, matrix products: 33.2 us -> none  [the longest x1 14.1 us: per_device(): jnp.einsum('tfs,tds->tfd', picked, adj_tiles[0], preferred_element_type=j...]
    all_to_all x1, blocking collectives: 46.5 us -> 25.9 us  [per_device(): pieces = lax.all_to_all(pair, ('x', 'y'), 0, 0, tiled=True)]
    all_gather x0 -> x1, blocking collectives: none -> 15.3 us  [per_device(): totals = lax.all_gather(part, 'grp', axis=0)]
    all_to_all x0 -> x2, starting transfers between devices: none -> 11.4 us  [the longest x1 7.4 us: per_device(): own_agg = lax.all_to_all(agg, FEAT, 0, 0, tiled=True)]
    dot_general x2 -> x0, local copies, waits for them, and re-layouts: 10.8 us -> none  [the longest x1 6.06 us: per_device(): jnp.dot(onehot, contrib.reshape(tile_count, col_count * tile_side), preci...]
  transfers between devices with their start and end apart: 1 -> 3, of which waited for: 1 -> 3; matrix products, arithmetic and copies ran while one was open for 0% -> 0% of each run, Pallas kernels for 0% -> 3%
where the time goes in v1:
time: 142 us; the launch traced here: 141 us
  waiting for transfers between devices  46.1 us (32%)
  blocking collectives  41.2 us (29%)
  Pallas kernels  33.7 us (24%)
  starting transfers between devices  11.4 us (8%)
  other arithmetic  6.07 us (4%)
  local copies, waits for them, and re-layouts  2.31 us (2%)
    all_to_all x1, blocking collectives, per_device(): pieces = lax.all_to_all(pair, ('x', 'y'), 0, 0, tiled=True)  25.9 us
    all_to_all x1, waiting for transfers between devices, per_device(): own_self = lax.all_to_all(mine, FEAT, 0, 0, tiled=True)  23.1 us
    all_to_all x1, waiting for transfers between devices, per_device(): own_agg = lax.all_to_all(agg, FEAT, 0, 0, tiled=True)  19.4 us
    pallas_call x1, Pallas kernels, aggregate_tiles(): pl.pallas_call(functools.partial(aggregate_body, unroll), out_shape=jax.S...  16.7 us
    all_gather x1, blocking collectives, per_device(): totals = lax.all_gather(part, 'grp', axis=0)  15.3 us
    pallas_call x1, Pallas kernels, dense_layer(): pl.pallas_call(dense_body, out_shape=(jax.ShapeDtypeStruct((nodes, hid),...  13.3 us
    all_to_all x1, starting transfers between devices, per_device(): own_agg = lax.all_to_all(agg, FEAT, 0, 0, tiled=True)  7.4 us
    all_to_all x1, starting transfers between devices, per_device(): own_self = lax.all_to_all(mine, FEAT, 0, 0, tiled=True)  3.97 us
  transfers between devices with their start and end apart: 3, of which 3 were waited for; matrix products, arithmetic and copies ran while one was open for 0% of the time, Pallas kernels for 3%

profile of v1, /device:TPU:0, one launch (start us, length us, event | category | flops | bytes accessed | tf_op | source)
XLA Modules:
  0.0 141.5 jit_solution(11605054520641519127)
XLA Ops:
  0.6 1.3 reduce.rows_ref
  1.9 1.3 reduce.1.cols_ref
  3.2 16.7 %aggregate_tiles.1 = bf16[256,24,128]{2,1,0:T(8,128)(2,1)} custom-call(s32[384]{0:T(512)} %reduce.rows_ref, s32[384]{0:T(512)} %reduce.1.cols_ref, bf16[768,24,128]{2,1,0:T(8,128)(2,1)} %bitcast.10, bf16[384,128,128]{2,1,0:T(8,128)(2,1)} %bitcast.12), custom_call_target="tpu_custom_call" | custom-call | tf_op jit(solution)/shard_map/aggregate_tiles/pallas_call | solution.py:82
  19.9 7.4 %all-to-all-start.1 = ((bf16[256,24,128]{2,1,0:T(8,128)(2,1)}), bf16[256,24,128]{2,1,0:T(8,128)(2,1)S(1)}, u32[]{:S(2)}, u32[]{:S(2)}) async-start(bf16[256,24,128]{2,1,0:T(8,128)(2,1)} %aggregate_tiles.1), calls=%async_computation.1 | async-start | bytes 3145728 | tf_op jit(solution)/shard_map/all_to_all | solution.py:168
  27.3 3.7 %gather_self.1 = bf16[256,24,128]{2,1,0:T(8,128)(2,1)} custom-call(s32[256]{0:T(256)} %bitcast.18, bf16[768,24,128]{2,1,0:T(8,128)(2,1)} %bitcast.11), custom_call_target="tpu_custom_call" | custom-call | tf_op jit(solution)/shard_map/gather_self/pallas_call | solution.py:28
  31.0 19.4 %all-to-all-done.1 = bf16[256,24,128]{2,1,0:T(8,128)(2,1)S(1)} async-done(((bf16[256,24,128]{2,1,0:T(8,128)(2,1)}), bf16[256,24,128]{2,1,0:T(8,128)(2,1)S(1)}, u32[]{:S(2)}, u32[]{:S(2)}) %all-to-all-start.1) | async-done | bytes 1572896 | tf_op jit(solution)/shard_map/all_to_all | solution.py:168
  50.4 0.0 copy-start
  50.4 1.2 copy-done
  51.6 4.0 %all-to-all-start = ((bf16[256,24,128]{2,1,0:T(8,128)(2,1)}), bf16[256,24,128]{2,1,0:T(8,128)(2,1)S(1)}, u32[]{:S(2)}, u32[]{:S(2)}) async-start(bf16[256,24,128]{2,1,0:T(8,128)(2,1)} %gather_self.1), calls=%async_computation | async-start | bytes 3145728 | tf_op jit(solution)/shard_map/all_to_all | solution.py:166
  55.6 23.1 %all-to-all-done = bf16[256,24,128]{2,1,0:T(8,128)(2,1)S(1)} async-done(((bf16[256,24,128]{2,1,0:T(8,128)(2,1)}), bf16[256,24,128]{2,1,0:T(8,128)(2,1)S(1)}, u32[]{:S(2)}, u32[]{:S(2)}) %all-to-all-start) | async-done | bytes 1572896 | tf_op jit(solution)/shard_map/all_to_all | solution.py:166
  78.7 0.0 copy-start.1
  78.7 1.1 copy-done.1
  79.8 13.3 %dense_layer.1 = (bf16[1024,1024]{1,0:T(8,128)(2,1)}, bf16[16,48,1024]{2,1,0:T(8,128)(2,1)}, f32[16,48,1024]{2,1,0:T(8,128)}) custom-call(s32[1]{0:T(128)} %bitcast.core_ref, bf16[32,8,24,128]{3,2,1,0:T(8,128)(2,1)} %bitcast.14, bf16[32,8,24,128]{3,2,1,0:T(8,128)(2,1)} %bitcast.13, bf16[1536,1024]{1,0:T(8,128)(2,1)} %weight_ref.1, f32[1,1024]{1,0:T(1,128)} %bitcast.17, ...), custom_call_target="tpu_custom_call" | custom-call | tf_op jit(solution)/shard_map/dense_layer/pallas_call | solution.py:141
  93.1 0.0 collective-permute-start
  93.1 3.6 %collective-permute-done = bf16[16,48,1024]{2,1,0:T(8,128)(2,1)S(1)} collective-permute-done((bf16[16,48,1024]{2,1,0:T(8,128)(2,1)}, bf16[16,48,1024]{2,1,0:T(8,128)(2,1)S(1)}, u32[]{:S(2)}, u32[]{:S(2)}) %collective-permute-start) | collective-permute-done | bytes 1572896 | tf_op jit(solution)/shard_map/ppermute | solution.py:174
  96.7 2.5 %add_convert_fusion = bf16[16,48,1024]{2,1,0:T(8,128)(2,1)S(1)} fusion(f32[16,48,1024]{2,1,0:T(8,128)} %get-tuple-element.6, bf16[16,48,1024]{2,1,0:T(8,128)(2,1)S(1)} %collective-permute-done), kind=kLoop, calls=%fused_computation.1 | loop fusion | flops 2359296 | bytes 6291456 | tf_op jit(solution)/shard_map/convert_element_type | solution.py:175
  99.3 25.9 %all_to_all.15 = bf16[16,48,1024]{2,1,0:T(8,128)(2,1)S(1)} all-to-all(bf16[16,48,1024]{2,1,0:T(8,128)(2,1)S(1)} %add_convert_fusion), channel_id=1, replica_groups=mesh['grp'=4,'x'=4,'y'=4,'core'=2] {'x','y'}, dimensions={0} | all-to-all | bytes 3145728 | tf_op jit(solution)/shard_map/all_to_all | solution.py:176
  125.2 0.3 convert_reduce_fusion
  125.5 15.3 %all-gather = f32[192,1024]{1,0:T(8,128)S(1)} all-gather(f32[48,1024]{1,0:T(8,128)S(1)} %convert_reduce_fusion), channel_id=2, replica_groups=mesh['grp'=4,'x'=4,'y'=4,'core'=2] {'grp'}, dimensions={0}, use_global_device_ids=true | all-gather | bytes 983040 | tf_op jit(solution)/shard_map/all_gather | solution.py:178
  140.8 0.7 reduce_sum.19
Async XLA Ops:
  19.9 30.5 %all-to-all-start.1 = ((bf16[256,24,128]{2,1,0:T(8,128)(2,1)}), bf16[256,24,128]{2,1,0:T(8,128)(2,1)S(1)}, u32[]{:S(2)}, u32[]{:S(2)}) async-start(bf16[256,24,128]{2,1,0:T(8,128)(2,1)} %aggregate_tiles.1), calls=%async_computation.1 | async-start | bytes 3145728 | tf_op jit(solution)/shard_map/all_to_all | solution.py:168
  50.4 1.2 copy-start
  51.6 27.1 %all-to-all-start = ((bf16[256,24,128]{2,1,0:T(8,128)(2,1)}), bf16[256,24,128]{2,1,0:T(8,128)(2,1)S(1)}, u32[]{:S(2)}, u32[]{:S(2)}) async-start(bf16[256,24,128]{2,1,0:T(8,128)(2,1)} %gather_self.1), calls=%async_computation | async-start | bytes 3145728 | tf_op jit(solution)/shard_map/all_to_all | solution.py:166
  78.7 1.1 copy-start.1
  93.1 3.6 %collective-permute-start = (bf16[16,48,1024]{2,1,0:T(8,128)(2,1)}, bf16[16,48,1024]{2,1,0:T(8,128)(2,1)S(1)}, u32[]{:S(2)}, u32[]{:S(2)}) collective-permute-start(bf16[16,48,1024]{2,1,0:T(8,128)(2,1)} %get-tuple-element.7), channel_id=1, source_target_pairs={{0,1},{1,0},{2,3},{3,2},{4,5},{5,4},{6,7},{7,6},{8,9},{9,8},{10,11... | collective-permute-start | bytes 4718600 | tf_op jit(solution)/shard_map/ppermute | solution.py:174

commit v2 on v1

--- a/solution.py
+++ b/solution.py
@@ -16,7 +16,7 @@
     count = out_ref.shape[0]
 
     def start(r, carry):
-        pltpu.make_async_copy(feat_ref.at[blocks_ref[r]], out_ref.at[r], sem).start()
+        pltpu.make_async_copy(feat_ref.at[blocks_ref[0, r]], out_ref.at[r], sem).start()
         return carry
 
     lax.fori_loop(0, count, start, 0, unroll=8)
@@ -24,7 +24,7 @@
 
 
 def gather_self(blocks, feat):
-    count = blocks.shape[0]
+    count = blocks.shape[1]
     return pl.pallas_call(
         gather_body,
         out_shape=jax.ShapeDtypeStruct((count,) + feat.shape[1:], feat.dtype),
@@ -53,7 +53,7 @@
         for u in range(unroll):
             local = k * unroll + u
             part_ref[local] = lax.dot_general(
-                feat_ref[cols_ref[base + local]],
+                feat_ref[cols_ref[0, base + local]],
                 adj_ref[local],
                 (((1,), (1,)), ((), ())),
                 preferred_element_type=F32,
@@ -66,8 +66,8 @@
         for u in range(unroll):
             local = k * unroll + u
             tile = base + local
-            row = rows_ref[tile]
-            same = jnp.logical_and(tile > 0, rows_ref[jnp.maximum(tile - 1, 0)] == row)
+            row = rows_ref[0, tile]
+            same = jnp.logical_and(tile > 0, rows_ref[0, jnp.maximum(tile - 1, 0)] == row)
             keep = jnp.where(same, 1.0, 0.0).astype(F32)
             acc = part_ref[local] + acc * keep
             out_ref[row] = acc.astype(BF)
@@ -98,13 +98,18 @@
         compiler_params=pltpu.CompilerParams(
             vmem_limit_bytes=VMEM_LIMIT, dimension_semantics=("arbitrary",)
         ),
+        cost_estimate=pl.CostEstimate(
+            flops=2 * count * width * side * side,
+            transcendentals=0,
+            bytes_accessed=2 * (feat.size + adj.size + nrb * width * side),
+        ),
         name="aggregate_tiles",
     )(rows, cols, feat, adj)
 
 
 def dense_body(
-    core_ref, self_ref, agg_ref, weight_ref, bias_ref, cot_ref, hidden_ref, send_ref, keep_ref,
-    comb_ref, grad_ref
+    place_ref, self_ref, agg_ref, weight_ref, bias_ref, cot_ref,
+    hidden_ref, send0_ref, send1_ref, keep0_ref, keep1_ref, comb_ref, grad_ref,
 ):
     sources, own, width, side = self_ref.shape
     half = sources * width
@@ -122,35 +127,55 @@
         decay = jnp.exp(jnp.minimum(pre, 0.0))
         hidden_ref[rows, :] = jnp.where(pre > 0, pre, decay - 1.0).astype(BF)
         grad_ref[rows, :] = (cot_ref[rows, :].astype(F32) * decay).astype(BF)
-    core = core_ref[0]
-    blocks, share, hid = send_ref.shape
-    for dest, out_ref in ((1 - core, send_ref), (core, keep_ref)):
-        for b in range(0, blocks, 4):
-            lhs = jnp.concatenate(
-                [comb_ref[pl.ds(pl.multiple_of((2 * (b + i) + dest) * share, share), share), :] for i in range(4)],
-                axis=0,
-            )
-            part = jnp.dot(lhs, grad_ref[...], preferred_element_type=F32)
-            out_ref[b:b + 4] = part.reshape(4, share, hid).astype(out_ref.dtype)
-
-
-def dense_layer(core, own_self, own_agg, weight, bias, cot):
+    x, y, core = place_ref[0], place_ref[1], place_ref[2]
+    hid = cot_ref.shape[1]
+    share = comb_ref.shape[0] // 32
+
+    def block(dx, dy, dest):
+        first = (8 * ((x + dx) % 4) + 2 * ((y + dy) % 4) + dest) * share
+        return comb_ref[pl.ds(pl.multiple_of(first, share), share), :]
+
+    outs = ((send0_ref, send1_ref), (keep0_ref, keep1_ref))
+    for dest, refs in zip((1 - core, core), outs):
+        for part in range(2):
+            pairs = [(k, j) if part == 0 else (j, k) for k in range(4) for j in range(4)]
+            lhs = jnp.concatenate([block(dx, dy, dest) for dx, dy in pairs], axis=0)
+            cols = pl.ds(part * (hid // 2), hid // 2)
+            total = jnp.dot(lhs, grad_ref[:, cols], preferred_element_type=F32)
+            refs[part][...] = total.reshape(refs[part].shape).astype(refs[part].dtype)
+
+
+def dense_layer(place, own_self, own_agg, weight, bias, cot):
     nodes, hid = cot.shape
     channels = weight.shape[0]
-    share = channels // 32
+    piece = (4, channels // 8, hid // 2)
+    vmem = pl.BlockSpec(memory_space=pltpu.VMEM)
     return pl.pallas_call(
         dense_body,
         out_shape=(
             jax.ShapeDtypeStruct((nodes, hid), BF),
-            jax.ShapeDtypeStruct((16, share, hid), BF),
-            jax.ShapeDtypeStruct((16, share, hid), F32),
-        ),
-        in_specs=[pl.BlockSpec(memory_space=pltpu.SMEM)] + [pl.BlockSpec(memory_space=pltpu.VMEM)] * 5,
-        out_specs=(pl.BlockSpec(memory_space=pltpu.VMEM),) * 3,
+            jax.ShapeDtypeStruct(piece, BF),
+            jax.ShapeDtypeStruct(piece, BF),
+            jax.ShapeDtypeStruct(piece, F32),
+            jax.ShapeDtypeStruct(piece, F32),
+        ),
+        in_specs=[pl.BlockSpec(memory_space=pltpu.SMEM)] + [vmem] * 5,
+        out_specs=(vmem,) * 5,
         scratch_shapes=[pltpu.VMEM((channels, nodes), BF), pltpu.VMEM((nodes, hid), BF)],
         compiler_params=pltpu.CompilerParams(vmem_limit_bytes=VMEM_LIMIT),
         name="dense_layer",
-    )(core, own_self, own_agg, weight, bias, cot)
+    )(place, own_self, own_agg, weight, bias, cot)
+
+
+def shift(value, axis, k):
+    return lax.ppermute(value, axis, [(i, (i + k) % 4) for i in range(4)])
+
+
+def exchange(parts, axis):
+    total = parts[0].astype(F32)
+    for k in (1, 2, 3):
+        total = total + shift(parts[k].astype(BF), axis, k).astype(F32)
+    return total
 
 
 FEAT = ("x", "y", "core")
@@ -162,21 +187,28 @@
     feat = features[0]
     width, side = feat.shape[1:]
     nrb = self_blocks.shape[1]
-    mine = gather_self(self_blocks[0], feat)
+    mine = gather_self(self_blocks, feat)
+    feat, mine = lax.optimization_barrier((feat, mine))
     own_self = lax.all_to_all(mine, FEAT, 0, 0, tiled=True)
-    agg = aggregate_tiles(tile_rows[0], tile_cols[0], feat, adj_tiles[0], nrb)
+    agg = aggregate_tiles(tile_rows, tile_cols, feat, adj_tiles[0], nrb)
     own_agg = lax.all_to_all(agg, FEAT, 0, 0, tiled=True)
     shape = (32, nrb // 32, width, side)
-    core = lax.axis_index("core").astype(jnp.int32).reshape(1)
-    hidden, send, keep = dense_layer(
-        core, own_self.reshape(shape), own_agg.reshape(shape), weight, proj_bias[None], cotangent[0]
+    place = jnp.stack([lax.axis_index(a) for a in FEAT]).astype(jnp.int32)
+    hidden, send0, send1, keep0, keep1 = dense_layer(
+        place, own_self.reshape(shape), own_agg.reshape(shape), weight, proj_bias[None], cotangent[0]
     )
-    other = lax.ppermute(send, "core", [(0, 1), (1, 0)])
-    pair = (keep + other.astype(F32)).astype(BF)
-    pieces = lax.all_to_all(pair, ("x", "y"), 0, 0, tiled=True)
-    part = jnp.sum(pieces.astype(F32), axis=0)
-    totals = lax.all_gather(part, "grp", axis=0)
-    return hidden[None], jnp.sum(totals, axis=0)
+    share, half = weight.shape[0] // 32, weight.shape[1] // 2
+    swap = [(0, 1), (1, 0)]
+    totals = []
+    for send, keep, first, second in ((send0, keep0, "x", "y"), (send1, keep1, "y", "x")):
+        pair = keep + lax.ppermute(send, "core", swap).astype(F32)
+        once = exchange([pair[k] for k in range(4)], first).reshape(4, share, half)
+        totals.append(exchange([once[k] for k in range(4)], second))
+    mine = jnp.concatenate(totals, axis=1).astype(BF)
+    n1, n2, n3 = (shift(mine, "grp", -k).astype(F32) for k in (1, 2, 3))
+    odd = lax.axis_index("grp") % 2 == 1
+    total = (mine.astype(F32) + jnp.where(odd, n3, n1)) + (n2 + jnp.where(odd, n1, n3))
+    return hidden[None], total
 
 
 def solution(mesh):

time: 142 us -> 125 us (0.88)
  blocking collectives: 41.2 us -> 0 us
  starting transfers between devices: 11.4 us -> 33.4 us
  waiting for transfers between devices: 46.1 us -> 49.9 us
  other arithmetic: 6.07 us -> 3.79 us
    all_to_all x1 -> x0, blocking collectives: 25.9 us -> none  [per_device(): pieces = lax.all_to_all(pair, ('x', 'y'), 0, 0, tiled=True)]
    ppermute x1 -> x17, starting transfers between devices: 0.01 us -> 22 us  [the longest x15 21.5 us: shift(): return lax.ppermute(value, axis, [(i, (i + k) % 4) for i in range(4)])]
    ppermute x1 -> x17, waiting for transfers between devices: 3.62 us -> 21 us  [the longest x15 19 us: shift(): return lax.ppermute(value, axis, [(i, (i + k) % 4) for i in range(4)])]
    all_to_all x1, waiting for transfers between devices: 23.1 us -> 6.41 us  [per_device(): own_self = lax.all_to_all(mine, FEAT, 0, 0, tiled=True)]
    all_gather x1 -> x0, blocking collectives: 15.3 us -> none  [per_device(): totals = lax.all_gather(part, 'grp', axis=0)]
    all_to_all x1, starting transfers between devices: 3.97 us -> 7.41 us  [per_device(): own_self = lax.all_to_all(mine, FEAT, 0, 0, tiled=True)]
    all_to_all x1, starting transfers between devices: 7.4 us -> 3.97 us  [per_device(): own_agg = lax.all_to_all(agg, FEAT, 0, 0, tiled=True)]
    all_to_all x1, waiting for transfers between devices: 19.4 us -> 22.5 us  [per_device(): own_agg = lax.all_to_all(agg, FEAT, 0, 0, tiled=True)]
  transfers between devices with their start and end apart: 3 -> 19, of which waited for: 3 -> 9; matrix products, arithmetic and copies ran while one was open for 0% -> 3% of each run, Pallas kernels for 3% -> 13%
where the time goes in v2:
time: 125 us; the launch traced here: 124 us
  waiting for transfers between devices  49.9 us (40%)
  Pallas kernels  33.8 us (27%)
  starting transfers between devices  33.4 us (27%)
  other arithmetic  3.79 us (3%)
  local copies, waits for them, and re-layouts  2.44 us (2%)
    all_to_all x1, waiting for transfers between devices, per_device(): own_agg = lax.all_to_all(agg, FEAT, 0, 0, tiled=True)  22.5 us
    ppermute x15, starting transfers between devices, shift(): return lax.ppermute(value, axis, [(i, (i + k) % 4) for i in range(4)])  21.5 us
    ppermute x15, waiting for transfers between devices, shift(): return lax.ppermute(value, axis, [(i, (i + k) % 4) for i in range(4)])  19 us
    pallas_call x1, Pallas kernels, aggregate_tiles(): pl.pallas_call(functools.partial(aggregate_body, unroll), out_shape=jax.S...  16.7 us
    pallas_call x1, Pallas kernels, dense_layer(): pl.pallas_call(dense_body, out_shape=(jax.ShapeDtypeStruct((nodes, hid),...  13.4 us
    all_to_all x1, starting transfers between devices, per_device(): own_self = lax.all_to_all(mine, FEAT, 0, 0, tiled=True)  7.41 us
    all_to_all x1, waiting for transfers between devices, per_device(): own_self = lax.all_to_all(mine, FEAT, 0, 0, tiled=True)  6.41 us
    all_to_all x1, starting transfers between devices, per_device(): own_agg = lax.all_to_all(agg, FEAT, 0, 0, tiled=True)  3.97 us
  transfers between devices with their start and end apart: 19, of which 9 were waited for; matrix products, arithmetic and copies ran while one was open for 3% of the time, Pallas kernels for 13%

profile of v2, /device:TPU:0, one launch (start us, length us, event | category | flops | bytes accessed | tf_op | source)
XLA Modules:
  0.0 124.2 jit_solution(10009206790367455852)
XLA Ops:
  0.6 3.7 %gather_self.1 = bf16[256,24,128]{2,1,0:T(8,128)(2,1)} custom-call(s32[1,256]{1,0:T(1,128)} %blocks_ref.1, bf16[768,24,128]{2,1,0:T(8,128)(2,1)} %bitcast.40), custom_call_target="tpu_custom_call" | custom-call | tf_op jit(solution)/shard_map/gather_self/pallas_call | solution.py:28
  4.3 7.4 %all-to-all-start = ((bf16[256,24,128]{2,1,0:T(8,128)(2,1)}), bf16[256,24,128]{2,1,0:T(8,128)(2,1)S(1)}, u32[]{:S(2)}, u32[]{:S(2)}) async-start(bf16[256,24,128]{2,1,0:T(8,128)(2,1)} %gather_self.1), calls=%async_computation | async-start | bytes 3145728 | tf_op jit(solution)/shard_map/all_to_all | solution.py:192
  11.8 16.7 %aggregate_tiles.1 = bf16[256,24,128]{2,1,0:T(8,128)(2,1)} custom-call(s32[1,384]{1,0:T(1,128)} %rows_ref.1, s32[1,384]{1,0:T(1,128)} %cols_ref.1, bf16[768,24,128]{2,1,0:T(8,128)(2,1)} %bitcast.41, bf16[384,128,128]{2,1,0:T(8,128)(2,1)} %bitcast.42), custom_call_target="tpu_custom_call" | custom-call | flops 301989888 | bytes 18874368 | tf_op jit(solution)/shard_map/aggregate_tiles/pallas_call | solution.py:82
  28.5 6.4 %all-to-all-done = bf16[256,24,128]{2,1,0:T(8,128)(2,1)S(1)} async-done(((bf16[256,24,128]{2,1,0:T(8,128)(2,1)}), bf16[256,24,128]{2,1,0:T(8,128)(2,1)S(1)}, u32[]{:S(2)}, u32[]{:S(2)}) %all-to-all-start) | async-done | bytes 1572896 | tf_op jit(solution)/shard_map/all_to_all | solution.py:192
  34.9 1.2 copy-done
  36.1 4.0 %all-to-all-start.1 = ((bf16[256,24,128]{2,1,0:T(8,128)(2,1)}), bf16[256,24,128]{2,1,0:T(8,128)(2,1)S(1)}, u32[]{:S(2)}, u32[]{:S(2)}) async-start(bf16[256,24,128]{2,1,0:T(8,128)(2,1)} %aggregate_tiles.1), calls=%async_computation.1 | async-start | bytes 3145728 | tf_op jit(solution)/shard_map/all_to_all | solution.py:194
  40.1 0.6 pad_add_fusion.place_ref
  40.7 22.5 %all-to-all-done.1 = bf16[256,24,128]{2,1,0:T(8,128)(2,1)S(1)} async-done(((bf16[256,24,128]{2,1,0:T(8,128)(2,1)}), bf16[256,24,128]{2,1,0:T(8,128)(2,1)S(1)}, u32[]{:S(2)}, u32[]{:S(2)}) %all-to-all-start.1) | async-done | bytes 1572896 | tf_op jit(solution)/shard_map/all_to_all | solution.py:194
  63.2 1.1 copy-done.1
  64.3 13.4 %dense_layer.1 = (bf16[1024,1024]{1,0:T(8,128)(2,1)}, bf16[4,192,512]{2,1,0:T(8,128)(2,1)}, bf16[4,192,512]{2,1,0:T(8,128)(2,1)}, f32[4,192,512]{2,1,0:T(8,128)}, f32[4,192,512]{2,1,0:T(8,128)}) custom-call(s32[3]{0:T(128)} %pad_add_fusion.place_ref, bf16[32,8,24,128]{3,2,1,0:T(8,128)(2,1)} %bitcast.43, bf16[32,8,24,128]{3,2,1,0:T(8,128)(2,1)} %bitcast.44, ...), custom_call_target="tpu_custom_call" | custom-call | tf_op jit(solution)/shard_map/dense_layer/pallas_call | solution.py:153
  77.7 0.0 collective-permute-start
  77.7 0.5 collective-permute-start.7
  78.2 2.0 %collective-permute-done = bf16[4,192,512]{2,1,0:T(8,128)(2,1)S(1)} collective-permute-done((bf16[4,192,512]{2,1,0:T(8,128)(2,1)}, bf16[4,192,512]{2,1,0:T(8,128)(2,1)S(1)}, u32[]{:S(2)}, u32[]{:S(2)}) %collective-permute-start) | collective-permute-done | bytes 786464 | tf_op jit(solution)/shard_map/ppermute | solution.py:204
  80.2 1.8 %fusion.17 = (bf16[4,192,512]{2,1,0:T(8,128)(2,1)S(1)}, f32[4,192,512]{2,1,0:T(8,128)S(1)}) fusion(f32[4,192,512]{2,1,0:T(8,128)} %get-tuple-element.12, bf16[4,192,512]{2,1,0:T(8,128)(2,1)S(1)} %collective-permute-done), kind=kLoop, calls=%fused_computation.32 | loop fusion | flops 1179648 | bytes 4718592 | tf_op jit(solution)/shard_map/convert.13
  82.1 0.1 collective-permute-start.1
  82.2 3.2 %collective-permute-start.3 = (bf16[192,512]{1,0:T(8,128)(2,1)S(1)}, bf16[192,512]{1,0:T(8,128)(2,1)S(1)}, u32[]{:S(2)}, u32[]{:S(2)}) collective-permute-start(bf16[192,512]{1,0:T(8,128)(2,1)S(1)} %get-tuple-element.25), channel_id=1, source_target_pairs={{0,24},{8,0},{16,8},{24,16},{1,25},{9,1},{17,9},{25,17},{2,26},{10... | collective-permute-start | bytes 589832 | tf_op jit(solution)/shard_map/ppermute | solution.py:171
  85.4 0.0 collective-permute-start.2
  85.4 0.0 collective-permute-done.7
  85.4 0.3 fusion.20
  85.8 0.3 collective-permute-start.8
  86.1 3.0 %collective-permute-start.10 = (bf16[192,512]{1,0:T(8,128)(2,1)S(1)}, bf16[192,512]{1,0:T(8,128)(2,1)S(1)}, u32[]{:S(2)}, u32[]{:S(2)}) collective-permute-start(bf16[192,512]{1,0:T(8,128)(2,1)S(1)} %get-tuple-element.28), channel_id=1, source_target_pairs={{0,6},{2,0},{4,2},{6,4},{1,7},{3,1},{5,3},{7,5},{8,14},{10,8},{12,... | collective-permute-start | bytes 589832 | tf_op jit(solution)/shard_map/ppermute | solution.py:171
  89.1 5.4 %collective-permute-done.1 = bf16[192,512]{1,0:T(8,128)(2,1)S(1)} collective-permute-done((bf16[192,512]{1,0:T(8,128)(2,1)S(1)}, bf16[192,512]{1,0:T(8,128)(2,1)S(1)}, u32[]{:S(2)}, u32[]{:S(2)}) %collective-permute-start.1) | collective-permute-done | bytes 196640 | tf_op jit(solution)/shard_map/ppermute | solution.py:171
  94.6 1.1 collective-permute-start.9
  95.7 0.0 collective-permute-done.3
  95.7 0.0 collective-permute-done.2
  95.7 0.1 fusion.15
  95.8 0.7 collective-permute-start.4
  96.5 2.6 %collective-permute-start.6 = (bf16[48,512]{1,0:T(8,128)(2,1)S(1)}, bf16[48,512]{1,0:T(8,128)(2,1)S(1)}, u32[]{:S(2)}, u32[]{:S(2)}) collective-permute-start(bf16[48,512]{1,0:T(8,128)(2,1)S(1)} %get-tuple-element.31), channel_id=1, source_target_pairs={{0,6},{2,0},{4,2},{6,4},{1,7},{3,1},{5,3},{7,5},{8,14},{10,8},{12,... | collective-permute-start | bytes 147464 | tf_op jit(solution)/shard_map/ppermute | solution.py:171
  99.1 0.0 collective-permute-done.8
  99.1 1.2 collective-permute-start.5
  100.3 0.0 collective-permute-done.10
  100.3 3.0 %collective-permute-done.9 = bf16[192,512]{1,0:T(8,128)(2,1)S(1)} collective-permute-done((bf16[192,512]{1,0:T(8,128)(2,1)S(1)}, bf16[192,512]{1,0:T(8,128)(2,1)S(1)}, u32[]{:S(2)}, u32[]{:S(2)}) %collective-permute-start.9) | collective-permute-done | bytes 196640 | tf_op jit(solution)/shard_map/ppermute | solution.py:171
  103.3 0.1 fusion.18
  103.5 0.1 collective-permute-start.11
  103.5 3.2 %collective-permute-start.13 = (bf16[48,512]{1,0:T(8,128)(2,1)S(1)}, bf16[48,512]{1,0:T(8,128)(2,1)S(1)}, u32[]{:S(2)}, u32[]{:S(2)}) collective-permute-start(bf16[48,512]{1,0:T(8,128)(2,1)S(1)} %get-tuple-element.34), channel_id=1, source_target_pairs={{0,24},{8,0},{16,8},{24,16},{1,25},{9,1},{17,9},{25,17},{2,26},{10... | collective-permute-start | bytes 147464 | tf_op jit(solution)/shard_map/ppermute | solution.py:171
  106.8 0.0 collective-permute-done.4
  106.8 0.0 collective-permute-start.12
  106.8 0.0 collective-permute-done.6
  106.8 0.0 collective-permute-done.5
  106.8 2.0 %collective-permute-done.11 = bf16[48,512]{1,0:T(8,128)(2,1)S(1)} collective-permute-done((bf16[48,512]{1,0:T(8,128)(2,1)S(1)}, bf16[48,512]{1,0:T(8,128)(2,1)S(1)}, u32[]{:S(2)}, u32[]{:S(2)}) %collective-permute-start.11) | collective-permute-done | bytes 49184 | tf_op jit(solution)/shard_map/ppermute | solution.py:171
  108.8 0.0 collective-permute-done.13
  108.8 3.5 %collective-permute-done.12 = bf16[48,512]{1,0:T(8,128)(2,1)S(1)} collective-permute-done((bf16[48,512]{1,0:T(8,128)(2,1)S(1)}, bf16[48,512]{1,0:T(8,128)(2,1)S(1)}, u32[]{:S(2)}, u32[]{:S(2)}) %collective-permute-start.12) | collective-permute-done | bytes 49184 | tf_op jit(solution)/shard_map/ppermute | solution.py:171
  112.4 4.1 %collective-permute-start.15 = (bf16[48,1024]{1,0:T(8,128)(2,1)S(1)}, bf16[48,1024]{1,0:T(8,128)(2,1)S(1)}, u32[]{:S(2)}, u32[]{:S(2)}) collective-permute-start(bf16[48,1024]{1,0:T(8,128)(2,1)S(1)} %pad_maximum_fusion), channel_id=1, source_target_pairs={{0,96},{32,0},{64,32},{96,64},{1,97},{33,1},{65,33},{97,65},{2,98}... | collective-permute-start | bytes 294920 | tf_op jit(solution)/shard_map/ppermute | solution.py:171
  116.5 1.9 %collective-permute-start.16 = (bf16[48,1024]{1,0:T(8,128)(2,1)S(1)}, bf16[48,1024]{1,0:T(8,128)(2,1)S(1)}, u32[]{:S(2)}, u32[]{:S(2)}) collective-permute-start(bf16[48,1024]{1,0:T(8,128)(2,1)S(1)} %pad_maximum_fusion), channel_id=1, source_target_pairs={{0,64},{32,96},{64,0},{96,32},{1,65},{33,97},{65,1},{97,33},{2,66}... | collective-permute-start | bytes 294920 | tf_op jit(solution)/shard_map/ppermute | solution.py:171
  118.4 0.4 collective-permute-done.15
  118.7 4.7 %collective-permute-done.14 = bf16[48,1024]{1,0:T(8,128)(2,1)S(1)} collective-permute-done((bf16[48,1024]{1,0:T(8,128)(2,1)S(1)}, bf16[48,1024]{1,0:T(8,128)(2,1)S(1)}, u32[]{:S(2)}, u32[]{:S(2)}) %collective-permute-start.14) | collective-permute-done | bytes 98336 | tf_op jit(solution)/shard_map/ppermute | solution.py:171
  123.4 0.0 collective-permute-done.16
  123.4 0.7 fusion.7
  (12 shorter events, 0.2 us)
Async XLA Ops:
  4.3 30.5 %all-to-all-start = ((bf16[256,24,128]{2,1,0:T(8,128)(2,1)}), bf16[256,24,128]{2,1,0:T(8,128)(2,1)S(1)}, u32[]{:S(2)}, u32[]{:S(2)}) async-start(bf16[256,24,128]{2,1,0:T(8,128)(2,1)} %gather_self.1), calls=%async_computation | async-start | bytes 3145728 | tf_op jit(solution)/shard_map/all_to_all | solution.py:192
  34.9 1.2 copy-start
  36.1 27.1 %all-to-all-start.1 = ((bf16[256,24,128]{2,1,0:T(8,128)(2,1)}), bf16[256,24,128]{2,1,0:T(8,128)(2,1)S(1)}, u32[]{:S(2)}, u32[]{:S(2)}) async-start(bf16[256,24,128]{2,1,0:T(8,128)(2,1)} %aggregate_tiles.1), calls=%async_computation.1 | async-start | bytes 3145728 | tf_op jit(solution)/shard_map/all_to_all | solution.py:194
  63.2 1.1 copy-start.1
  77.7 2.5 %collective-permute-start = (bf16[4,192,512]{2,1,0:T(8,128)(2,1)}, bf16[4,192,512]{2,1,0:T(8,128)(2,1)S(1)}, u32[]{:S(2)}, u32[]{:S(2)}) collective-permute-start(bf16[4,192,512]{2,1,0:T(8,128)(2,1)} %get-tuple-element.13), channel_id=1, source_target_pairs={{0,1},{1,0},{2,3},{3,2},{4,5},{5,4},{6,7},{7,6},{8,9},{9,8},{10,11... | collective-permute-start | bytes 2359304 | tf_op jit(solution)/shard_map/ppermute | solution.py:204
  77.7 7.7 %collective-permute-start.7 = (bf16[4,192,512]{2,1,0:T(8,128)(2,1)}, bf16[4,192,512]{2,1,0:T(8,128)(2,1)S(1)}, u32[]{:S(2)}, u32[]{:S(2)}) collective-permute-start(bf16[4,192,512]{2,1,0:T(8,128)(2,1)} %get-tuple-element.15), channel_id=1, source_target_pairs={{0,1},{1,0},{2,3},{3,2},{4,5},{5,4},{6,7},{7,6},{8,9},{9,8},{10,11... | collective-permute-start | bytes 2359304 | tf_op jit(solution)/shard_map/ppermute | solution.py:204
  80.2 5.2 %copy-start.2 = (f32[4,192,512]{2,1,0:T(8,128)S(1)}, f32[4,192,512]{2,1,0:T(8,128)}, u32[]{:S(2)}) copy-start(f32[4,192,512]{2,1,0:T(8,128)} %get-tuple-element.14) | copy-start | bytes 4718596
  82.1 12.4 %collective-permute-start.1 = (bf16[192,512]{1,0:T(8,128)(2,1)S(1)}, bf16[192,512]{1,0:T(8,128)(2,1)S(1)}, u32[]{:S(2)}, u32[]{:S(2)}) collective-permute-start(bf16[192,512]{1,0:T(8,128)(2,1)S(1)} %get-tuple-element.24), channel_id=1, source_target_pairs={{0,8},{8,16},{16,24},{24,0},{1,9},{9,17},{17,25},{25,1},{2,10},{10... | collective-permute-start | bytes 589832 | tf_op jit(solution)/shard_map/ppermute | solution.py:171
  82.2 13.5 %collective-permute-start.3 = (bf16[192,512]{1,0:T(8,128)(2,1)S(1)}, bf16[192,512]{1,0:T(8,128)(2,1)S(1)}, u32[]{:S(2)}, u32[]{:S(2)}) collective-permute-start(bf16[192,512]{1,0:T(8,128)(2,1)S(1)} %get-tuple-element.25), channel_id=1, source_target_pairs={{0,24},{8,0},{16,8},{24,16},{1,25},{9,1},{17,9},{25,17},{2,26},{10... | collective-permute-start | bytes 589832 | tf_op jit(solution)/shard_map/ppermute | solution.py:171
  85.4 10.3 %collective-permute-start.2 = (bf16[192,512]{1,0:T(8,128)(2,1)S(1)}, bf16[192,512]{1,0:T(8,128)(2,1)S(1)}, u32[]{:S(2)}, u32[]{:S(2)}) collective-permute-start(bf16[192,512]{1,0:T(8,128)(2,1)S(1)} %get-tuple-element.26), channel_id=1, source_target_pairs={{0,16},{8,24},{16,0},{24,8},{1,17},{9,25},{17,1},{25,9},{2,18},{10... | collective-permute-start | bytes 589832 | tf_op jit(solution)/shard_map/ppermute | solution.py:171
  85.8 13.3 %collective-permute-start.8 = (bf16[192,512]{1,0:T(8,128)(2,1)S(1)}, bf16[192,512]{1,0:T(8,128)(2,1)S(1)}, u32[]{:S(2)}, u32[]{:S(2)}) collective-permute-start(bf16[192,512]{1,0:T(8,128)(2,1)S(1)} %get-tuple-element.27), channel_id=1, source_target_pairs={{0,2},{2,4},{4,6},{6,0},{1,3},{3,5},{5,7},{7,1},{8,10},{10,12},{12... | collective-permute-start | bytes 589832 | tf_op jit(solution)/shard_map/ppermute | solution.py:171
  86.1 14.2 %collective-permute-start.10 = (bf16[192,512]{1,0:T(8,128)(2,1)S(1)}, bf16[192,512]{1,0:T(8,128)(2,1)S(1)}, u32[]{:S(2)}, u32[]{:S(2)}) collective-permute-start(bf16[192,512]{1,0:T(8,128)(2,1)S(1)} %get-tuple-element.28), channel_id=1, source_target_pairs={{0,6},{2,0},{4,2},{6,4},{1,7},{3,1},{5,3},{7,5},{8,14},{10,8},{12,... | collective-permute-start | bytes 589832 | tf_op jit(solution)/shard_map/ppermute | solution.py:171
  94.6 8.8 %collective-permute-start.9 = (bf16[192,512]{1,0:T(8,128)(2,1)S(1)}, bf16[192,512]{1,0:T(8,128)(2,1)S(1)}, u32[]{:S(2)}, u32[]{:S(2)}) collective-permute-start(bf16[192,512]{1,0:T(8,128)(2,1)S(1)} %get-tuple-element.29), channel_id=1, source_target_pairs={{0,4},{2,6},{4,0},{6,2},{1,5},{3,7},{5,1},{7,3},{8,12},{10,14},{12... | collective-permute-start | bytes 589832 | tf_op jit(solution)/shard_map/ppermute | solution.py:171
  95.8 10.9 %collective-permute-start.4 = (bf16[48,512]{1,0:T(8,128)(2,1)S(1)}, bf16[48,512]{1,0:T(8,128)(2,1)S(1)}, u32[]{:S(2)}, u32[]{:S(2)}) collective-permute-start(bf16[48,512]{1,0:T(8,128)(2,1)S(1)} %get-tuple-element.30), channel_id=1, source_target_pairs={{0,2},{2,4},{4,6},{6,0},{1,3},{3,5},{5,7},{7,1},{8,10},{10,12},{12... | collective-permute-start | bytes 147464 | tf_op jit(solution)/shard_map/ppermute | solution.py:171
  96.5 10.2 %collective-permute-start.6 = (bf16[48,512]{1,0:T(8,128)(2,1)S(1)}, bf16[48,512]{1,0:T(8,128)(2,1)S(1)}, u32[]{:S(2)}, u32[]{:S(2)}) collective-permute-start(bf16[48,512]{1,0:T(8,128)(2,1)S(1)} %get-tuple-element.31), channel_id=1, source_target_pairs={{0,6},{2,0},{4,2},{6,4},{1,7},{3,1},{5,3},{7,5},{8,14},{10,8},{12,... | collective-permute-start | bytes 147464 | tf_op jit(solution)/shard_map/ppermute | solution.py:171
  99.1 7.6 %collective-permute-start.5 = (bf16[48,512]{1,0:T(8,128)(2,1)S(1)}, bf16[48,512]{1,0:T(8,128)(2,1)S(1)}, u32[]{:S(2)}, u32[]{:S(2)}) collective-permute-start(bf16[48,512]{1,0:T(8,128)(2,1)S(1)} %get-tuple-element.32), channel_id=1, source_target_pairs={{0,4},{2,6},{4,0},{6,2},{1,5},{3,7},{5,1},{7,3},{8,12},{10,14},{12... | collective-permute-start | bytes 147464 | tf_op jit(solution)/shard_map/ppermute | solution.py:171
  103.5 5.4 %collective-permute-start.11 = (bf16[48,512]{1,0:T(8,128)(2,1)S(1)}, bf16[48,512]{1,0:T(8,128)(2,1)S(1)}, u32[]{:S(2)}, u32[]{:S(2)}) collective-permute-start(bf16[48,512]{1,0:T(8,128)(2,1)S(1)} %get-tuple-element.33), channel_id=1, source_target_pairs={{0,8},{8,16},{16,24},{24,0},{1,9},{9,17},{17,25},{25,1},{2,10},{10... | collective-permute-start | bytes 147464 | tf_op jit(solution)/shard_map/ppermute | solution.py:171
  103.5 5.3 %collective-permute-start.13 = (bf16[48,512]{1,0:T(8,128)(2,1)S(1)}, bf16[48,512]{1,0:T(8,128)(2,1)S(1)}, u32[]{:S(2)}, u32[]{:S(2)}) collective-permute-start(bf16[48,512]{1,0:T(8,128)(2,1)S(1)} %get-tuple-element.34), channel_id=1, source_target_pairs={{0,24},{8,0},{16,8},{24,16},{1,25},{9,1},{17,9},{25,17},{2,26},{10... | collective-permute-start | bytes 147464 | tf_op jit(solution)/shard_map/ppermute | solution.py:171
  106.8 5.6 %collective-permute-start.12 = (bf16[48,512]{1,0:T(8,128)(2,1)S(1)}, bf16[48,512]{1,0:T(8,128)(2,1)S(1)}, u32[]{:S(2)}, u32[]{:S(2)}) collective-permute-start(bf16[48,512]{1,0:T(8,128)(2,1)S(1)} %get-tuple-element.35), channel_id=1, source_target_pairs={{0,16},{8,24},{16,0},{24,8},{1,17},{9,25},{17,1},{25,9},{2,18},{10... | collective-permute-start | bytes 147464 | tf_op jit(solution)/shard_map/ppermute | solution.py:171
  112.4 6.3 %collective-permute-start.15 = (bf16[48,1024]{1,0:T(8,128)(2,1)S(1)}, bf16[48,1024]{1,0:T(8,128)(2,1)S(1)}, u32[]{:S(2)}, u32[]{:S(2)}) collective-permute-start(bf16[48,1024]{1,0:T(8,128)(2,1)S(1)} %pad_maximum_fusion), channel_id=1, source_target_pairs={{0,96},{32,0},{64,32},{96,64},{1,97},{33,1},{65,33},{97,65},{2,98}... | collective-permute-start | bytes 294920 | tf_op jit(solution)/shard_map/ppermute | solution.py:171
  116.5 6.9 %collective-permute-start.14 = (bf16[48,1024]{1,0:T(8,128)(2,1)S(1)}, bf16[48,1024]{1,0:T(8,128)(2,1)S(1)}, u32[]{:S(2)}, u32[]{:S(2)}) collective-permute-start(bf16[48,1024]{1,0:T(8,128)(2,1)S(1)} %pad_maximum_fusion), channel_id=1, source_target_pairs={{0,32},{32,64},{64,96},{96,0},{1,33},{33,65},{65,97},{97,1},{2,34}... | collective-permute-start | bytes 294920 | tf_op jit(solution)/shard_map/ppermute | solution.py:171
  116.5 6.9 %collective-permute-start.16 = (bf16[48,1024]{1,0:T(8,128)(2,1)S(1)}, bf16[48,1024]{1,0:T(8,128)(2,1)S(1)}, u32[]{:S(2)}, u32[]{:S(2)}) collective-permute-start(bf16[48,1024]{1,0:T(8,128)(2,1)S(1)} %pad_maximum_fusion), channel_id=1, source_target_pairs={{0,64},{32,96},{64,0},{96,32},{1,65},{33,97},{65,1},{97,33},{2,66}... | collective-permute-start | bytes 294920 | tf_op jit(solution)/shard_map/ppermute | solution.py:171

commit v3 on v2

--- a/solution.py
+++ b/solution.py
@@ -9,7 +9,15 @@
 
 BF = jnp.bfloat16
 F32 = jnp.float32
-VMEM_LIMIT = 56 << 20
+MIB = 1 << 20
+
+
+def in_vmem(value):
+    return pltpu.with_memory_space_constraint(value, pltpu.VMEM)
+
+
+def in_hbm(value):
+    return pltpu.with_memory_space_constraint(value, pltpu.HBM)
 
 
 def gather_body(blocks_ref, feat_ref, out_ref, sem):
@@ -35,7 +43,7 @@
             out_specs=pl.BlockSpec((count,) + feat.shape[1:], lambda i, b: (0, 0, 0)),
             scratch_shapes=[pltpu.SemaphoreType.DMA(())],
         ),
-        compiler_params=pltpu.CompilerParams(vmem_limit_bytes=VMEM_LIMIT),
+        compiler_params=pltpu.CompilerParams(vmem_limit_bytes=56 * MIB),
         name="gather_self",
     )(blocks, feat)
 
@@ -96,7 +104,7 @@
             ],
         ),
         compiler_params=pltpu.CompilerParams(
-            vmem_limit_bytes=VMEM_LIMIT, dimension_semantics=("arbitrary",)
+            vmem_limit_bytes=56 * MIB, dimension_semantics=("arbitrary",)
         ),
         cost_estimate=pl.CostEstimate(
             flops=2 * count * width * side * side,
@@ -107,75 +115,122 @@
     )(rows, cols, feat, adj)
 
 
-def dense_body(
-    place_ref, self_ref, agg_ref, weight_ref, bias_ref, cot_ref,
-    hidden_ref, send0_ref, send1_ref, keep0_ref, keep1_ref, comb_ref, grad_ref,
-):
-    sources, own, width, side = self_ref.shape
-    half = sources * width
+def stack_channels(own_ref, comb_ref):
+    sources, own, width, side = own_ref.shape
     for r in range(own):
-        cols = pl.ds(r * side, side)
-        comb_ref[0:half, cols] = self_ref[:, r].reshape(half, side)
-        comb_ref[half:, cols] = agg_ref[:, r].reshape(half, side)
-    chunk = 4 * side
-    for m in range(own // 4):
+        comb_ref[:, pl.ds(r * side, side)] = own_ref[:, r].reshape(sources * width, side)
+
+
+def dense_self_body(self_ref, weight_ref, bias_ref, comb_ref, pre_ref):
+    stack_channels(self_ref, comb_ref)
+    half, nodes = comb_ref.shape
+    chunk = nodes // 2
+    for m in range(2):
         rows = pl.ds(m * chunk, chunk)
         pre = lax.dot_general(
+            comb_ref[:, rows], weight_ref[:half, :], (((0,), (0,)), ((), ())), preferred_element_type=F32
+        )
+        pre_ref[rows, :] = pre + bias_ref[...]
+
+
+def dense_self(own_self, weight, bias):
+    sources, own, width, side = own_self.shape
+    vmem = pl.BlockSpec(memory_space=pltpu.VMEM)
+    return pl.pallas_call(
+        dense_self_body,
+        out_shape=(
+            pltpu.HBM((sources * width, own * side), BF),
+            pltpu.HBM((own * side, weight.shape[1]), F32),
+        ),
+        in_specs=[vmem] * 3,
+        out_specs=(vmem,) * 2,
+        compiler_params=pltpu.CompilerParams(vmem_limit_bytes=56 * MIB),
+        name="dense_self",
+    )(in_vmem(own_self), in_hbm(weight), in_hbm(bias))
+
+
+def dense_rest_body(
+    core_ref, agg_ref, comb_self_hbm, pre_hbm, weight_hbm, cot_hbm,
+    hidden_hbm, send_ref, keep_ref,
+    comb_ref, grad_ref, hidden_ref, comb_self_ref, pre_ref, weight_ref, cot_ref, sem,
+):
+    half, nodes = comb_ref.shape
+    chunk = nodes // 2
+    chunks = [pl.ds(m * chunk, chunk) for m in range(2)]
+    sources = [(weight_hbm.at[pl.ds(half, half)], weight_ref)]
+    for rows in chunks:
+        sources.append((pre_hbm.at[rows], pre_ref.at[rows]))
+        sources.append((cot_hbm.at[rows], cot_ref.at[rows]))
+    sources.append((comb_self_hbm, comb_self_ref))
+    loads = [pltpu.make_async_copy(a, b, sem.at[i]) for i, (a, b) in enumerate(sources)]
+    for load in loads:
+        load.start()
+    stack_channels(agg_ref, comb_ref)
+    loads[0].wait()
+    stores = []
+    for m, rows in enumerate(chunks):
+        part = lax.dot_general(
             comb_ref[:, rows], weight_ref[...], (((0,), (0,)), ((), ())), preferred_element_type=F32
         )
-        pre = pre + bias_ref[...]
+        loads[1 + 2 * m].wait()
+        loads[2 + 2 * m].wait()
+        pre = pre_ref[rows, :] + part
         decay = jnp.exp(jnp.minimum(pre, 0.0))
         hidden_ref[rows, :] = jnp.where(pre > 0, pre, decay - 1.0).astype(BF)
         grad_ref[rows, :] = (cot_ref[rows, :].astype(F32) * decay).astype(BF)
-    x, y, core = place_ref[0], place_ref[1], place_ref[2]
-    hid = cot_ref.shape[1]
-    share = comb_ref.shape[0] // 32
-
-    def block(dx, dy, dest):
-        first = (8 * ((x + dx) % 4) + 2 * ((y + dy) % 4) + dest) * share
-        return comb_ref[pl.ds(pl.multiple_of(first, share), share), :]
-
-    outs = ((send0_ref, send1_ref), (keep0_ref, keep1_ref))
-    for dest, refs in zip((1 - core, core), outs):
-        for part in range(2):
-            pairs = [(k, j) if part == 0 else (j, k) for k in range(4) for j in range(4)]
-            lhs = jnp.concatenate([block(dx, dy, dest) for dx, dy in pairs], axis=0)
-            cols = pl.ds(part * (hid // 2), hid // 2)
-            total = jnp.dot(lhs, grad_ref[:, cols], preferred_element_type=F32)
-            refs[part][...] = total.reshape(refs[part].shape).astype(refs[part].dtype)
-
-
-def dense_layer(place, own_self, own_agg, weight, bias, cot):
+        stores.append(pltpu.make_async_copy(hidden_ref.at[rows], hidden_hbm.at[rows], sem.at[6 + m]))
+        stores[m].start()
+    loads[5].wait()
+    core = core_ref[0]
+    zs, blocks, share, width = send_ref.shape
+    for dest, out_ref in ((1 - core, send_ref), (core, keep_ref)):
+        lhs = jnp.concatenate(
+            [
+                source[pl.ds(pl.multiple_of((2 * b + dest) * share, share), share), :]
+                for source in (comb_self_ref, comb_ref)
+                for b in range(blocks // 2)
+            ],
+            axis=0,
+        )
+        for z in range(zs):
+            total = jnp.dot(lhs, grad_ref[:, pl.ds(z * width, width)], preferred_element_type=F32)
+            out_ref[z] = total.reshape(blocks, share, width).astype(out_ref.dtype)
+    for store in stores:
+        store.wait()
+
+
+def dense_rest(core, own_agg, comb_self, pre, weight, cot):
     nodes, hid = cot.shape
-    channels = weight.shape[0]
-    piece = (4, channels // 8, hid // 2)
+    half = comb_self.shape[0]
+    pieces = (4, 16, half // 16, hid // 4)
     vmem = pl.BlockSpec(memory_space=pltpu.VMEM)
     return pl.pallas_call(
-        dense_body,
+        dense_rest_body,
         out_shape=(
             jax.ShapeDtypeStruct((nodes, hid), BF),
-            jax.ShapeDtypeStruct(piece, BF),
-            jax.ShapeDtypeStruct(piece, BF),
-            jax.ShapeDtypeStruct(piece, F32),
-            jax.ShapeDtypeStruct(piece, F32),
-        ),
-        in_specs=[pl.BlockSpec(memory_space=pltpu.SMEM)] + [vmem] * 5,
-        out_specs=(vmem,) * 5,
-        scratch_shapes=[pltpu.VMEM((channels, nodes), BF), pltpu.VMEM((nodes, hid), BF)],
-        compiler_params=pltpu.CompilerParams(vmem_limit_bytes=VMEM_LIMIT),
-        name="dense_layer",
-    )(place, own_self, own_agg, weight, bias, cot)
+            pltpu.VMEM(pieces, BF),
+            pltpu.VMEM(pieces, F32),
+        ),
+        in_specs=[pl.BlockSpec(memory_space=pltpu.SMEM), vmem]
+        + [pl.BlockSpec(memory_space=pl.ANY)] * 4,
+        out_specs=(pl.BlockSpec(memory_space=pl.ANY), vmem, vmem),
+        scratch_shapes=[
+            pltpu.VMEM((half, nodes), BF),
+            pltpu.VMEM((nodes, hid), BF),
+            pltpu.VMEM((nodes, hid), BF),
+            pltpu.VMEM((half, nodes), BF),
+            pltpu.VMEM((nodes, hid), F32),
+            pltpu.VMEM((half, hid), BF),
+            pltpu.VMEM((nodes, hid), BF),
+            pltpu.SemaphoreType.DMA((8,)),
+        ],
+        compiler_params=pltpu.CompilerParams(vmem_limit_bytes=32 * MIB),
+        name="dense_rest",
+    )(core, in_vmem(own_agg), *map(in_hbm, (comb_self, pre, weight, cot)))
 
 
 def shift(value, axis, k):
     return lax.ppermute(value, axis, [(i, (i + k) % 4) for i in range(4)])
-
-
-def exchange(parts, axis):
-    total = parts[0].astype(F32)
-    for k in (1, 2, 3):
-        total = total + shift(parts[k].astype(BF), axis, k).astype(F32)
-    return total
 
 
 FEAT = ("x", "y", "core")
@@ -193,22 +248,24 @@
     agg = aggregate_tiles(tile_rows, tile_cols, feat, adj_tiles[0], nrb)
     own_agg = lax.all_to_all(agg, FEAT, 0, 0, tiled=True)
     shape = (32, nrb // 32, width, side)
-    place = jnp.stack([lax.axis_index(a) for a in FEAT]).astype(jnp.int32)
-    hidden, send0, send1, keep0, keep1 = dense_layer(
-        place, own_self.reshape(shape), own_agg.reshape(shape), weight, proj_bias[None], cotangent[0]
+    comb_self, pre = dense_self(own_self.reshape(shape), weight, proj_bias[None])
+    core = lax.axis_index("core").astype(jnp.int32).reshape(1)
+    hidden, send, keep = dense_rest(
+        core, own_agg.reshape(shape), comb_self, pre, weight, cotangent[0]
     )
-    share, half = weight.shape[0] // 32, weight.shape[1] // 2
-    swap = [(0, 1), (1, 0)]
-    totals = []
-    for send, keep, first, second in ((send0, keep0, "x", "y"), (send1, keep1, "y", "x")):
-        pair = keep + lax.ppermute(send, "core", swap).astype(F32)
-        once = exchange([pair[k] for k in range(4)], first).reshape(4, share, half)
-        totals.append(exchange([once[k] for k in range(4)], second))
-    mine = jnp.concatenate(totals, axis=1).astype(BF)
-    n1, n2, n3 = (shift(mine, "grp", -k).astype(F32) for k in (1, 2, 3))
-    odd = lax.axis_index("grp") % 2 == 1
-    total = (mine.astype(F32) + jnp.where(odd, n3, n1)) + (n2 + jnp.where(odd, n1, n3))
-    return hidden[None], total
+    pair = (keep + lax.ppermute(send, "core", [(0, 1), (1, 0)]).astype(F32)).astype(BF)
+    pair = pair.reshape((64,) + pair.shape[2:])
+    pieces = lax.all_to_all(pair, ("grp", "x", "y"), 0, 0, tiled=True)
+    piece = jnp.sum(pieces.astype(F32), axis=0)
+    near = [piece] + [shift(piece, "grp", -k) for k in (1, 2, 3)]
+    grp = lax.axis_index("grp")
+    columns = []
+    for z in range(4):
+        k = (z - grp) % 4
+        columns.append(
+            jnp.where(k == 0, near[0], jnp.where(k == 1, near[1], jnp.where(k == 2, near[2], near[3])))
+        )
+    return hidden[None], jnp.concatenate(columns, axis=1)
 
 
 def solution(mesh):

time: 125 us -> 115 us (0.920)
  blocking collectives: 0 us -> 31.7 us
  starting transfers between devices: 33.4 us -> 13.6 us
  waiting for transfers between devices: 49.9 us -> 32.4 us
  local copies, waits for them, and re-layouts: 2.44 us -> 0 us
  other arithmetic: 3.79 us -> 1.6 us
    all_to_all x0 -> x1, blocking collectives: none -> 31.7 us  [per_device(): pieces = lax.all_to_all(pair, ('grp', 'x', 'y'), 0, 0, tiled=True)]
    ppermute x15 -> x3, starting transfers between devices: 21.5 us -> 2.12 us  [shift(): return lax.ppermute(value, axis, [(i, (i + k) % 4) for i in range(4)])]
    ppermute x15 -> x3, waiting for transfers between devices: 19 us -> 5.27 us  [shift(): return lax.ppermute(value, axis, [(i, (i + k) % 4) for i in range(4)])]
    all_to_all x1, waiting for transfers between devices: 22.5 us -> 17.3 us  [per_device(): own_agg = lax.all_to_all(agg, FEAT, 0, 0, tiled=True)]
    another operation x7 -> x0, other arithmetic: 3.04 us -> none
    unnamed x6 -> x0, local copies, waits for them, and re-layouts: 2.34 us -> none
    ppermute x2 -> x1, waiting for transfers between devices: 1.99 us -> 3.4 us  [per_device(): lax.ppermute(send, 'core', [(0, 1), (1, 0)]).astype(F32)]
    pallas_call x1 -> x2, Pallas kernels: 13.4 us -> 14.3 us  [the longest x1 8.56 us: dense_rest(): pl.pallas_call(dense_rest_body, out_shape=(jax.ShapeDtypeStruct((nodes, h...]
  transfers between devices with their start and end apart: 19 -> 6, of which waited for: 9 -> 6; matrix products, arithmetic and copies ran while one was open for 3% -> 0% of each run, Pallas kernels for 13% -> 20%
where the time goes in v3:
time: 115 us
  Pallas kernels  34.8 us (30%)
  waiting for transfers between devices  32.4 us (28%)
  blocking collectives  31.7 us (28%)
  starting transfers between devices  13.6 us (12%)
  other arithmetic  1.6 us (1%)
    all_to_all x1, blocking collectives, per_device(): pieces = lax.all_to_all(pair, ('grp', 'x', 'y'), 0, 0, tiled=True)  31.7 us
    all_to_all x1, waiting for transfers between devices, per_device(): own_agg = lax.all_to_all(agg, FEAT, 0, 0, tiled=True)  17.3 us
    pallas_call x1, Pallas kernels, aggregate_tiles(): pl.pallas_call(functools.partial(aggregate_body, unroll), out_shape=jax.S...  16.7 us
    pallas_call x1, Pallas kernels, dense_rest(): pl.pallas_call(dense_rest_body, out_shape=(jax.ShapeDtypeStruct((nodes, h...  8.56 us
    all_to_all x1, starting transfers between devices, per_device(): own_self = lax.all_to_all(mine, FEAT, 0, 0, tiled=True)  7.42 us
    all_to_all x1, waiting for transfers between devices, per_device(): own_self = lax.all_to_all(mine, FEAT, 0, 0, tiled=True)  6.41 us
    pallas_call x1, Pallas kernels, dense_self(): pl.pallas_call(dense_self_body, out_shape=(pltpu.HBM((sources * width, ow...  5.77 us
    ppermute x3, waiting for transfers between devices, shift(): return lax.ppermute(value, axis, [(i, (i + k) % 4) for i in range(4)])  5.27 us
  transfers between devices with their start and end apart: 6, of which 6 were waited for; matrix products, arithmetic and copies ran while one was open for 0% of the time, Pallas kernels for 20%

profile of v3, /device:TPU:0, one launch (start us, length us, event | category | flops | bytes accessed | tf_op | source)
XLA Modules:
  0.0 114.8 jit_solution(11832294384360561349)
XLA Ops:
  0.6 3.7 %gather_self.1 = bf16[256,24,128]{2,1,0:T(8,128)(2,1)} custom-call(s32[1,256]{1,0:T(1,128)} %blocks_ref.1, bf16[768,24,128]{2,1,0:T(8,128)(2,1)} %bitcast.11), custom_call_target="tpu_custom_call" | custom-call | tf_op jit(solution)/shard_map/gather_self/pallas_call | solution.py:36
  4.4 7.4 %all-to-all-start.1 = ((bf16[256,24,128]{2,1,0:T(8,128)(2,1)}), bf16[256,24,128]{2,1,0:T(8,128)(2,1)S(1)}, u32[]{:S(2)}, u32[]{:S(2)}) async-start(bf16[256,24,128]{2,1,0:T(8,128)(2,1)} %gather_self.1), calls=%async_computation.1 | async-start | bytes 3145728 | tf_op jit(solution)/shard_map/all_to_all | solution.py:247
  11.8 16.7 %aggregate_tiles.1 = bf16[256,24,128]{2,1,0:T(8,128)(2,1)} custom-call(s32[1,384]{1,0:T(1,128)} %rows_ref.1, s32[1,384]{1,0:T(1,128)} %cols_ref.1, bf16[768,24,128]{2,1,0:T(8,128)(2,1)} %bitcast.12, bf16[384,128,128]{2,1,0:T(8,128)(2,1)} %bitcast.13), custom_call_target="tpu_custom_call" | custom-call | flops 301989888 | bytes 18874368 | tf_op jit(solution)/shard_map/aggregate_tiles/pallas_call | solution.py:90
  28.5 6.4 %all-to-all-done.1 = bf16[256,24,128]{2,1,0:T(8,128)(2,1)S(1)} async-done(((bf16[256,24,128]{2,1,0:T(8,128)(2,1)}), bf16[256,24,128]{2,1,0:T(8,128)(2,1)S(1)}, u32[]{:S(2)}, u32[]{:S(2)}) %all-to-all-start.1) | async-done | bytes 1572896 | tf_op jit(solution)/shard_map/all_to_all | solution.py:247
  34.9 4.0 %all-to-all-start = ((bf16[256,24,128]{2,1,0:T(8,128)(2,1)}), bf16[256,24,128]{2,1,0:T(8,128)(2,1)S(1)}, u32[]{:S(2)}, u32[]{:S(2)}) async-start(bf16[256,24,128]{2,1,0:T(8,128)(2,1)} %aggregate_tiles.1), calls=%async_computation | async-start | bytes 3145728 | tf_op jit(solution)/shard_map/all_to_all | solution.py:249
  38.9 5.8 %dense_self.1 = (bf16[768,1024]{1,0:T(8,128)(2,1)}, f32[1024,1024]{1,0:T(8,128)}) custom-call(bf16[32,8,24,128]{3,2,1,0:T(8,128)(2,1)S(1)} %bitcast.10, bf16[1536,1024]{1,0:T(8,128)(2,1)} %weight_hbm.1, f32[1,1024]{1,0:T(1,128)} %bitcast.16), custom_call_target="tpu_custom_call" | custom-call | tf_op jit(solution)/shard_map/dense_self/pallas_call | solution.py:139
  44.7 17.3 %all-to-all-done = bf16[256,24,128]{2,1,0:T(8,128)(2,1)S(1)} async-done(((bf16[256,24,128]{2,1,0:T(8,128)(2,1)}), bf16[256,24,128]{2,1,0:T(8,128)(2,1)S(1)}, u32[]{:S(2)}, u32[]{:S(2)}) %all-to-all-start) | async-done | bytes 1572896 | tf_op jit(solution)/shard_map/all_to_all | solution.py:249
  62.0 8.6 %dense_rest.1 = (bf16[1024,1024]{1,0:T(8,128)(2,1)}, bf16[4,16,48,256]{3,2,1,0:T(8,128)(2,1)S(1)}, f32[4,16,48,256]{3,2,1,0:T(8,128)S(1)}) custom-call(s32[1]{0:T(128)} %bitcast.core_ref, bf16[32,8,24,128]{3,2,1,0:T(8,128)(2,1)S(1)} %bitcast.9, bf16[768,1024]{1,0:T(8,128)(2,1)} %get-tuple-element.11.comb_self_hbm, f32[1024,1024]{1,0:T(8,128)} %get-tuple-element.12.pre_hbm, ...), custom_call_target="tpu_custom_call" | custom-call | tf_op jit(solution)/shard_map/dense_rest/pallas_call | solution.py:207
  70.6 0.1 collective-permute-start
  70.7 3.4 %collective-permute-done = bf16[4,16,48,256]{3,2,1,0:T(8,128)(2,1)S(1)} collective-permute-done((bf16[4,16,48,256]{3,2,1,0:T(8,128)(2,1)S(1)}, bf16[4,16,48,256]{3,2,1,0:T(8,128)(2,1)S(1)}, u32[]{:S(2)}, u32[]{:S(2)}) %collective-permute-start) | collective-permute-done | bytes 1572896 | tf_op jit(solution)/shard_map/ppermute | solution.py:256
  74.1 0.6 add_convert_fusion
  74.7 31.7 %all_to_all.15 = bf16[64,48,256]{2,1,0:T(8,128)(2,1)S(1)} all-to-all(bf16[64,48,256]{2,1,0:T(8,128)(2,1)S(1)} %bitcast.14), channel_id=1, replica_groups=mesh['grp'=4,'x'=4,'y'=4,'core'=2] {'grp','x','y'}, dimensions={0} | all-to-all | bytes 3145728 | tf_op jit(solution)/shard_map/all_to_all | solution.py:258
  106.4 0.2 convert_reduce_fusion
  106.7 0.8 collective-permute-start.1
  107.5 1.3 %collective-permute-start.2 = (f32[48,256]{1,0:T(8,128)S(1)}, f32[48,256]{1,0:T(8,128)S(1)}, u32[]{:S(2)}, u32[]{:S(2)}) collective-permute-start(f32[48,256]{1,0:T(8,128)S(1)} %convert_reduce_fusion), channel_id=1, source_target_pairs={{0,64},{32,96},{64,0},{96,32},{1,65},{33,97},{65,1},{97,33},{2,66}... | collective-permute-start | bytes 147464 | tf_op jit(solution)/shard_map/ppermute | solution.py:233
  108.8 0.0 collective-permute-start.3
  108.8 2.0 %collective-permute-done.1 = f32[48,256]{1,0:T(8,128)S(1)} collective-permute-done((f32[48,256]{1,0:T(8,128)S(1)}, f32[48,256]{1,0:T(8,128)S(1)}, u32[]{:S(2)}, u32[]{:S(2)}) %collective-permute-start.1) | collective-permute-done | bytes 49184 | tf_op jit(solution)/shard_map/ppermute | solution.py:233
  110.8 2.3 %collective-permute-done.2 = f32[48,256]{1,0:T(8,128)S(1)} collective-permute-done((f32[48,256]{1,0:T(8,128)S(1)}, f32[48,256]{1,0:T(8,128)S(1)}, u32[]{:S(2)}, u32[]{:S(2)}) %collective-permute-start.2) | collective-permute-done | bytes 49184 | tf_op jit(solution)/shard_map/ppermute | solution.py:233
  113.1 1.0 collective-permute-done.3
  114.1 0.7 pad_maximum_fusion
  (1 shorter events, 0.0 us)
Async XLA Ops:
  4.4 30.6 %all-to-all-start.1 = ((bf16[256,24,128]{2,1,0:T(8,128)(2,1)}), bf16[256,24,128]{2,1,0:T(8,128)(2,1)S(1)}, u32[]{:S(2)}, u32[]{:S(2)}) async-start(bf16[256,24,128]{2,1,0:T(8,128)(2,1)} %gather_self.1), calls=%async_computation.1 | async-start | bytes 3145728 | tf_op jit(solution)/shard_map/all_to_all | solution.py:247
  34.9 27.1 %all-to-all-start = ((bf16[256,24,128]{2,1,0:T(8,128)(2,1)}), bf16[256,24,128]{2,1,0:T(8,128)(2,1)S(1)}, u32[]{:S(2)}, u32[]{:S(2)}) async-start(bf16[256,24,128]{2,1,0:T(8,128)(2,1)} %aggregate_tiles.1), calls=%async_computation | async-start | bytes 3145728 | tf_op jit(solution)/shard_map/all_to_all | solution.py:249
  70.6 3.5 %collective-permute-start = (bf16[4,16,48,256]{3,2,1,0:T(8,128)(2,1)S(1)}, bf16[4,16,48,256]{3,2,1,0:T(8,128)(2,1)S(1)}, u32[]{:S(2)}, u32[]{:S(2)}) collective-permute-start(bf16[4,16,48,256]{3,2,1,0:T(8,128)(2,1)S(1)} %get-tuple-element.15), channel_id=1, source_target_pairs={{0,1},{1,0},{2,3},{3,2},{4,5},{5,4},{6,7},{7,6},{8,9},{9,8},{10,11... | collective-permute-start | bytes 4718600 | tf_op jit(solution)/shard_map/ppermute | solution.py:256
  106.7 4.2 %collective-permute-start.1 = (f32[48,256]{1,0:T(8,128)S(1)}, f32[48,256]{1,0:T(8,128)S(1)}, u32[]{:S(2)}, u32[]{:S(2)}) collective-permute-start(f32[48,256]{1,0:T(8,128)S(1)} %convert_reduce_fusion), channel_id=1, source_target_pairs={{0,96},{32,0},{64,32},{96,64},{1,97},{33,1},{65,33},{97,65},{2,98}... | collective-permute-start | bytes 147464 | tf_op jit(solution)/shard_map/ppermute | solution.py:233
  107.5 5.6 %collective-permute-start.2 = (f32[48,256]{1,0:T(8,128)S(1)}, f32[48,256]{1,0:T(8,128)S(1)}, u32[]{:S(2)}, u32[]{:S(2)}) collective-permute-start(f32[48,256]{1,0:T(8,128)S(1)} %convert_reduce_fusion), channel_id=1, source_target_pairs={{0,64},{32,96},{64,0},{96,32},{1,65},{33,97},{65,1},{97,33},{2,66}... | collective-permute-start | bytes 147464 | tf_op jit(solution)/shard_map/ppermute | solution.py:233
  108.8 5.3 %collective-permute-start.3 = (f32[48,256]{1,0:T(8,128)S(1)}, f32[48,256]{1,0:T(8,128)S(1)}, u32[]{:S(2)}, u32[]{:S(2)}) collective-permute-start(f32[48,256]{1,0:T(8,128)S(1)} %convert_reduce_fusion), channel_id=1, source_target_pairs={{0,32},{32,64},{64,96},{96,0},{1,33},{33,65},{65,97},{97,1},{2,34}... | collective-permute-start | bytes 147464 | tf_op jit(solution)/shard_map/ppermute | solution.py:233

commit v4 on v3

--- a/solution.py
+++ b/solution.py
@@ -40,7 +40,7 @@
             num_scalar_prefetch=1,
             grid=(1,),
             in_specs=[pl.BlockSpec(memory_space=pl.ANY)],
-            out_specs=pl.BlockSpec((count,) + feat.shape[1:], lambda i, b: (0, 0, 0)),
+            out_specs=pl.BlockSpec(memory_space=pl.ANY),
             scratch_shapes=[pltpu.SemaphoreType.DMA(())],
         ),
         compiler_params=pltpu.CompilerParams(vmem_limit_bytes=56 * MIB),
@@ -151,8 +151,8 @@
 
 def dense_rest_body(
     core_ref, agg_ref, comb_self_hbm, pre_hbm, weight_hbm, cot_hbm,
-    hidden_hbm, send_ref, keep_ref,
-    comb_ref, grad_ref, hidden_ref, comb_self_ref, pre_ref, weight_ref, cot_ref, sem,
+    total_hbm, comb_ref, grad_ref, send_ref,
+    comb_self_ref, pre_ref, weight_ref, cot_ref, sem,
 ):
     half, nodes = comb_ref.shape
     chunk = nodes // 2
@@ -175,58 +175,82 @@
         loads[1 + 2 * m].wait()
         loads[2 + 2 * m].wait()
         pre = pre_ref[rows, :] + part
-        decay = jnp.exp(jnp.minimum(pre, 0.0))
-        hidden_ref[rows, :] = jnp.where(pre > 0, pre, decay - 1.0).astype(BF)
-        grad_ref[rows, :] = (cot_ref[rows, :].astype(F32) * decay).astype(BF)
-        stores.append(pltpu.make_async_copy(hidden_ref.at[rows], hidden_hbm.at[rows], sem.at[6 + m]))
+        pre_ref[rows, :] = pre
+        stores.append(pltpu.make_async_copy(pre_ref.at[rows], total_hbm.at[rows], sem.at[6 + m]))
         stores[m].start()
+        grad_ref[rows, :] = (cot_ref[rows, :].astype(F32) * jnp.exp(jnp.minimum(pre, 0.0))).astype(BF)
     loads[5].wait()
-    core = core_ref[0]
-    zs, blocks, share, width = send_ref.shape
-    for dest, out_ref in ((1 - core, send_ref), (core, keep_ref)):
-        lhs = jnp.concatenate(
-            [
-                source[pl.ds(pl.multiple_of((2 * b + dest) * share, share), share), :]
-                for source in (comb_self_ref, comb_ref)
-                for b in range(blocks // 2)
-            ],
-            axis=0,
-        )
-        for z in range(zs):
-            total = jnp.dot(lhs, grad_ref[:, pl.ds(z * width, width)], preferred_element_type=F32)
-            out_ref[z] = total.reshape(blocks, share, width).astype(out_ref.dtype)
+    weight_terms(1 - core_ref[0], comb_self_ref, comb_ref, grad_ref, send_ref)
     for store in stores:
         store.wait()
+
+
+def weight_terms(dest, comb_self_ref, comb_ref, grad_ref, out_ref):
+    zs, blocks, share, width = out_ref.shape
+    lhs = jnp.concatenate(
+        [
+            source[pl.ds(pl.multiple_of((2 * b + dest) * share, share), share), :]
+            for source in (comb_self_ref, comb_ref)
+            for b in range(blocks // 2)
+        ],
+        axis=0,
+    )
+    for z in range(zs):
+        total = jnp.dot(lhs, grad_ref[:, pl.ds(z * width, width)], preferred_element_type=F32)
+        out_ref[z] = total.reshape(blocks, share, width).astype(out_ref.dtype)
+
+
+def pieces_of(half, hid):
+    return (4, 16, half // 16, hid // 4)
 
 
 def dense_rest(core, own_agg, comb_self, pre, weight, cot):
     nodes, hid = cot.shape
     half = comb_self.shape[0]
-    pieces = (4, 16, half // 16, hid // 4)
     vmem = pl.BlockSpec(memory_space=pltpu.VMEM)
     return pl.pallas_call(
         dense_rest_body,
         out_shape=(
-            jax.ShapeDtypeStruct((nodes, hid), BF),
-            pltpu.VMEM(pieces, BF),
-            pltpu.VMEM(pieces, F32),
+            pltpu.HBM((nodes, hid), F32),
+            pltpu.VMEM((half, nodes), BF),
+            pltpu.VMEM((nodes, hid), BF),
+            pltpu.VMEM(pieces_of(half, hid), BF),
         ),
         in_specs=[pl.BlockSpec(memory_space=pltpu.SMEM), vmem]
         + [pl.BlockSpec(memory_space=pl.ANY)] * 4,
-        out_specs=(pl.BlockSpec(memory_space=pl.ANY), vmem, vmem),
+        out_specs=(pl.BlockSpec(memory_space=pl.ANY),) + (vmem,) * 3,
         scratch_shapes=[
-            pltpu.VMEM((half, nodes), BF),
-            pltpu.VMEM((nodes, hid), BF),
-            pltpu.VMEM((nodes, hid), BF),
             pltpu.VMEM((half, nodes), BF),
             pltpu.VMEM((nodes, hid), F32),
             pltpu.VMEM((half, hid), BF),
             pltpu.VMEM((nodes, hid), BF),
             pltpu.SemaphoreType.DMA((8,)),
         ],
-        compiler_params=pltpu.CompilerParams(vmem_limit_bytes=32 * MIB),
+        compiler_params=pltpu.CompilerParams(vmem_limit_bytes=24 * MIB),
         name="dense_rest",
     )(core, in_vmem(own_agg), *map(in_hbm, (comb_self, pre, weight, cot)))
+
+
+def dense_keep_body(core_ref, comb_self_hbm, comb_ref, grad_ref, keep_ref, comb_self_ref, sem):
+    load = pltpu.make_async_copy(comb_self_hbm, comb_self_ref, sem)
+    load.start()
+    load.wait()
+    weight_terms(core_ref[0], comb_self_ref, comb_ref, grad_ref, keep_ref)
+
+
+def dense_keep(core, comb_self, comb_agg, grad):
+    half, nodes = comb_self.shape
+    hid = grad.shape[1]
+    vmem = pl.BlockSpec(memory_space=pltpu.VMEM)
+    return pl.pallas_call(
+        dense_keep_body,
+        out_shape=pltpu.VMEM(pieces_of(half, hid), F32),
+        in_specs=[pl.BlockSpec(memory_space=pltpu.SMEM), pl.BlockSpec(memory_space=pl.ANY), vmem, vmem],
+        out_specs=vmem,
+        scratch_shapes=[pltpu.VMEM((half, nodes), BF), pltpu.SemaphoreType.DMA(())],
+        compiler_params=pltpu.CompilerParams(vmem_limit_bytes=16 * MIB),
+        name="dense_keep",
+    )(core, in_hbm(comb_self), in_vmem(comb_agg), in_vmem(grad))
 
 
 def shift(value, axis, k):
@@ -250,10 +274,13 @@
     shape = (32, nrb // 32, width, side)
     comb_self, pre = dense_self(own_self.reshape(shape), weight, proj_bias[None])
     core = lax.axis_index("core").astype(jnp.int32).reshape(1)
-    hidden, send, keep = dense_rest(
+    pre, comb_agg, grad, send = dense_rest(
         core, own_agg.reshape(shape), comb_self, pre, weight, cotangent[0]
     )
-    pair = (keep + lax.ppermute(send, "core", [(0, 1), (1, 0)]).astype(F32)).astype(BF)
+    other = lax.ppermute(send, "core", [(0, 1), (1, 0)])
+    keep = dense_keep(core, comb_self, comb_agg, grad)
+    hidden = jnp.where(pre > 0, pre, jnp.exp(jnp.minimum(pre, 0.0)) - 1.0).astype(BF)
+    pair = (keep + other.astype(F32)).astype(BF)
     pair = pair.reshape((64,) + pair.shape[2:])
     pieces = lax.all_to_all(pair, ("grp", "x", "y"), 0, 0, tiled=True)
     piece = jnp.sum(pieces.astype(F32), axis=0)

time: 115 us -> 161 us (1.40)
  Pallas kernels: 34.8 us -> 81.9 us
  blocking collectives: 31.7 us -> 0 us
  waiting for transfers between devices: 32.4 us -> 49.4 us
  starting transfers between devices: 13.6 us -> 21.2 us
  other arithmetic: 1.6 us -> 7 us
    pallas_call x1, Pallas kernels: 3.72 us -> 49.5 us  [gather_self(): pl.pallas_call(gather_body, out_shape=jax.ShapeDtypeStruct((count,) + fea...]
    all_to_all x1 -> x0, blocking collectives: 31.7 us -> none  [per_device(): pieces = lax.all_to_all(pair, ('grp', 'x', 'y'), 0, 0, tiled=True)]
    all_to_all x0 -> x1, waiting for transfers between devices: none -> 24.6 us  [per_device(): pieces = lax.all_to_all(pair, ('grp', 'x', 'y'), 0, 0, tiled=True)]
    all_to_all x0 -> x1, starting transfers between devices: none -> 7.48 us  [per_device(): pieces = lax.all_to_all(pair, ('grp', 'x', 'y'), 0, 0, tiled=True)]
    broadcast_in_dim x0 -> x1, other arithmetic: none -> 4.39 us  [per_device(): return (hidden[None], jnp.concatenate(columns, axis=1))]
    ppermute x3, waiting for transfers between devices: 5.27 us -> 0.91 us  [shift(): return lax.ppermute(value, axis, [(i, (i + k) % 4) for i in range(4)])]
    ppermute x1, waiting for transfers between devices: 3.4 us -> 0.18 us  [per_device(): other = lax.ppermute(send, 'core', [(0, 1), (1, 0)])]
    pallas_call x1 -> x2, Pallas kernels: 8.56 us -> 9.9 us  [the longest x1 6.69 us: dense_rest(): pl.pallas_call(dense_rest_body, out_shape=(pltpu.HBM((nodes, hid), F32),...]
  transfers between devices with their start and end apart: 6 -> 7, of which waited for: 6 -> 5; matrix products, arithmetic and copies ran while one was open for 0% -> 3% of each run, Pallas kernels for 20% -> 16%
where the time goes in v4:
time: 161 us; the launch traced here: 160 us
  Pallas kernels  81.9 us (51%)
  waiting for transfers between devices  49.4 us (31%)
  starting transfers between devices  21.2 us (13%)
  other arithmetic  7 us (4%)
    pallas_call x1, Pallas kernels, gather_self(): pl.pallas_call(gather_body, out_shape=jax.ShapeDtypeStruct((count,) + fea...  49.5 us
    all_to_all x1, waiting for transfers between devices, per_device(): pieces = lax.all_to_all(pair, ('grp', 'x', 'y'), 0, 0, tiled=True)  24.6 us
    all_to_all x1, waiting for transfers between devices, per_device(): own_agg = lax.all_to_all(agg, FEAT, 0, 0, tiled=True)  17.3 us
    pallas_call x1, Pallas kernels, aggregate_tiles(): pl.pallas_call(functools.partial(aggregate_body, unroll), out_shape=jax.S...  16.7 us
    all_to_all x1, starting transfers between devices, per_device(): pieces = lax.all_to_all(pair, ('grp', 'x', 'y'), 0, 0, tiled=True)  7.48 us
    all_to_all x1, starting transfers between devices, per_device(): own_self = lax.all_to_all(mine, FEAT, 0, 0, tiled=True)  7.42 us
    pallas_call x1, Pallas kernels, dense_rest(): pl.pallas_call(dense_rest_body, out_shape=(pltpu.HBM((nodes, hid), F32),...  6.69 us
    all_to_all x1, waiting for transfers between devices, per_device(): own_self = lax.all_to_all(mine, FEAT, 0, 0, tiled=True)  6.41 us
  transfers between devices with their start and end apart: 7, of which 5 were waited for; matrix products, arithmetic and copies ran while one was open for 3% of the time, Pallas kernels for 16%

profile of v4, /device:TPU:0, one launch (start us, length us, event | category | flops | bytes accessed | tf_op | source)
XLA Modules:
  0.0 160.2 jit_solution(13438206794420281313)
XLA Ops:
  0.6 49.5 %gather_self.1 = bf16[256,24,128]{2,1,0:T(8,128)(2,1)} custom-call(s32[1,256]{1,0:T(1,128)} %blocks_ref.1, bf16[768,24,128]{2,1,0:T(8,128)(2,1)} %bitcast.12), custom_call_target="tpu_custom_call" | custom-call | tf_op jit(solution)/shard_map/gather_self/pallas_call | solution.py:36
  50.1 7.4 %all-to-all-start.1 = ((bf16[256,24,128]{2,1,0:T(8,128)(2,1)}), bf16[256,24,128]{2,1,0:T(8,128)(2,1)S(1)}, u32[]{:S(2)}, u32[]{:S(2)}) async-start(bf16[256,24,128]{2,1,0:T(8,128)(2,1)} %gather_self.1), calls=%async_computation.1 | async-start | bytes 3145728 | tf_op jit(solution)/shard_map/all_to_all | solution.py:271
  57.6 16.7 %aggregate_tiles.1 = bf16[256,24,128]{2,1,0:T(8,128)(2,1)} custom-call(s32[1,384]{1,0:T(1,128)} %rows_ref.1, s32[1,384]{1,0:T(1,128)} %cols_ref.1, bf16[768,24,128]{2,1,0:T(8,128)(2,1)} %bitcast.13, bf16[384,128,128]{2,1,0:T(8,128)(2,1)} %bitcast.14), custom_call_target="tpu_custom_call" | custom-call | flops 301989888 | bytes 18874368 | tf_op jit(solution)/shard_map/aggregate_tiles/pallas_call | solution.py:90
  74.3 6.4 %all-to-all-done.1 = bf16[256,24,128]{2,1,0:T(8,128)(2,1)S(1)} async-done(((bf16[256,24,128]{2,1,0:T(8,128)(2,1)}), bf16[256,24,128]{2,1,0:T(8,128)(2,1)S(1)}, u32[]{:S(2)}, u32[]{:S(2)}) %all-to-all-start.1) | async-done | bytes 1572896 | tf_op jit(solution)/shard_map/all_to_all | solution.py:271
  80.7 4.0 %all-to-all-start = ((bf16[256,24,128]{2,1,0:T(8,128)(2,1)}), bf16[256,24,128]{2,1,0:T(8,128)(2,1)S(1)}, u32[]{:S(2)}, u32[]{:S(2)}) async-start(bf16[256,24,128]{2,1,0:T(8,128)(2,1)} %aggregate_tiles.1), calls=%async_computation | async-start | bytes 3145728 | tf_op jit(solution)/shard_map/all_to_all | solution.py:273
  84.7 5.8 %dense_self.1 = (bf16[768,1024]{1,0:T(8,128)(2,1)}, f32[1024,1024]{1,0:T(8,128)}) custom-call(bf16[32,8,24,128]{3,2,1,0:T(8,128)(2,1)S(1)} %bitcast.11, bf16[1536,1024]{1,0:T(8,128)(2,1)} %weight_hbm.1, f32[1,1024]{1,0:T(1,128)} %bitcast.16), custom_call_target="tpu_custom_call" | custom-call | tf_op jit(solution)/shard_map/dense_self/pallas_call | solution.py:139
  90.5 17.3 %all-to-all-done = bf16[256,24,128]{2,1,0:T(8,128)(2,1)S(1)} async-done(((bf16[256,24,128]{2,1,0:T(8,128)(2,1)}), bf16[256,24,128]{2,1,0:T(8,128)(2,1)S(1)}, u32[]{:S(2)}, u32[]{:S(2)}) %all-to-all-start) | async-done | bytes 1572896 | tf_op jit(solution)/shard_map/all_to_all | solution.py:273
  107.8 6.7 %dense_rest.1 = (f32[1024,1024]{1,0:T(8,128)}, bf16[768,1024]{1,0:T(8,128)(2,1)S(1)}, bf16[1024,1024]{1,0:T(8,128)(2,1)S(1)}, bf16[4,16,48,256]{3,2,1,0:T(8,128)(2,1)S(1)}) custom-call(s32[1]{0:T(128)} %bitcast.core_ref, bf16[32,8,24,128]{3,2,1,0:T(8,128)(2,1)S(1)} %bitcast.10, bf16[768,1024]{1,0:T(8,128)(2,1)} %get-tuple-element.12.comb_self_hbm, ...), custom_call_target="tpu_custom_call" | custom-call | tf_op jit(solution)/shard_map/dense_rest/pallas_call | solution.py:211
  114.5 0.1 collective-permute-start
  114.6 3.2 %dense_keep.1 = f32[4,16,48,256]{3,2,1,0:T(8,128)S(1)} custom-call(s32[1]{0:T(128)} %bitcast.core_ref, bf16[768,1024]{1,0:T(8,128)(2,1)} %get-tuple-element.12.comb_self_hbm, bf16[768,1024]{1,0:T(8,128)(2,1)S(1)} %get-tuple-element.15.comb_ref, bf16[1024,1024]{1,0:T(8,128)(2,1)S(1)} %get-tuple-element.16.grad_ref), custom_call_target="tpu_custom_call" | custom-call | tf_op jit(solution)/shard_map/dense_keep/pallas_call | solution.py:245
  117.8 0.2 collective-permute-done
  118.0 1.7 %add_convert_fusion = bf16[4,16,48,256]{3,2,1,0:T(8,128)(2,1)} fusion(f32[4,16,48,256]{3,2,1,0:T(8,128)S(1)} %dense_keep.1, bf16[4,16,48,256]{3,2,1,0:T(8,128)(2,1)S(1)} %collective-permute-done), kind=kLoop, calls=%fused_computation.3 | loop fusion | flops 2359296 | bytes 6291456 | tf_op jit(solution)/shard_map/convert_element_type | solution.py:283
  119.6 7.5 %all-to-all-start.2 = ((bf16[64,48,256]{2,1,0:T(8,128)(2,1)}), bf16[64,48,256]{2,1,0:T(8,128)(2,1)S(1)}, u32[]{:S(2)}, u32[]{:S(2)}) async-start(bf16[64,48,256]{2,1,0:T(8,128)(2,1)} %bitcast.8), calls=%async_computation.2 | async-start | bytes 3145728 | tf_op jit(solution)/shard_map/all_to_all | solution.py:285
  127.2 24.6 %all-to-all-done.2 = bf16[64,48,256]{2,1,0:T(8,128)(2,1)S(1)} async-done(((bf16[64,48,256]{2,1,0:T(8,128)(2,1)}), bf16[64,48,256]{2,1,0:T(8,128)(2,1)S(1)}, u32[]{:S(2)}, u32[]{:S(2)}) %all-to-all-start.2) | async-done | bytes 1572896 | tf_op jit(solution)/shard_map/all_to_all | solution.py:285
  151.7 0.2 convert_reduce_fusion
  152.0 0.8 collective-permute-start.1
  152.8 1.4 collective-permute-start.2
  154.2 0.0 collective-permute-start.3
  154.2 4.4 %fusion.1 = bf16[1,1024,1024]{2,1,0:T(8,128)(2,1)} fusion(f32[1024,1024]{1,0:T(8,128)} %get-tuple-element.14), kind=kLoop, calls=%fused_computation.4 | loop fusion | flops 5242880 | bytes 6291456 | tf_op jit(solution)/shard_map/broadcast_in_dim | solution.py:295
  158.6 0.0 collective-permute-done.1
  158.6 0.0 collective-permute-done.2
  158.6 0.9 collective-permute-done.3
  159.5 0.7 pad_maximum_fusion
  (1 shorter events, 0.0 us)
Async XLA Ops:
  50.1 30.6 %all-to-all-start.1 = ((bf16[256,24,128]{2,1,0:T(8,128)(2,1)}), bf16[256,24,128]{2,1,0:T(8,128)(2,1)S(1)}, u32[]{:S(2)}, u32[]{:S(2)}) async-start(bf16[256,24,128]{2,1,0:T(8,128)(2,1)} %gather_self.1), calls=%async_computation.1 | async-start | bytes 3145728 | tf_op jit(solution)/shard_map/all_to_all | solution.py:271
  80.7 27.1 %all-to-all-start = ((bf16[256,24,128]{2,1,0:T(8,128)(2,1)}), bf16[256,24,128]{2,1,0:T(8,128)(2,1)S(1)}, u32[]{:S(2)}, u32[]{:S(2)}) async-start(bf16[256,24,128]{2,1,0:T(8,128)(2,1)} %aggregate_tiles.1), calls=%async_computation | async-start | bytes 3145728 | tf_op jit(solution)/shard_map/all_to_all | solution.py:273
  114.5 3.5 %collective-permute-start = (bf16[4,16,48,256]{3,2,1,0:T(8,128)(2,1)S(1)}, bf16[4,16,48,256]{3,2,1,0:T(8,128)(2,1)S(1)}, u32[]{:S(2)}, u32[]{:S(2)}) collective-permute-start(bf16[4,16,48,256]{3,2,1,0:T(8,128)(2,1)S(1)} %get-tuple-element.17), channel_id=1, source_target_pairs={{0,1},{1,0},{2,3},{3,2},{4,5},{5,4},{6,7},{7,6},{8,9},{9,8},{10,11... | collective-permute-start | bytes 4718600 | tf_op jit(solution)/shard_map/ppermute | solution.py:280
  119.6 32.1 %all-to-all-start.2 = ((bf16[64,48,256]{2,1,0:T(8,128)(2,1)}), bf16[64,48,256]{2,1,0:T(8,128)(2,1)S(1)}, u32[]{:S(2)}, u32[]{:S(2)}) async-start(bf16[64,48,256]{2,1,0:T(8,128)(2,1)} %bitcast.8), calls=%async_computation.2 | async-start | bytes 3145728 | tf_op jit(solution)/shard_map/all_to_all | solution.py:285
  152.0 6.6 %collective-permute-start.1 = (f32[48,256]{1,0:T(8,128)S(1)}, f32[48,256]{1,0:T(8,128)S(1)}, u32[]{:S(2)}, u32[]{:S(2)}) collective-permute-start(f32[48,256]{1,0:T(8,128)S(1)} %convert_reduce_fusion), channel_id=1, source_target_pairs={{0,96},{32,0},{64,32},{96,64},{1,97},{33,1},{65,33},{97,65},{2,98}... | collective-permute-start | bytes 147464 | tf_op jit(solution)/shard_map/ppermute | solution.py:257
  152.8 5.8 %collective-permute-start.2 = (f32[48,256]{1,0:T(8,128)S(1)}, f32[48,256]{1,0:T(8,128)S(1)}, u32[]{:S(2)}, u32[]{:S(2)}) collective-permute-start(f32[48,256]{1,0:T(8,128)S(1)} %convert_reduce_fusion), channel_id=1, source_target_pairs={{0,64},{32,96},{64,0},{96,32},{1,65},{33,97},{65,1},{97,33},{2,66}... | collective-permute-start | bytes 147464 | tf_op jit(solution)/shard_map/ppermute | solution.py:257
  154.2 5.3 %collective-permute-start.3 = (f32[48,256]{1,0:T(8,128)S(1)}, f32[48,256]{1,0:T(8,128)S(1)}, u32[]{:S(2)}, u32[]{:S(2)}) collective-permute-start(f32[48,256]{1,0:T(8,128)S(1)} %convert_reduce_fusion), channel_id=1, source_target_pairs={{0,32},{32,64},{64,96},{96,0},{1,33},{33,65},{65,97},{97,1},{2,34}... | collective-permute-start | bytes 147464 | tf_op jit(solution)/shard_map/ppermute | solution.py:257

commit v5 on v4

--- a/solution.py
+++ b/solution.py
@@ -40,7 +40,7 @@
             num_scalar_prefetch=1,
             grid=(1,),
             in_specs=[pl.BlockSpec(memory_space=pl.ANY)],
-            out_specs=pl.BlockSpec(memory_space=pl.ANY),
+            out_specs=pl.BlockSpec((count,) + feat.shape[1:], lambda i, b: (0, 0, 0)),
             scratch_shapes=[pltpu.SemaphoreType.DMA(())],
         ),
         compiler_params=pltpu.CompilerParams(vmem_limit_bytes=56 * MIB),
@@ -186,7 +186,7 @@
 
 
 def weight_terms(dest, comb_self_ref, comb_ref, grad_ref, out_ref):
-    zs, blocks, share, width = out_ref.shape
+    blocks, share, hid = out_ref.shape
     lhs = jnp.concatenate(
         [
             source[pl.ds(pl.multiple_of((2 * b + dest) * share, share), share), :]
@@ -195,13 +195,15 @@
         ],
         axis=0,
     )
-    for z in range(zs):
-        total = jnp.dot(lhs, grad_ref[:, pl.ds(z * width, width)], preferred_element_type=F32)
-        out_ref[z] = total.reshape(blocks, share, width).astype(out_ref.dtype)
+    width = hid // 4
+    for n in range(4):
+        cols = pl.ds(n * width, width)
+        total = jnp.dot(lhs, grad_ref[:, cols], preferred_element_type=F32)
+        out_ref[:, :, cols] = total.reshape(blocks, share, width).astype(out_ref.dtype)
 
 
 def pieces_of(half, hid):
-    return (4, 16, half // 16, hid // 4)
+    return (16, half // 16, hid)
 
 
 def dense_rest(core, own_agg, comb_self, pre, weight, cot):
@@ -251,6 +253,41 @@
         compiler_params=pltpu.CompilerParams(vmem_limit_bytes=16 * MIB),
         name="dense_keep",
     )(core, in_hbm(comb_self), in_vmem(comb_agg), in_vmem(grad))
+
+
+def sum_pieces_body(pieces_ref, sum_ref):
+    sum_ref[...] = jnp.sum(pieces_ref[...].astype(F32), axis=0).astype(BF)
+
+
+def sum_pieces(pieces):
+    vmem = pl.BlockSpec(memory_space=pltpu.VMEM)
+    return pl.pallas_call(
+        sum_pieces_body,
+        out_shape=pltpu.VMEM(pieces.shape[1:], BF),
+        in_specs=[vmem],
+        out_specs=vmem,
+        compiler_params=pltpu.CompilerParams(vmem_limit_bytes=16 * MIB),
+        name="sum_pieces",
+    )(in_vmem(pieces))
+
+
+def hidden_body(pre_ref, after_ref, hidden_ref):
+    pre = pre_ref[...]
+    hidden_ref[...] = jnp.where(pre > 0, pre, jnp.exp(jnp.minimum(pre, 0.0)) - 1.0).astype(BF)
+
+
+def hidden_of(pre, after):
+    nodes, hid = pre.shape
+    rows = nodes // 8
+    return pl.pallas_call(
+        hidden_body,
+        out_shape=jax.ShapeDtypeStruct((nodes, hid), BF),
+        grid=(8,),
+        in_specs=[pl.BlockSpec((rows, hid), lambda i: (i, 0)), pl.BlockSpec(memory_space=pl.ANY)],
+        out_specs=pl.BlockSpec((rows, hid), lambda i: (i, 0)),
+        compiler_params=pltpu.CompilerParams(vmem_limit_bytes=56 * MIB),
+        name="hidden",
+    )(pre, after)
 
 
 def shift(value, axis, k):
@@ -279,20 +316,14 @@
     )
     other = lax.ppermute(send, "core", [(0, 1), (1, 0)])
     keep = dense_keep(core, comb_self, comb_agg, grad)
-    hidden = jnp.where(pre > 0, pre, jnp.exp(jnp.minimum(pre, 0.0)) - 1.0).astype(BF)
     pair = (keep + other.astype(F32)).astype(BF)
-    pair = pair.reshape((64,) + pair.shape[2:])
-    pieces = lax.all_to_all(pair, ("grp", "x", "y"), 0, 0, tiled=True)
-    piece = jnp.sum(pieces.astype(F32), axis=0)
-    near = [piece] + [shift(piece, "grp", -k) for k in (1, 2, 3)]
-    grp = lax.axis_index("grp")
-    columns = []
-    for z in range(4):
-        k = (z - grp) % 4
-        columns.append(
-            jnp.where(k == 0, near[0], jnp.where(k == 1, near[1], jnp.where(k == 2, near[2], near[3])))
-        )
-    return hidden[None], jnp.concatenate(columns, axis=1)
+    pieces = lax.all_to_all(pair, ("x", "y"), 0, 0, tiled=True)
+    mine = sum_pieces(pieces)
+    hidden = hidden_of(pre, mine)
+    n1, n2, n3 = (shift(mine, "grp", -k).astype(F32) for k in (1, 2, 3))
+    odd = lax.axis_index("grp") % 2 == 1
+    total = (mine.astype(F32) + jnp.where(odd, n3, n1)) + (n2 + jnp.where(odd, n1, n3))
+    return hidden[None], total
 
 
 def solution(mesh):

time: 161 us -> 114 us (0.71)
  Pallas kernels: 81.9 us -> 42.8 us
  blocking collectives: 0 us -> 26.1 us
  waiting for transfers between devices: 49.4 us -> 23.9 us
  other arithmetic: 7 us -> 2.22 us
  starting transfers between devices: 21.2 us -> 17.5 us
    pallas_call x1, Pallas kernels: 49.5 us -> 3.72 us  [gather_self(): pl.pallas_call(gather_body, out_shape=jax.ShapeDtypeStruct((count,) + fea...]
    all_to_all x0 -> x1, blocking collectives: none -> 26.1 us  [per_device(): pieces = lax.all_to_all(pair, ('x', 'y'), 0, 0, tiled=True)]
    all_to_all x1 -> x0, waiting for transfers between devices: 24.6 us -> none  [per_device(): pieces = lax.all_to_all(pair, ('grp', 'x', 'y'), 0, 0, tiled=True)]
    all_to_all x1 -> x0, starting transfers between devices: 7.48 us -> none  [per_device(): pieces = lax.all_to_all(pair, ('grp', 'x', 'y'), 0, 0, tiled=True)]
    pallas_call x0 -> x2, Pallas kernels: none -> 6.63 us  [the longest x1 6.42 us: hidden_of(): pl.pallas_call(hidden_body, out_shape=jax.ShapeDtypeStruct((nodes, hid),...]
    broadcast_in_dim x1 -> x0, other arithmetic: 4.39 us -> none  [per_device(): return (hidden[None], jnp.concatenate(columns, axis=1))]
    ppermute x3, starting transfers between devices: 2.22 us -> 5.98 us  [shift(): return lax.ppermute(value, axis, [(i, (i + k) % 4) for i in range(4)])]
    add x0 -> x1, other arithmetic: none -> 1.63 us  [per_device(): mine.astype(F32) + jnp.where(odd, n3, n1) + (n2 + jnp.where(odd, n1, n3))]
  transfers between devices with their start and end apart: 7 -> 6, of which waited for: 5 -> 3; matrix products, arithmetic and copies ran while one was open for 3% -> 0% of each run, Pallas kernels for 16% -> 28%
where the time goes in v5:
time: 114 us; the launch traced here: 113 us
  Pallas kernels  42.8 us (38%)
  blocking collectives  26.1 us (23%)
  waiting for transfers between devices  23.9 us (21%)
  starting transfers between devices  17.5 us (15%)
  other arithmetic  2.22 us (2%)
    all_to_all x1, blocking collectives, per_device(): pieces = lax.all_to_all(pair, ('x', 'y'), 0, 0, tiled=True)  26.1 us
    all_to_all x1, waiting for transfers between devices, per_device(): own_agg = lax.all_to_all(agg, FEAT, 0, 0, tiled=True)  17.3 us
    pallas_call x1, Pallas kernels, aggregate_tiles(): pl.pallas_call(functools.partial(aggregate_body, unroll), out_shape=jax.S...  16.7 us
    all_to_all x1, starting transfers between devices, per_device(): own_self = lax.all_to_all(mine, FEAT, 0, 0, tiled=True)  7.41 us
    pallas_call x1, Pallas kernels, dense_rest(): pl.pallas_call(dense_rest_body, out_shape=(pltpu.HBM((nodes, hid), F32),...  6.69 us
    pallas_call x1, Pallas kernels, hidden_of(): pl.pallas_call(hidden_body, out_shape=jax.ShapeDtypeStruct((nodes, hid),...  6.42 us
    all_to_all x1, waiting for transfers between devices, per_device(): own_self = lax.all_to_all(mine, FEAT, 0, 0, tiled=True)  6.41 us
    ppermute x3, starting transfers between devices, shift(): return lax.ppermute(value, axis, [(i, (i + k) % 4) for i in range(4)])  5.98 us
  transfers between devices with their start and end apart: 6, of which 3 were waited for; matrix products, arithmetic and copies ran while one was open for 0% of the time, Pallas kernels for 28%

profile of v5, /device:TPU:0, one launch (start us, length us, event | category | flops | bytes accessed | tf_op | source)
XLA Modules:
  0.0 113.2 jit_solution(3857917022261128897)
XLA Ops:
  0.6 3.7 %gather_self.1 = bf16[256,24,128]{2,1,0:T(8,128)(2,1)} custom-call(s32[1,256]{1,0:T(1,128)} %blocks_ref.1, bf16[768,24,128]{2,1,0:T(8,128)(2,1)} %bitcast.10), custom_call_target="tpu_custom_call" | custom-call | tf_op jit(solution)/shard_map/gather_self/pallas_call | solution.py:36
  4.4 7.4 %all-to-all-start.1 = ((bf16[256,24,128]{2,1,0:T(8,128)(2,1)}), bf16[256,24,128]{2,1,0:T(8,128)(2,1)S(1)}, u32[]{:S(2)}, u32[]{:S(2)}) async-start(bf16[256,24,128]{2,1,0:T(8,128)(2,1)} %gather_self.1), calls=%async_computation.1 | async-start | bytes 3145728 | tf_op jit(solution)/shard_map/all_to_all | solution.py:308
  11.8 16.7 %aggregate_tiles.1 = bf16[256,24,128]{2,1,0:T(8,128)(2,1)} custom-call(s32[1,384]{1,0:T(1,128)} %rows_ref.1, s32[1,384]{1,0:T(1,128)} %cols_ref.1, bf16[768,24,128]{2,1,0:T(8,128)(2,1)} %bitcast.11, bf16[384,128,128]{2,1,0:T(8,128)(2,1)} %bitcast.12), custom_call_target="tpu_custom_call" | custom-call | flops 301989888 | bytes 18874368 | tf_op jit(solution)/shard_map/aggregate_tiles/pallas_call | solution.py:90
  28.5 6.4 %all-to-all-done.1 = bf16[256,24,128]{2,1,0:T(8,128)(2,1)S(1)} async-done(((bf16[256,24,128]{2,1,0:T(8,128)(2,1)}), bf16[256,24,128]{2,1,0:T(8,128)(2,1)S(1)}, u32[]{:S(2)}, u32[]{:S(2)}) %all-to-all-start.1) | async-done | bytes 1572896 | tf_op jit(solution)/shard_map/all_to_all | solution.py:308
  34.9 4.0 %all-to-all-start = ((bf16[256,24,128]{2,1,0:T(8,128)(2,1)}), bf16[256,24,128]{2,1,0:T(8,128)(2,1)S(1)}, u32[]{:S(2)}, u32[]{:S(2)}) async-start(bf16[256,24,128]{2,1,0:T(8,128)(2,1)} %aggregate_tiles.1), calls=%async_computation | async-start | bytes 3145728 | tf_op jit(solution)/shard_map/all_to_all | solution.py:310
  38.9 5.8 %dense_self.1 = (bf16[768,1024]{1,0:T(8,128)(2,1)}, f32[1024,1024]{1,0:T(8,128)}) custom-call(bf16[32,8,24,128]{3,2,1,0:T(8,128)(2,1)S(1)} %bitcast.9, bf16[1536,1024]{1,0:T(8,128)(2,1)} %weight_hbm.1, f32[1,1024]{1,0:T(1,128)} %bitcast.15), custom_call_target="tpu_custom_call" | custom-call | tf_op jit(solution)/shard_map/dense_self/pallas_call | solution.py:139
  44.7 17.3 %all-to-all-done = bf16[256,24,128]{2,1,0:T(8,128)(2,1)S(1)} async-done(((bf16[256,24,128]{2,1,0:T(8,128)(2,1)}), bf16[256,24,128]{2,1,0:T(8,128)(2,1)S(1)}, u32[]{:S(2)}, u32[]{:S(2)}) %all-to-all-start) | async-done | bytes 1572896 | tf_op jit(solution)/shard_map/all_to_all | solution.py:310
  62.0 6.7 %dense_rest.1 = (f32[1024,1024]{1,0:T(8,128)}, bf16[768,1024]{1,0:T(8,128)(2,1)S(1)}, bf16[1024,1024]{1,0:T(8,128)(2,1)S(1)}, bf16[16,48,1024]{2,1,0:T(8,128)(2,1)S(1)}) custom-call(s32[1]{0:T(128)} %bitcast.core_ref, bf16[32,8,24,128]{3,2,1,0:T(8,128)(2,1)S(1)} %bitcast.8, bf16[768,1024]{1,0:T(8,128)(2,1)} %get-tuple-element.12.comb_self_hbm, ...), custom_call_target="tpu_custom_call" | custom-call | tf_op jit(solution)/shard_map/dense_rest/pallas_call | solution.py:213
  68.7 0.1 collective-permute-start
  68.8 3.2 %dense_keep.1 = f32[16,48,1024]{2,1,0:T(8,128)S(1)} custom-call(s32[1]{0:T(128)} %bitcast.core_ref, bf16[768,1024]{1,0:T(8,128)(2,1)} %get-tuple-element.12.comb_self_hbm, bf16[768,1024]{1,0:T(8,128)(2,1)S(1)} %get-tuple-element.15.comb_ref, bf16[1024,1024]{1,0:T(8,128)(2,1)S(1)} %get-tuple-element.16.grad_ref), custom_call_target="tpu_custom_call" | custom-call | tf_op jit(solution)/shard_map/dense_keep/pallas_call | solution.py:247
  72.0 0.2 collective-permute-done
  72.2 0.6 add_convert_fusion
  72.8 26.1 %all_to_all.15.pieces_ref = bf16[16,48,1024]{2,1,0:T(8,128)(2,1)S(1)} all-to-all(bf16[16,48,1024]{2,1,0:T(8,128)(2,1)S(1)} %add_convert_fusion), channel_id=1, replica_groups=mesh['grp'=4,'x'=4,'y'=4,'core'=2] {'x','y'}, dimensions={0} | all-to-all | bytes 3145728 | tf_op jit(solution)/shard_map/all_to_all | solution.py:320
  98.9 0.2 sum_pieces.1.after_ref
  99.1 0.0 copy-start
  99.1 4.0 %collective-permute-start.3 = (bf16[48,1024]{1,0:T(8,128)(2,1)S(1)}, bf16[48,1024]{1,0:T(8,128)(2,1)S(1)}, u32[]{:S(2)}, u32[]{:S(2)}) collective-permute-start(bf16[48,1024]{1,0:T(8,128)(2,1)S(1)} %sum_pieces.1.after_ref), channel_id=1, source_target_pairs={{0,64},{32,96},{64,0},{96,32},{1,65},{33,97},{65,1},{97,33},{2,66}... | collective-permute-start | bytes 294920 | tf_op jit(solution)/shard_map/ppermute | solution.py:294
  103.1 0.7 collective-permute-start.2
  103.8 1.3 %collective-permute-start.1 = (bf16[48,1024]{1,0:T(8,128)(2,1)S(1)}, bf16[48,1024]{1,0:T(8,128)(2,1)S(1)}, u32[]{:S(2)}, u32[]{:S(2)}) collective-permute-start(bf16[48,1024]{1,0:T(8,128)(2,1)S(1)} %sum_pieces.1.after_ref), channel_id=1, source_target_pairs={{0,32},{32,64},{64,96},{96,0},{1,33},{33,65},{65,97},{97,1},{2,34}... | collective-permute-start | bytes 294920 | tf_op jit(solution)/shard_map/ppermute | solution.py:294
  105.1 0.0 copy-done
  105.1 6.4 %hidden.1 = bf16[1024,1024]{1,0:T(8,128)(2,1)} custom-call(f32[1024,1024]{1,0:T(8,128)} %get-tuple-element.14.pre_ref, bf16[48,1024]{1,0:T(8,128)(2,1)} %copy-done), custom_call_target="tpu_custom_call" | custom-call | tf_op jit(solution)/shard_map/hidden/pallas_call | solution.py:282
  111.5 0.0 collective-permute-done.3
  111.5 0.0 collective-permute-done.2
  111.5 0.0 collective-permute-done.1
  111.5 1.6 %fusion.1 = f32[48,1024]{1,0:T(8,128)} fusion(bf16[48,1024]{1,0:T(8,128)(2,1)S(1)} %collective-permute-done.2, bf16[48,1024]{1,0:T(8,128)(2,1)S(1)} %collective-permute-done.1, bf16[48,1024]{1,0:T(8,128)(2,1)S(1)} %collective-permute-done.3, bf16[48,1024]{1,0:T(8,128)(2,1)} %copy-done, pred[]{:T(512)S(6)} %eq.5), kind=kLoop, calls=%fused_computation.4 | loop fusion | flops 442368 | bytes 589825 | tf_op jit(solution)/shard_map/add | solution.py:325
Async XLA Ops:
  4.4 30.5 %all-to-all-start.1 = ((bf16[256,24,128]{2,1,0:T(8,128)(2,1)}), bf16[256,24,128]{2,1,0:T(8,128)(2,1)S(1)}, u32[]{:S(2)}, u32[]{:S(2)}) async-start(bf16[256,24,128]{2,1,0:T(8,128)(2,1)} %gather_self.1), calls=%async_computation.1 | async-start | bytes 3145728 | tf_op jit(solution)/shard_map/all_to_all | solution.py:308
  34.9 27.1 %all-to-all-start = ((bf16[256,24,128]{2,1,0:T(8,128)(2,1)}), bf16[256,24,128]{2,1,0:T(8,128)(2,1)S(1)}, u32[]{:S(2)}, u32[]{:S(2)}) async-start(bf16[256,24,128]{2,1,0:T(8,128)(2,1)} %aggregate_tiles.1), calls=%async_computation | async-start | bytes 3145728 | tf_op jit(solution)/shard_map/all_to_all | solution.py:310
  68.7 3.5 %collective-permute-start = (bf16[16,48,1024]{2,1,0:T(8,128)(2,1)S(1)}, bf16[16,48,1024]{2,1,0:T(8,128)(2,1)S(1)}, u32[]{:S(2)}, u32[]{:S(2)}) collective-permute-start(bf16[16,48,1024]{2,1,0:T(8,128)(2,1)S(1)} %get-tuple-element.17), channel_id=1, source_target_pairs={{0,1},{1,0},{2,3},{3,2},{4,5},{5,4},{6,7},{7,6},{8,9},{9,8},{10,11... | collective-permute-start | bytes 4718600 | tf_op jit(solution)/shard_map/ppermute | solution.py:317
  99.1 6.0 %copy-start = (bf16[48,1024]{1,0:T(8,128)(2,1)}, bf16[48,1024]{1,0:T(8,128)(2,1)S(1)}, u32[]{:S(2)}) copy-start(bf16[48,1024]{1,0:T(8,128)(2,1)S(1)} %sum_pieces.1.after_ref) | copy-start | bytes 294916
  99.1 12.4 %collective-permute-start.3 = (bf16[48,1024]{1,0:T(8,128)(2,1)S(1)}, bf16[48,1024]{1,0:T(8,128)(2,1)S(1)}, u32[]{:S(2)}, u32[]{:S(2)}) collective-permute-start(bf16[48,1024]{1,0:T(8,128)(2,1)S(1)} %sum_pieces.1.after_ref), channel_id=1, source_target_pairs={{0,64},{32,96},{64,0},{96,32},{1,65},{33,97},{65,1},{97,33},{2,66}... | collective-permute-start | bytes 294920 | tf_op jit(solution)/shard_map/ppermute | solution.py:294
  103.1 8.5 %collective-permute-start.2 = (bf16[48,1024]{1,0:T(8,128)(2,1)S(1)}, bf16[48,1024]{1,0:T(8,128)(2,1)S(1)}, u32[]{:S(2)}, u32[]{:S(2)}) collective-permute-start(bf16[48,1024]{1,0:T(8,128)(2,1)S(1)} %sum_pieces.1.after_ref), channel_id=1, source_target_pairs={{0,96},{32,0},{64,32},{96,64},{1,97},{33,1},{65,33},{97,65},{2,98}... | collective-permute-start | bytes 294920 | tf_op jit(solution)/shard_map/ppermute | solution.py:294
  103.8 7.7 %collective-permute-start.1 = (bf16[48,1024]{1,0:T(8,128)(2,1)S(1)}, bf16[48,1024]{1,0:T(8,128)(2,1)S(1)}, u32[]{:S(2)}, u32[]{:S(2)}) collective-permute-start(bf16[48,1024]{1,0:T(8,128)(2,1)S(1)} %sum_pieces.1.after_ref), channel_id=1, source_target_pairs={{0,32},{32,64},{64,96},{96,0},{1,33},{33,65},{65,97},{97,1},{2,34}... | collective-permute-start | bytes 294920 | tf_op jit(solution)/shard_map/ppermute | solution.py:294

commit v6 on v5

--- a/solution.py
+++ b/solution.py
@@ -151,8 +151,8 @@
 
 def dense_rest_body(
     core_ref, agg_ref, comb_self_hbm, pre_hbm, weight_hbm, cot_hbm,
-    total_hbm, comb_ref, grad_ref, send_ref,
-    comb_self_ref, pre_ref, weight_ref, cot_ref, sem,
+    hidden_hbm, comb_ref, grad_ref, send_ref,
+    comb_self_ref, pre_ref, weight_ref, cot_ref, hidden_ref, sem,
 ):
     half, nodes = comb_ref.shape
     chunk = nodes // 2
@@ -175,10 +175,11 @@
         loads[1 + 2 * m].wait()
         loads[2 + 2 * m].wait()
         pre = pre_ref[rows, :] + part
-        pre_ref[rows, :] = pre
-        stores.append(pltpu.make_async_copy(pre_ref.at[rows], total_hbm.at[rows], sem.at[6 + m]))
+        decay = jnp.exp(jnp.minimum(pre, 0.0))
+        hidden_ref[rows, :] = jnp.where(pre > 0, pre, decay - 1.0).astype(BF)
+        grad_ref[rows, :] = (cot_ref[rows, :].astype(F32) * decay).astype(BF)
+        stores.append(pltpu.make_async_copy(hidden_ref.at[rows], hidden_hbm.at[rows], sem.at[6 + m]))
         stores[m].start()
-        grad_ref[rows, :] = (cot_ref[rows, :].astype(F32) * jnp.exp(jnp.minimum(pre, 0.0))).astype(BF)
     loads[5].wait()
     weight_terms(1 - core_ref[0], comb_self_ref, comb_ref, grad_ref, send_ref)
     for store in stores:
@@ -213,7 +214,7 @@
     return pl.pallas_call(
         dense_rest_body,
         out_shape=(
-            pltpu.HBM((nodes, hid), F32),
+            pltpu.HBM((nodes, hid), BF),
             pltpu.VMEM((half, nodes), BF),
             pltpu.VMEM((nodes, hid), BF),
             pltpu.VMEM(pieces_of(half, hid), BF),
@@ -226,6 +227,7 @@
             pltpu.VMEM((nodes, hid), F32),
             pltpu.VMEM((half, hid), BF),
             pltpu.VMEM((nodes, hid), BF),
+            pltpu.VMEM((nodes, hid), BF),
             pltpu.SemaphoreType.DMA((8,)),
         ],
         compiler_params=pltpu.CompilerParams(vmem_limit_bytes=24 * MIB),
@@ -269,25 +271,6 @@
         compiler_params=pltpu.CompilerParams(vmem_limit_bytes=16 * MIB),
         name="sum_pieces",
     )(in_vmem(pieces))
-
-
-def hidden_body(pre_ref, after_ref, hidden_ref):
-    pre = pre_ref[...]
-    hidden_ref[...] = jnp.where(pre > 0, pre, jnp.exp(jnp.minimum(pre, 0.0)) - 1.0).astype(BF)
-
-
-def hidden_of(pre, after):
-    nodes, hid = pre.shape
-    rows = nodes // 8
-    return pl.pallas_call(
-        hidden_body,
-        out_shape=jax.ShapeDtypeStruct((nodes, hid), BF),
-        grid=(8,),
-        in_specs=[pl.BlockSpec((rows, hid), lambda i: (i, 0)), pl.BlockSpec(memory_space=pl.ANY)],
-        out_specs=pl.BlockSpec((rows, hid), lambda i: (i, 0)),
-        compiler_params=pltpu.CompilerParams(vmem_limit_bytes=56 * MIB),
-        name="hidden",
-    )(pre, after)
 
 
 def shift(value, axis, k):
@@ -311,7 +294,7 @@
     shape = (32, nrb // 32, width, side)
     comb_self, pre = dense_self(own_self.reshape(shape), weight, proj_bias[None])
     core = lax.axis_index("core").astype(jnp.int32).reshape(1)
-    pre, comb_agg, grad, send = dense_rest(
+    hidden, comb_agg, grad, send = dense_rest(
         core, own_agg.reshape(shape), comb_self, pre, weight, cotangent[0]
     )
     other = lax.ppermute(send, "core", [(0, 1), (1, 0)])
@@ -319,7 +302,6 @@
     pair = (keep + other.astype(F32)).astype(BF)
     pieces = lax.all_to_all(pair, ("x", "y"), 0, 0, tiled=True)
     mine = sum_pieces(pieces)
-    hidden = hidden_of(pre, mine)
     n1, n2, n3 = (shift(mine, "grp", -k).astype(F32) for k in (1, 2, 3))
     odd = lax.axis_index("grp") % 2 == 1
     total = (mine.astype(F32) + jnp.where(odd, n3, n1)) + (n2 + jnp.where(odd, n1, n3))

time: 114 us -> 111 us (0.974)
  Pallas kernels: 42.8 us -> 36.7 us
  waiting for transfers between devices: 23.9 us -> 28.4 us
    pallas_call x2 -> x1, Pallas kernels: 13.1 us -> 7.07 us  [dense_rest(): pl.pallas_call(dense_rest_body, out_shape=(pltpu.HBM((nodes, hid), BF), p...]
    ppermute x3, waiting for transfers between devices: 0.01 us -> 4.52 us  [shift(): return lax.ppermute(value, axis, [(i, (i + k) % 4) for i in range(4)])]
  transfers between devices with their start and end apart: 6 -> 6, of which waited for: 3 -> 6; matrix products, arithmetic and copies ran while one was open for 0% -> 0% of each run, Pallas kernels for 28% -> 23%
where the time goes in v6:
time: 111 us
  Pallas kernels  36.7 us (33%)
  waiting for transfers between devices  28.4 us (26%)
  blocking collectives  26.1 us (24%)
  starting transfers between devices  17.5 us (16%)
  other arithmetic  1.33 us (1%)
    all_to_all x1, blocking collectives, per_device(): pieces = lax.all_to_all(pair, ('x', 'y'), 0, 0, tiled=True)  26.1 us
    all_to_all x1, waiting for transfers between devices, per_device(): own_agg = lax.all_to_all(agg, FEAT, 0, 0, tiled=True)  17.3 us
    pallas_call x1, Pallas kernels, aggregate_tiles(): pl.pallas_call(functools.partial(aggregate_body, unroll), out_shape=jax.S...  16.7 us
    all_to_all x1, starting transfers between devices, per_device(): own_self = lax.all_to_all(mine, FEAT, 0, 0, tiled=True)  7.41 us
    pallas_call x1, Pallas kernels, dense_rest(): pl.pallas_call(dense_rest_body, out_shape=(pltpu.HBM((nodes, hid), BF), p...  7.07 us
    all_to_all x1, waiting for transfers between devices, per_device(): own_self = lax.all_to_all(mine, FEAT, 0, 0, tiled=True)  6.41 us
    ppermute x3, starting transfers between devices, shift(): return lax.ppermute(value, axis, [(i, (i + k) % 4) for i in range(4)])  5.98 us
    pallas_call x1, Pallas kernels, dense_self(): pl.pallas_call(dense_self_body, out_shape=(pltpu.HBM((sources * width, ow...  5.78 us
  transfers between devices with their start and end apart: 6, of which 6 were waited for; matrix products, arithmetic and copies ran while one was open for 0% of the time, Pallas kernels for 23%

profile of v6, /device:TPU:0, one launch (start us, length us, event | category | flops | bytes accessed | tf_op | source)
XLA Modules:
  0.0 110.7 jit_solution(9414014707385725992)
XLA Ops:
  0.6 3.7 %gather_self.1 = bf16[256,24,128]{2,1,0:T(8,128)(2,1)} custom-call(s32[1,256]{1,0:T(1,128)} %blocks_ref.1, bf16[768,24,128]{2,1,0:T(8,128)(2,1)} %bitcast.10), custom_call_target="tpu_custom_call" | custom-call | tf_op jit(solution)/shard_map/gather_self/pallas_call | solution.py:36
  4.3 7.4 %all-to-all-start.1 = ((bf16[256,24,128]{2,1,0:T(8,128)(2,1)}), bf16[256,24,128]{2,1,0:T(8,128)(2,1)S(1)}, u32[]{:S(2)}, u32[]{:S(2)}) async-start(bf16[256,24,128]{2,1,0:T(8,128)(2,1)} %gather_self.1), calls=%async_computation.1 | async-start | bytes 3145728 | tf_op jit(solution)/shard_map/all_to_all | solution.py:291
  11.8 16.7 %aggregate_tiles.1 = bf16[256,24,128]{2,1,0:T(8,128)(2,1)} custom-call(s32[1,384]{1,0:T(1,128)} %rows_ref.1, s32[1,384]{1,0:T(1,128)} %cols_ref.1, bf16[768,24,128]{2,1,0:T(8,128)(2,1)} %bitcast.11, bf16[384,128,128]{2,1,0:T(8,128)(2,1)} %bitcast.12), custom_call_target="tpu_custom_call" | custom-call | flops 301989888 | bytes 18874368 | tf_op jit(solution)/shard_map/aggregate_tiles/pallas_call | solution.py:90
  28.5 6.4 %all-to-all-done.1 = bf16[256,24,128]{2,1,0:T(8,128)(2,1)S(1)} async-done(((bf16[256,24,128]{2,1,0:T(8,128)(2,1)}), bf16[256,24,128]{2,1,0:T(8,128)(2,1)S(1)}, u32[]{:S(2)}, u32[]{:S(2)}) %all-to-all-start.1) | async-done | bytes 1572896 | tf_op jit(solution)/shard_map/all_to_all | solution.py:291
  34.9 4.0 %all-to-all-start = ((bf16[256,24,128]{2,1,0:T(8,128)(2,1)}), bf16[256,24,128]{2,1,0:T(8,128)(2,1)S(1)}, u32[]{:S(2)}, u32[]{:S(2)}) async-start(bf16[256,24,128]{2,1,0:T(8,128)(2,1)} %aggregate_tiles.1), calls=%async_computation | async-start | bytes 3145728 | tf_op jit(solution)/shard_map/all_to_all | solution.py:293
  38.9 5.8 %dense_self.1 = (bf16[768,1024]{1,0:T(8,128)(2,1)}, f32[1024,1024]{1,0:T(8,128)}) custom-call(bf16[32,8,24,128]{3,2,1,0:T(8,128)(2,1)S(1)} %bitcast.9, bf16[1536,1024]{1,0:T(8,128)(2,1)} %weight_hbm.1, f32[1,1024]{1,0:T(1,128)} %bitcast.14), custom_call_target="tpu_custom_call" | custom-call | tf_op jit(solution)/shard_map/dense_self/pallas_call | solution.py:139
  44.7 17.3 %all-to-all-done = bf16[256,24,128]{2,1,0:T(8,128)(2,1)S(1)} async-done(((bf16[256,24,128]{2,1,0:T(8,128)(2,1)}), bf16[256,24,128]{2,1,0:T(8,128)(2,1)S(1)}, u32[]{:S(2)}, u32[]{:S(2)}) %all-to-all-start) | async-done | bytes 1572896 | tf_op jit(solution)/shard_map/all_to_all | solution.py:293
  62.0 7.1 %dense_rest.1 = (bf16[1024,1024]{1,0:T(8,128)(2,1)}, bf16[768,1024]{1,0:T(8,128)(2,1)S(1)}, bf16[1024,1024]{1,0:T(8,128)(2,1)S(1)}, bf16[16,48,1024]{2,1,0:T(8,128)(2,1)S(1)}) custom-call(s32[1]{0:T(128)} %bitcast.core_ref, bf16[32,8,24,128]{3,2,1,0:T(8,128)(2,1)S(1)} %bitcast.8, bf16[768,1024]{1,0:T(8,128)(2,1)} %get-tuple-element.12.comb_self_hbm, ...), custom_call_target="tpu_custom_call" | custom-call | tf_op jit(solution)/shard_map/dense_rest/pallas_call | solution.py:214
  69.1 0.1 collective-permute-start
  69.2 3.2 %dense_keep.1 = f32[16,48,1024]{2,1,0:T(8,128)S(1)} custom-call(s32[1]{0:T(128)} %bitcast.core_ref, bf16[768,1024]{1,0:T(8,128)(2,1)} %get-tuple-element.12.comb_self_hbm, bf16[768,1024]{1,0:T(8,128)(2,1)S(1)} %get-tuple-element.15.comb_ref, bf16[1024,1024]{1,0:T(8,128)(2,1)S(1)} %get-tuple-element.16.grad_ref), custom_call_target="tpu_custom_call" | custom-call | tf_op jit(solution)/shard_map/dense_keep/pallas_call | solution.py:249
  72.4 0.2 collective-permute-done
  72.6 0.6 add_convert_fusion
  73.1 26.1 %all_to_all.15.pieces_ref = bf16[16,48,1024]{2,1,0:T(8,128)(2,1)S(1)} all-to-all(bf16[16,48,1024]{2,1,0:T(8,128)(2,1)S(1)} %add_convert_fusion), channel_id=1, replica_groups=mesh['grp'=4,'x'=4,'y'=4,'core'=2] {'x','y'}, dimensions={0} | all-to-all | bytes 3145728 | tf_op jit(solution)/shard_map/all_to_all | solution.py:303
  99.3 0.2 sum_pieces.1
  99.5 4.0 %collective-permute-start.3 = (bf16[48,1024]{1,0:T(8,128)(2,1)S(1)}, bf16[48,1024]{1,0:T(8,128)(2,1)S(1)}, u32[]{:S(2)}, u32[]{:S(2)}) collective-permute-start(bf16[48,1024]{1,0:T(8,128)(2,1)S(1)} %sum_pieces.1), channel_id=1, source_target_pairs={{0,64},{32,96},{64,0},{96,32},{1,65},{33,97},{65,1},{97,33},{2,66}... | collective-permute-start | bytes 294920 | tf_op jit(solution)/shard_map/ppermute | solution.py:277
  103.4 0.7 collective-permute-start.2
  104.1 1.3 %collective-permute-start.1 = (bf16[48,1024]{1,0:T(8,128)(2,1)S(1)}, bf16[48,1024]{1,0:T(8,128)(2,1)S(1)}, u32[]{:S(2)}, u32[]{:S(2)}) collective-permute-start(bf16[48,1024]{1,0:T(8,128)(2,1)S(1)} %sum_pieces.1), channel_id=1, source_target_pairs={{0,32},{32,64},{64,96},{96,0},{1,33},{33,65},{65,97},{97,1},{2,34}... | collective-permute-start | bytes 294920 | tf_op jit(solution)/shard_map/ppermute | solution.py:277
  105.5 1.4 %collective-permute-done.3 = bf16[48,1024]{1,0:T(8,128)(2,1)S(1)} collective-permute-done((bf16[48,1024]{1,0:T(8,128)(2,1)S(1)}, bf16[48,1024]{1,0:T(8,128)(2,1)S(1)}, u32[]{:S(2)}, u32[]{:S(2)}) %collective-permute-start.3) | collective-permute-done | bytes 98336 | tf_op jit(solution)/shard_map/ppermute | solution.py:277
  106.9 1.2 %collective-permute-done.2 = bf16[48,1024]{1,0:T(8,128)(2,1)S(1)} collective-permute-done((bf16[48,1024]{1,0:T(8,128)(2,1)S(1)}, bf16[48,1024]{1,0:T(8,128)(2,1)S(1)}, u32[]{:S(2)}, u32[]{:S(2)}) %collective-permute-start.2) | collective-permute-done | bytes 98336 | tf_op jit(solution)/shard_map/ppermute | solution.py:277
  108.1 1.9 %collective-permute-done.1 = bf16[48,1024]{1,0:T(8,128)(2,1)S(1)} collective-permute-done((bf16[48,1024]{1,0:T(8,128)(2,1)S(1)}, bf16[48,1024]{1,0:T(8,128)(2,1)S(1)}, u32[]{:S(2)}, u32[]{:S(2)}) %collective-permute-start.1) | collective-permute-done | bytes 98336 | tf_op jit(solution)/shard_map/ppermute | solution.py:277
  110.0 0.7 fusion.1
Async XLA Ops:
  4.3 30.5 %all-to-all-start.1 = ((bf16[256,24,128]{2,1,0:T(8,128)(2,1)}), bf16[256,24,128]{2,1,0:T(8,128)(2,1)S(1)}, u32[]{:S(2)}, u32[]{:S(2)}) async-start(bf16[256,24,128]{2,1,0:T(8,128)(2,1)} %gather_self.1), calls=%async_computation.1 | async-start | bytes 3145728 | tf_op jit(solution)/shard_map/all_to_all | solution.py:291
  34.9 27.1 %all-to-all-start = ((bf16[256,24,128]{2,1,0:T(8,128)(2,1)}), bf16[256,24,128]{2,1,0:T(8,128)(2,1)S(1)}, u32[]{:S(2)}, u32[]{:S(2)}) async-start(bf16[256,24,128]{2,1,0:T(8,128)(2,1)} %aggregate_tiles.1), calls=%async_computation | async-start | bytes 3145728 | tf_op jit(solution)/shard_map/all_to_all | solution.py:293
  69.1 3.5 %collective-permute-start = (bf16[16,48,1024]{2,1,0:T(8,128)(2,1)S(1)}, bf16[16,48,1024]{2,1,0:T(8,128)(2,1)S(1)}, u32[]{:S(2)}, u32[]{:S(2)}) collective-permute-start(bf16[16,48,1024]{2,1,0:T(8,128)(2,1)S(1)} %get-tuple-element.17), channel_id=1, source_target_pairs={{0,1},{1,0},{2,3},{3,2},{4,5},{5,4},{6,7},{7,6},{8,9},{9,8},{10,11... | collective-permute-start | bytes 4718600 | tf_op jit(solution)/shard_map/ppermute | solution.py:300
  99.5 7.4 %collective-permute-start.3 = (bf16[48,1024]{1,0:T(8,128)(2,1)S(1)}, bf16[48,1024]{1,0:T(8,128)(2,1)S(1)}, u32[]{:S(2)}, u32[]{:S(2)}) collective-permute-start(bf16[48,1024]{1,0:T(8,128)(2,1)S(1)} %sum_pieces.1), channel_id=1, source_target_pairs={{0,64},{32,96},{64,0},{96,32},{1,65},{33,97},{65,1},{97,33},{2,66}... | collective-permute-start | bytes 294920 | tf_op jit(solution)/shard_map/ppermute | solution.py:277
  103.4 4.7 %collective-permute-start.2 = (bf16[48,1024]{1,0:T(8,128)(2,1)S(1)}, bf16[48,1024]{1,0:T(8,128)(2,1)S(1)}, u32[]{:S(2)}, u32[]{:S(2)}) collective-permute-start(bf16[48,1024]{1,0:T(8,128)(2,1)S(1)} %sum_pieces.1), channel_id=1, source_target_pairs={{0,96},{32,0},{64,32},{96,64},{1,97},{33,1},{65,33},{97,65},{2,98}... | collective-permute-start | bytes 294920 | tf_op jit(solution)/shard_map/ppermute | solution.py:277
  104.1 5.8 %collective-permute-start.1 = (bf16[48,1024]{1,0:T(8,128)(2,1)S(1)}, bf16[48,1024]{1,0:T(8,128)(2,1)S(1)}, u32[]{:S(2)}, u32[]{:S(2)}) collective-permute-start(bf16[48,1024]{1,0:T(8,128)(2,1)S(1)} %sum_pieces.1), channel_id=1, source_target_pairs={{0,32},{32,64},{64,96},{96,0},{1,33},{33,65},{65,97},{97,1},{2,34}... | collective-permute-start | bytes 294920 | tf_op jit(solution)/shard_map/ppermute | solution.py:277

commit v7 on v6

--- a/solution.py
+++ b/solution.py
@@ -150,27 +150,28 @@
 
 
 def dense_rest_body(
-    core_ref, agg_ref, comb_self_hbm, pre_hbm, weight_hbm, cot_hbm,
+    place_ref, agg_ref, comb_self_hbm, pre_hbm, weight_hbm, cot_hbm,
     hidden_hbm, comb_ref, grad_ref, send_ref,
-    comb_self_ref, pre_ref, weight_ref, cot_ref, hidden_ref, sem,
+    pre_ref, weight_ref, cot_ref, hidden_ref, sem,
 ):
-    half, nodes = comb_ref.shape
+    half, nodes = comb_self_hbm.shape
+    agg_rows = pl.ds(half, half)
     chunk = nodes // 2
     chunks = [pl.ds(m * chunk, chunk) for m in range(2)]
-    sources = [(weight_hbm.at[pl.ds(half, half)], weight_ref)]
+    sources = [(weight_hbm.at[agg_rows], weight_ref)]
     for rows in chunks:
         sources.append((pre_hbm.at[rows], pre_ref.at[rows]))
         sources.append((cot_hbm.at[rows], cot_ref.at[rows]))
-    sources.append((comb_self_hbm, comb_self_ref))
+    sources.append((comb_self_hbm, comb_ref.at[pl.ds(0, half)]))
     loads = [pltpu.make_async_copy(a, b, sem.at[i]) for i, (a, b) in enumerate(sources)]
     for load in loads:
         load.start()
-    stack_channels(agg_ref, comb_ref)
+    stack_channels(agg_ref, comb_ref.at[agg_rows])
     loads[0].wait()
     stores = []
     for m, rows in enumerate(chunks):
         part = lax.dot_general(
-            comb_ref[:, rows], weight_ref[...], (((0,), (0,)), ((), ())), preferred_element_type=F32
+            comb_ref[agg_rows, rows], weight_ref[...], (((0,), (0,)), ((), ())), preferred_element_type=F32
         )
         loads[1 + 2 * m].wait()
         loads[2 + 2 * m].wait()
@@ -181,33 +182,32 @@
         stores.append(pltpu.make_async_copy(hidden_ref.at[rows], hidden_hbm.at[rows], sem.at[6 + m]))
         stores[m].start()
     loads[5].wait()
-    weight_terms(1 - core_ref[0], comb_self_ref, comb_ref, grad_ref, send_ref)
+    weight_terms(place_ref, 1 - place_ref[2], comb_ref, grad_ref, send_ref)
     for store in stores:
         store.wait()
 
 
-def weight_terms(dest, comb_self_ref, comb_ref, grad_ref, out_ref):
-    blocks, share, hid = out_ref.shape
-    lhs = jnp.concatenate(
-        [
-            source[pl.ds(pl.multiple_of((2 * b + dest) * share, share), share), :]
-            for source in (comb_self_ref, comb_ref)
-            for b in range(blocks // 2)
-        ],
-        axis=0,
-    )
-    width = hid // 4
-    for n in range(4):
-        cols = pl.ds(n * width, width)
-        total = jnp.dot(lhs, grad_ref[:, cols], preferred_element_type=F32)
-        out_ref[:, :, cols] = total.reshape(blocks, share, width).astype(out_ref.dtype)
+def weight_terms(place_ref, dest, comb_ref, grad_ref, out_ref):
+    x, y = place_ref[0], place_ref[1]
+    _, rows, width = out_ref.shape
+    share = rows // 4
+
+    def block(dx, dy):
+        first = (8 * ((x + dx) % 4) + 2 * ((y + dy) % 4) + dest) * share
+        return comb_ref[pl.ds(pl.multiple_of(first, share), share), :]
+
+    for part in range(2):
+        ahead = [(k + j, j) if part == 0 else (j, k + j) for k in range(4) for j in range(4)]
+        lhs = jnp.concatenate([block(dx, dy) for dx, dy in ahead], axis=0)
+        total = jnp.dot(lhs, grad_ref[:, pl.ds(part * width, width)], preferred_element_type=F32)
+        out_ref[pl.ds(4 * part, 4)] = total.reshape(4, rows, width).astype(out_ref.dtype)
 
 
 def pieces_of(half, hid):
-    return (16, half // 16, hid)
-
-
-def dense_rest(core, own_agg, comb_self, pre, weight, cot):
+    return (8, half // 4, hid // 2)
+
+
+def dense_rest(place, own_agg, comb_self, pre, weight, cot):
     nodes, hid = cot.shape
     half = comb_self.shape[0]
     vmem = pl.BlockSpec(memory_space=pltpu.VMEM)
@@ -215,7 +215,7 @@
         dense_rest_body,
         out_shape=(
             pltpu.HBM((nodes, hid), BF),
-            pltpu.VMEM((half, nodes), BF),
+            pltpu.VMEM((2 * half, nodes), BF),
             pltpu.VMEM((nodes, hid), BF),
             pltpu.VMEM(pieces_of(half, hid), BF),
         ),
@@ -223,7 +223,6 @@
         + [pl.BlockSpec(memory_space=pl.ANY)] * 4,
         out_specs=(pl.BlockSpec(memory_space=pl.ANY),) + (vmem,) * 3,
         scratch_shapes=[
-            pltpu.VMEM((half, nodes), BF),
             pltpu.VMEM((nodes, hid), F32),
             pltpu.VMEM((half, hid), BF),
             pltpu.VMEM((nodes, hid), BF),
@@ -232,49 +231,33 @@
         ],
         compiler_params=pltpu.CompilerParams(vmem_limit_bytes=24 * MIB),
         name="dense_rest",
-    )(core, in_vmem(own_agg), *map(in_hbm, (comb_self, pre, weight, cot)))
-
-
-def dense_keep_body(core_ref, comb_self_hbm, comb_ref, grad_ref, keep_ref, comb_self_ref, sem):
-    load = pltpu.make_async_copy(comb_self_hbm, comb_self_ref, sem)
-    load.start()
-    load.wait()
-    weight_terms(core_ref[0], comb_self_ref, comb_ref, grad_ref, keep_ref)
-
-
-def dense_keep(core, comb_self, comb_agg, grad):
-    half, nodes = comb_self.shape
-    hid = grad.shape[1]
+    )(place, in_vmem(own_agg), *map(in_hbm, (comb_self, pre, weight, cot)))
+
+
+def dense_keep_body(place_ref, comb_ref, grad_ref, keep_ref):
+    weight_terms(place_ref, place_ref[2], comb_ref, grad_ref, keep_ref)
+
+
+def dense_keep(place, comb, grad):
+    channels = comb.shape[0]
     vmem = pl.BlockSpec(memory_space=pltpu.VMEM)
     return pl.pallas_call(
         dense_keep_body,
-        out_shape=pltpu.VMEM(pieces_of(half, hid), F32),
-        in_specs=[pl.BlockSpec(memory_space=pltpu.SMEM), pl.BlockSpec(memory_space=pl.ANY), vmem, vmem],
+        out_shape=pltpu.VMEM(pieces_of(channels // 2, grad.shape[1]), F32),
+        in_specs=[pl.BlockSpec(memory_space=pltpu.SMEM), vmem, vmem],
         out_specs=vmem,
-        scratch_shapes=[pltpu.VMEM((half, nodes), BF), pltpu.SemaphoreType.DMA(())],
         compiler_params=pltpu.CompilerParams(vmem_limit_bytes=16 * MIB),
         name="dense_keep",
-    )(core, in_hbm(comb_self), in_vmem(comb_agg), in_vmem(grad))
-
-
-def sum_pieces_body(pieces_ref, sum_ref):
-    sum_ref[...] = jnp.sum(pieces_ref[...].astype(F32), axis=0).astype(BF)
-
-
-def sum_pieces(pieces):
-    vmem = pl.BlockSpec(memory_space=pltpu.VMEM)
-    return pl.pallas_call(
-        sum_pieces_body,
-        out_shape=pltpu.VMEM(pieces.shape[1:], BF),
-        in_specs=[vmem],
-        out_specs=vmem,
-        compiler_params=pltpu.CompilerParams(vmem_limit_bytes=16 * MIB),
-        name="sum_pieces",
-    )(in_vmem(pieces))
+    )(place, in_vmem(comb), in_vmem(grad))
 
 
 def shift(value, axis, k):
     return lax.ppermute(value, axis, [(i, (i + k) % 4) for i in range(4)])
+
+
+def shift_diagonal(value, k):
+    pairs = [(4 * x + y, 4 * ((x + k) % 4) + (y + k) % 4) for x in range(4) for y in range(4)]
+    return lax.ppermute(value, ("x", "y"), pairs)
 
 
 FEAT = ("x", "y", "core")
@@ -293,15 +276,21 @@
     own_agg = lax.all_to_all(agg, FEAT, 0, 0, tiled=True)
     shape = (32, nrb // 32, width, side)
     comb_self, pre = dense_self(own_self.reshape(shape), weight, proj_bias[None])
-    core = lax.axis_index("core").astype(jnp.int32).reshape(1)
-    hidden, comb_agg, grad, send = dense_rest(
-        core, own_agg.reshape(shape), comb_self, pre, weight, cotangent[0]
+    place = jnp.stack([lax.axis_index(a) for a in FEAT]).astype(jnp.int32)
+    hidden, comb, grad, send = dense_rest(
+        place, own_agg.reshape(shape), comb_self, pre, weight, cotangent[0]
     )
     other = lax.ppermute(send, "core", [(0, 1), (1, 0)])
-    keep = dense_keep(core, comb_self, comb_agg, grad)
-    pair = (keep + other.astype(F32)).astype(BF)
-    pieces = lax.all_to_all(pair, ("x", "y"), 0, 0, tiled=True)
-    mine = sum_pieces(pieces)
+    pair = dense_keep(place, comb, grad) + other.astype(F32)
+    share, width = weight.shape[0] // 32, weight.shape[1] // 2
+    moved = [
+        [shift(pair[4 * part + k].astype(BF), axis, k).astype(F32) for k in (1, 2, 3)]
+        for part, axis in enumerate(("x", "y"))
+    ]
+    once = [(pair[4 * part] + sum(moved[part])).reshape(4, share, width) for part in range(2)]
+    once = jnp.concatenate(once, axis=2)
+    mine = once[0] + sum(shift_diagonal(once[j].astype(BF), j).astype(F32) for j in (1, 2, 3))
+    mine = mine.astype(BF)
     n1, n2, n3 = (shift(mine, "grp", -k).astype(F32) for k in (1, 2, 3))
     odd = lax.axis_index("grp") % 2 == 1
     total = (mine.astype(F32) + jnp.where(odd, n3, n1)) + (n2 + jnp.where(odd, n1, n3))

time: 111 us -> 119 us (1.072)
  blocking collectives: 26.1 us -> 0 us
  waiting for transfers between devices: 28.4 us -> 51.1 us
  starting transfers between devices: 17.5 us -> 28.8 us
    all_to_all x1 -> x0, blocking collectives: 26.1 us -> none  [per_device(): pieces = lax.all_to_all(pair, ('x', 'y'), 0, 0, tiled=True)]
    ppermute x3 -> x9, waiting for transfers between devices: 4.52 us -> 17.9 us  [shift(): return lax.ppermute(value, axis, [(i, (i + k) % 4) for i in range(4)])]
    ppermute x0 -> x3, waiting for transfers between devices: none -> 8.52 us  [shift_diagonal(): return lax.ppermute(value, ('x', 'y'), pairs)]
    ppermute x3 -> x9, starting transfers between devices: 5.98 us -> 11.9 us  [shift(): return lax.ppermute(value, axis, [(i, (i + k) % 4) for i in range(4)])]
    ppermute x0 -> x3, starting transfers between devices: none -> 5.41 us  [shift_diagonal(): return lax.ppermute(value, ('x', 'y'), pairs)]
    pallas_call x2 -> x1, Pallas kernels: 3.42 us -> 2.34 us  [dense_keep(): pl.pallas_call(dense_keep_body, out_shape=pltpu.VMEM(pieces_of(channels /...]
  transfers between devices with their start and end apart: 6 -> 15, of which waited for: 6 -> 11; matrix products, arithmetic and copies ran while one was open for 0% -> 0% of each run, Pallas kernels for 23% -> 21%
where the time goes in v7:
time: 119 us
  waiting for transfers between devices  51.1 us (43%)
  Pallas kernels  36.2 us (30%)
  starting transfers between devices  28.8 us (24%)
  other arithmetic  1.76 us (1%)
    ppermute x9, waiting for transfers between devices, shift(): return lax.ppermute(value, axis, [(i, (i + k) % 4) for i in range(4)])  17.9 us
    all_to_all x1, waiting for transfers between devices, per_device(): own_agg = lax.all_to_all(agg, FEAT, 0, 0, tiled=True)  17.3 us
    pallas_call x1, Pallas kernels, aggregate_tiles(): pl.pallas_call(functools.partial(aggregate_body, unroll), out_shape=jax.S...  16.7 us
    ppermute x9, starting transfers between devices, shift(): return lax.ppermute(value, axis, [(i, (i + k) % 4) for i in range(4)])  11.9 us
    ppermute x3, waiting for transfers between devices, shift_diagonal(): return lax.ppermute(value, ('x', 'y'), pairs)  8.52 us
    pallas_call x1, Pallas kernels, dense_rest(): pl.pallas_call(dense_rest_body, out_shape=(pltpu.HBM((nodes, hid), BF), p...  7.63 us
    all_to_all x1, starting transfers between devices, per_device(): own_self = lax.all_to_all(mine, FEAT, 0, 0, tiled=True)  7.41 us
    all_to_all x1, waiting for transfers between devices, per_device(): own_self = lax.all_to_all(mine, FEAT, 0, 0, tiled=True)  6.41 us
  transfers between devices with their start and end apart: 15, of which 11 were waited for; matrix products, arithmetic and copies ran while one was open for 0% of the time, Pallas kernels for 21%

profile of v7, /device:TPU:0, one launch (start us, length us, event | category | flops | bytes accessed | tf_op | source)
XLA Modules:
  0.0 118.8 jit_solution(805928326241469439)
XLA Ops:
  0.6 3.7 %gather_self.1 = bf16[256,24,128]{2,1,0:T(8,128)(2,1)} custom-call(s32[1,256]{1,0:T(1,128)} %blocks_ref.1, bf16[768,24,128]{2,1,0:T(8,128)(2,1)} %bitcast.46), custom_call_target="tpu_custom_call" | custom-call | tf_op jit(solution)/shard_map/gather_self/pallas_call | solution.py:36
  4.4 7.4 %all-to-all-start.1 = ((bf16[256,24,128]{2,1,0:T(8,128)(2,1)}), bf16[256,24,128]{2,1,0:T(8,128)(2,1)S(1)}, u32[]{:S(2)}, u32[]{:S(2)}) async-start(bf16[256,24,128]{2,1,0:T(8,128)(2,1)} %gather_self.1), calls=%async_computation.1 | async-start | bytes 3145728 | tf_op jit(solution)/shard_map/all_to_all | solution.py:274
  11.8 16.7 %aggregate_tiles.1 = bf16[256,24,128]{2,1,0:T(8,128)(2,1)} custom-call(s32[1,384]{1,0:T(1,128)} %rows_ref.1, s32[1,384]{1,0:T(1,128)} %cols_ref.1, bf16[768,24,128]{2,1,0:T(8,128)(2,1)} %bitcast.47, bf16[384,128,128]{2,1,0:T(8,128)(2,1)} %bitcast.48), custom_call_target="tpu_custom_call" | custom-call | flops 301989888 | bytes 18874368 | tf_op jit(solution)/shard_map/aggregate_tiles/pallas_call | solution.py:90
  28.5 6.4 %all-to-all-done.1 = bf16[256,24,128]{2,1,0:T(8,128)(2,1)S(1)} async-done(((bf16[256,24,128]{2,1,0:T(8,128)(2,1)}), bf16[256,24,128]{2,1,0:T(8,128)(2,1)S(1)}, u32[]{:S(2)}, u32[]{:S(2)}) %all-to-all-start.1) | async-done | bytes 1572896 | tf_op jit(solution)/shard_map/all_to_all | solution.py:274
  34.9 4.0 %all-to-all-start = ((bf16[256,24,128]{2,1,0:T(8,128)(2,1)}), bf16[256,24,128]{2,1,0:T(8,128)(2,1)S(1)}, u32[]{:S(2)}, u32[]{:S(2)}) async-start(bf16[256,24,128]{2,1,0:T(8,128)(2,1)} %aggregate_tiles.1), calls=%async_computation | async-start | bytes 3145728 | tf_op jit(solution)/shard_map/all_to_all | solution.py:276
  38.9 0.1 pad_add_fusion.place_ref
  39.0 5.8 %dense_self.1 = (bf16[768,1024]{1,0:T(8,128)(2,1)}, f32[1024,1024]{1,0:T(8,128)}) custom-call(bf16[32,8,24,128]{3,2,1,0:T(8,128)(2,1)S(1)} %bitcast.45, bf16[1536,1024]{1,0:T(8,128)(2,1)} %weight_hbm.1, f32[1,1024]{1,0:T(1,128)} %bitcast.54), custom_call_target="tpu_custom_call" | custom-call | tf_op jit(solution)/shard_map/dense_self/pallas_call | solution.py:139
  44.8 17.3 %all-to-all-done = bf16[256,24,128]{2,1,0:T(8,128)(2,1)S(1)} async-done(((bf16[256,24,128]{2,1,0:T(8,128)(2,1)}), bf16[256,24,128]{2,1,0:T(8,128)(2,1)S(1)}, u32[]{:S(2)}, u32[]{:S(2)}) %all-to-all-start) | async-done | bytes 1572896 | tf_op jit(solution)/shard_map/all_to_all | solution.py:276
  62.0 7.6 %dense_rest.1 = (bf16[1024,1024]{1,0:T(8,128)(2,1)}, bf16[1536,1024]{1,0:T(8,128)(2,1)S(1)}, bf16[1024,1024]{1,0:T(8,128)(2,1)S(1)}, bf16[8,192,512]{2,1,0:T(8,128)(2,1)S(1)}) custom-call(s32[3]{0:T(128)S(1)} %pad_add_fusion.place_ref, bf16[32,8,24,128]{3,2,1,0:T(8,128)(2,1)S(1)} %bitcast.44, bf16[768,1024]{1,0:T(8,128)(2,1)} %get-tuple-element.12.comb_self_hbm, ...), custom_call_target="tpu_custom_call" | custom-call | tf_op jit(solution)/shard_map/dense_rest/pallas_call | solution.py:214
  69.6 0.1 collective-permute-start
  69.7 2.3 %dense_keep.1 = f32[8,192,512]{2,1,0:T(8,128)S(1)} custom-call(s32[3]{0:T(128)S(1)} %pad_add_fusion.place_ref, bf16[1536,1024]{1,0:T(8,128)(2,1)S(1)} %get-tuple-element.15.comb_ref, bf16[1024,1024]{1,0:T(8,128)(2,1)S(1)} %get-tuple-element.16.grad_ref), custom_call_target="tpu_custom_call" | custom-call | tf_op jit(solution)/shard_map/dense_keep/pallas_call | solution.py:244
  72.1 1.1 collective-permute-done
  73.1 0.7 fusion.10
  73.8 0.1 slice_bitcast_fusion.4
  73.9 0.1 collective-permute-start.4
  74.0 3.2 %collective-permute-start.6 = (bf16[192,512]{1,0:T(8,128)(2,1)S(1)}, bf16[192,512]{1,0:T(8,128)(2,1)S(1)}, u32[]{:S(2)}, u32[]{:S(2)}) collective-permute-start(bf16[192,512]{1,0:T(8,128)(2,1)S(1)} %get-tuple-element.23), channel_id=1, source_target_pairs={{0,6},{2,0},{4,2},{6,4},{1,7},{3,1},{5,3},{7,5},{8,14},{10,8},{12,... | collective-permute-start | bytes 589832 | tf_op jit(solution)/shard_map/ppermute | solution.py:255
  77.2 0.0 collective-permute-start.5
  77.2 1.1 collective-permute-start.3
  78.3 1.6 %collective-permute-start.2 = (bf16[192,512]{1,0:T(8,128)(2,1)S(1)}, bf16[192,512]{1,0:T(8,128)(2,1)S(1)}, u32[]{:S(2)}, u32[]{:S(2)}) collective-permute-start(bf16[192,512]{1,0:T(8,128)(2,1)S(1)} %get-tuple-element.26), channel_id=1, source_target_pairs={{0,16},{8,24},{16,0},{24,8},{1,17},{9,25},{17,1},{25,9},{2,18},{10... | collective-permute-start | bytes 589832 | tf_op jit(solution)/shard_map/ppermute | solution.py:255
  79.9 6.5 %collective-permute-done.4 = bf16[192,512]{1,0:T(8,128)(2,1)S(1)} collective-permute-done((bf16[192,512]{1,0:T(8,128)(2,1)S(1)}, bf16[192,512]{1,0:T(8,128)(2,1)S(1)}, u32[]{:S(2)}, u32[]{:S(2)}) %collective-permute-start.4) | collective-permute-done | bytes 196640 | tf_op jit(solution)/shard_map/ppermute | solution.py:255
  86.4 0.0 collective-permute-start.1
  86.4 0.0 collective-permute-done.6
  86.4 0.0 collective-permute-done.5
  86.4 0.0 collective-permute-done.3
  86.4 0.3 collective-permute-done.2
  86.6 6.6 %collective-permute-done.1 = bf16[192,512]{1,0:T(8,128)(2,1)S(1)} collective-permute-done((bf16[192,512]{1,0:T(8,128)(2,1)S(1)}, bf16[192,512]{1,0:T(8,128)(2,1)S(1)}, u32[]{:S(2)}, u32[]{:S(2)}) %collective-permute-start.1) | collective-permute-done | bytes 196640 | tf_op jit(solution)/shard_map/ppermute | solution.py:255
  93.3 0.2 fusion.1
  93.5 0.1 collective-permute-start.7
  93.6 5.3 %collective-permute-start.9 = (bf16[48,1024]{1,0:T(8,128)(2,1)S(1)}, bf16[48,1024]{1,0:T(8,128)(2,1)S(1)}, u32[]{:S(2)}, u32[]{:S(2)}) collective-permute-start(bf16[48,1024]{1,0:T(8,128)(2,1)S(1)} %get-tuple-element.29), channel_id=1, source_target_pairs={{0,30},{2,24},{4,26},{6,28},{8,6},{10,0},{12,2},{14,4},{16,14},{18... | collective-permute-start | bytes 294920 | tf_op jit(solution)/shard_map/ppermute | solution.py:260
  99.0 0.0 collective-permute-start.8
  99.0 2.8 %collective-permute-done.7 = bf16[48,1024]{1,0:T(8,128)(2,1)S(1)} collective-permute-done((bf16[48,1024]{1,0:T(8,128)(2,1)S(1)}, bf16[48,1024]{1,0:T(8,128)(2,1)S(1)}, u32[]{:S(2)}, u32[]{:S(2)}) %collective-permute-start.7) | collective-permute-done | bytes 98336 | tf_op jit(solution)/shard_map/ppermute | solution.py:260
  101.8 0.0 collective-permute-done.9
  101.8 5.7 %collective-permute-done.8 = bf16[48,1024]{1,0:T(8,128)(2,1)S(1)} collective-permute-done((bf16[48,1024]{1,0:T(8,128)(2,1)S(1)}, bf16[48,1024]{1,0:T(8,128)(2,1)S(1)}, u32[]{:S(2)}, u32[]{:S(2)}) %collective-permute-start.8) | collective-permute-done | bytes 98336 | tf_op jit(solution)/shard_map/ppermute | solution.py:260
  107.5 0.1 fusion.9
  107.5 3.9 %collective-permute-start.12 = (bf16[48,1024]{1,0:T(8,128)(2,1)S(1)}, bf16[48,1024]{1,0:T(8,128)(2,1)S(1)}, u32[]{:S(2)}, u32[]{:S(2)}) collective-permute-start(bf16[48,1024]{1,0:T(8,128)(2,1)S(1)} %fusion.9), channel_id=1, source_target_pairs={{0,64},{32,96},{64,0},{96,32},{1,65},{33,97},{65,1},{97,33},{2,66}... | collective-permute-start | bytes 294920 | tf_op jit(solution)/shard_map/ppermute | solution.py:255
  111.5 0.7 collective-permute-start.11
  112.2 1.3 %collective-permute-start.10 = (bf16[48,1024]{1,0:T(8,128)(2,1)S(1)}, bf16[48,1024]{1,0:T(8,128)(2,1)S(1)}, u32[]{:S(2)}, u32[]{:S(2)}) collective-permute-start(bf16[48,1024]{1,0:T(8,128)(2,1)S(1)} %fusion.9), channel_id=1, source_target_pairs={{0,32},{32,64},{64,96},{96,0},{1,33},{33,65},{65,97},{97,1},{2,34}... | collective-permute-start | bytes 294920 | tf_op jit(solution)/shard_map/ppermute | solution.py:255
  113.5 0.6 collective-permute-done.12
  114.1 2.1 %collective-permute-done.11 = bf16[48,1024]{1,0:T(8,128)(2,1)S(1)} collective-permute-done((bf16[48,1024]{1,0:T(8,128)(2,1)S(1)}, bf16[48,1024]{1,0:T(8,128)(2,1)S(1)}, u32[]{:S(2)}, u32[]{:S(2)}) %collective-permute-start.11) | collective-permute-done | bytes 98336 | tf_op jit(solution)/shard_map/ppermute | solution.py:255
  116.1 1.9 %collective-permute-done.10 = bf16[48,1024]{1,0:T(8,128)(2,1)S(1)} collective-permute-done((bf16[48,1024]{1,0:T(8,128)(2,1)S(1)}, bf16[48,1024]{1,0:T(8,128)(2,1)S(1)}, u32[]{:S(2)}, u32[]{:S(2)}) %collective-permute-start.10) | collective-permute-done | bytes 98336 | tf_op jit(solution)/shard_map/ppermute | solution.py:255
  118.0 0.7 fusion.4
  (2 shorter events, 0.1 us)
Async XLA Ops:
  4.4 30.5 %all-to-all-start.1 = ((bf16[256,24,128]{2,1,0:T(8,128)(2,1)}), bf16[256,24,128]{2,1,0:T(8,128)(2,1)S(1)}, u32[]{:S(2)}, u32[]{:S(2)}) async-start(bf16[256,24,128]{2,1,0:T(8,128)(2,1)} %gather_self.1), calls=%async_computation.1 | async-start | bytes 3145728 | tf_op jit(solution)/shard_map/all_to_all | solution.py:274
  34.9 27.1 %all-to-all-start = ((bf16[256,24,128]{2,1,0:T(8,128)(2,1)}), bf16[256,24,128]{2,1,0:T(8,128)(2,1)S(1)}, u32[]{:S(2)}, u32[]{:S(2)}) async-start(bf16[256,24,128]{2,1,0:T(8,128)(2,1)} %aggregate_tiles.1), calls=%async_computation | async-start | bytes 3145728 | tf_op jit(solution)/shard_map/all_to_all | solution.py:276
  69.6 3.5 %collective-permute-start = (bf16[8,192,512]{2,1,0:T(8,128)(2,1)S(1)}, bf16[8,192,512]{2,1,0:T(8,128)(2,1)S(1)}, u32[]{:S(2)}, u32[]{:S(2)}) collective-permute-start(bf16[8,192,512]{2,1,0:T(8,128)(2,1)S(1)} %get-tuple-element.17), channel_id=1, source_target_pairs={{0,1},{1,0},{2,3},{3,2},{4,5},{5,4},{6,7},{7,6},{8,9},{9,8},{10,11... | collective-permute-start | bytes 4718600 | tf_op jit(solution)/shard_map/ppermute | solution.py:283
  73.9 12.4 %collective-permute-start.4 = (bf16[192,512]{1,0:T(8,128)(2,1)S(1)}, bf16[192,512]{1,0:T(8,128)(2,1)S(1)}, u32[]{:S(2)}, u32[]{:S(2)}) collective-permute-start(bf16[192,512]{1,0:T(8,128)(2,1)S(1)} %get-tuple-element.22), channel_id=1, source_target_pairs={{0,2},{2,4},{4,6},{6,0},{1,3},{3,5},{5,7},{7,1},{8,10},{10,12},{12... | collective-permute-start | bytes 589832 | tf_op jit(solution)/shard_map/ppermute | solution.py:255
  74.0 12.4 %collective-permute-start.6 = (bf16[192,512]{1,0:T(8,128)(2,1)S(1)}, bf16[192,512]{1,0:T(8,128)(2,1)S(1)}, u32[]{:S(2)}, u32[]{:S(2)}) collective-permute-start(bf16[192,512]{1,0:T(8,128)(2,1)S(1)} %get-tuple-element.23), channel_id=1, source_target_pairs={{0,6},{2,0},{4,2},{6,4},{1,7},{3,1},{5,3},{7,5},{8,14},{10,8},{12,... | collective-permute-start | bytes 589832 | tf_op jit(solution)/shard_map/ppermute | solution.py:255
  77.2 9.1 %collective-permute-start.5 = (bf16[192,512]{1,0:T(8,128)(2,1)S(1)}, bf16[192,512]{1,0:T(8,128)(2,1)S(1)}, u32[]{:S(2)}, u32[]{:S(2)}) collective-permute-start(bf16[192,512]{1,0:T(8,128)(2,1)S(1)} %get-tuple-element.24), channel_id=1, source_target_pairs={{0,4},{2,6},{4,0},{6,2},{1,5},{3,7},{5,1},{7,3},{8,12},{10,14},{12... | collective-permute-start | bytes 589832 | tf_op jit(solution)/shard_map/ppermute | solution.py:255
  77.2 9.1 %collective-permute-start.3 = (bf16[192,512]{1,0:T(8,128)(2,1)S(1)}, bf16[192,512]{1,0:T(8,128)(2,1)S(1)}, u32[]{:S(2)}, u32[]{:S(2)}) collective-permute-start(bf16[192,512]{1,0:T(8,128)(2,1)S(1)} %get-tuple-element.25), channel_id=1, source_target_pairs={{0,24},{8,0},{16,8},{24,16},{1,25},{9,1},{17,9},{25,17},{2,26},{10... | collective-permute-start | bytes 589832 | tf_op jit(solution)/shard_map/ppermute | solution.py:255
  78.3 8.3 %collective-permute-start.2 = (bf16[192,512]{1,0:T(8,128)(2,1)S(1)}, bf16[192,512]{1,0:T(8,128)(2,1)S(1)}, u32[]{:S(2)}, u32[]{:S(2)}) collective-permute-start(bf16[192,512]{1,0:T(8,128)(2,1)S(1)} %get-tuple-element.26), channel_id=1, source_target_pairs={{0,16},{8,24},{16,0},{24,8},{1,17},{9,25},{17,1},{25,9},{2,18},{10... | collective-permute-start | bytes 589832 | tf_op jit(solution)/shard_map/ppermute | solution.py:255
  86.4 6.9 %collective-permute-start.1 = (bf16[192,512]{1,0:T(8,128)(2,1)S(1)}, bf16[192,512]{1,0:T(8,128)(2,1)S(1)}, u32[]{:S(2)}, u32[]{:S(2)}) collective-permute-start(bf16[192,512]{1,0:T(8,128)(2,1)S(1)} %get-tuple-element.27), channel_id=1, source_target_pairs={{0,8},{8,16},{16,24},{24,0},{1,9},{9,17},{17,25},{25,1},{2,10},{10... | collective-permute-start | bytes 589832 | tf_op jit(solution)/shard_map/ppermute | solution.py:255
  93.5 8.3 %collective-permute-start.7 = (bf16[48,1024]{1,0:T(8,128)(2,1)S(1)}, bf16[48,1024]{1,0:T(8,128)(2,1)S(1)}, u32[]{:S(2)}, u32[]{:S(2)}) collective-permute-start(bf16[48,1024]{1,0:T(8,128)(2,1)S(1)} %get-tuple-element.28), channel_id=1, source_target_pairs={{0,10},{2,12},{4,14},{6,8},{8,18},{10,20},{12,22},{14,16},{16,26},... | collective-permute-start | bytes 294920 | tf_op jit(solution)/shard_map/ppermute | solution.py:260
  93.6 8.2 %collective-permute-start.9 = (bf16[48,1024]{1,0:T(8,128)(2,1)S(1)}, bf16[48,1024]{1,0:T(8,128)(2,1)S(1)}, u32[]{:S(2)}, u32[]{:S(2)}) collective-permute-start(bf16[48,1024]{1,0:T(8,128)(2,1)S(1)} %get-tuple-element.29), channel_id=1, source_target_pairs={{0,30},{2,24},{4,26},{6,28},{8,6},{10,0},{12,2},{14,4},{16,14},{18... | collective-permute-start | bytes 294920 | tf_op jit(solution)/shard_map/ppermute | solution.py:260
  99.0 8.5 %collective-permute-start.8 = (bf16[48,1024]{1,0:T(8,128)(2,1)S(1)}, bf16[48,1024]{1,0:T(8,128)(2,1)S(1)}, u32[]{:S(2)}, u32[]{:S(2)}) collective-permute-start(bf16[48,1024]{1,0:T(8,128)(2,1)S(1)} %get-tuple-element.30), channel_id=1, source_target_pairs={{0,20},{2,22},{4,16},{6,18},{8,28},{10,30},{12,24},{14,26},{16,4},... | collective-permute-start | bytes 294920 | tf_op jit(solution)/shard_map/ppermute | solution.py:260
  107.5 6.5 %collective-permute-start.12 = (bf16[48,1024]{1,0:T(8,128)(2,1)S(1)}, bf16[48,1024]{1,0:T(8,128)(2,1)S(1)}, u32[]{:S(2)}, u32[]{:S(2)}) collective-permute-start(bf16[48,1024]{1,0:T(8,128)(2,1)S(1)} %fusion.9), channel_id=1, source_target_pairs={{0,64},{32,96},{64,0},{96,32},{1,65},{33,97},{65,1},{97,33},{2,66}... | collective-permute-start | bytes 294920 | tf_op jit(solution)/shard_map/ppermute | solution.py:255
  111.5 4.7 %collective-permute-start.11 = (bf16[48,1024]{1,0:T(8,128)(2,1)S(1)}, bf16[48,1024]{1,0:T(8,128)(2,1)S(1)}, u32[]{:S(2)}, u32[]{:S(2)}) collective-permute-start(bf16[48,1024]{1,0:T(8,128)(2,1)S(1)} %fusion.9), channel_id=1, source_target_pairs={{0,96},{32,0},{64,32},{96,64},{1,97},{33,1},{65,33},{97,65},{2,98}... | collective-permute-start | bytes 294920 | tf_op jit(solution)/shard_map/ppermute | solution.py:255
  112.2 5.8 %collective-permute-start.10 = (bf16[48,1024]{1,0:T(8,128)(2,1)S(1)}, bf16[48,1024]{1,0:T(8,128)(2,1)S(1)}, u32[]{:S(2)}, u32[]{:S(2)}) collective-permute-start(bf16[48,1024]{1,0:T(8,128)(2,1)S(1)} %fusion.9), channel_id=1, source_target_pairs={{0,32},{32,64},{64,96},{96,0},{1,33},{33,65},{65,97},{97,1},{2,34}... | collective-permute-start | bytes 294920 | tf_op jit(solution)/shard_map/ppermute | solution.py:255

commit v8 on v6

--- a/solution.py
+++ b/solution.py
@@ -20,28 +20,51 @@
     return pltpu.with_memory_space_constraint(value, pltpu.HBM)
 
 
-def gather_body(blocks_ref, feat_ref, out_ref, sem):
-    count = out_ref.shape[0]
-
-    def start(r, carry):
-        pltpu.make_async_copy(feat_ref.at[blocks_ref[0, r]], out_ref.at[r], sem).start()
-        return carry
-
-    lax.fori_loop(0, count, start, 0, unroll=8)
-    pltpu.make_async_copy(feat_ref.at[pl.ds(0, count)], out_ref, sem).wait()
+def gather_body(blocks_ref, feat_ref, out_hbm, rows_ref, in_sem, out_sem):
+    count = rows_ref.shape[0]
+    part = count // 4
+
+    def quarter(q):
+        def start(r, carry):
+            row = q * part + r
+            pltpu.make_async_copy(feat_ref.at[blocks_ref[0, row]], rows_ref.at[row], in_sem.at[q]).start()
+            return carry
+
+        lax.fori_loop(0, part, start, 0, unroll=16)
+
+    def store(q):
+        rows = pl.ds(q * part, part)
+        pltpu.make_async_copy(feat_ref.at[pl.ds(0, part)], rows_ref.at[rows], in_sem.at[q]).wait()
+        copy = pltpu.make_async_copy(rows_ref.at[rows], out_hbm.at[rows], out_sem.at[q])
+        copy.start()
+        return copy
+
+    quarter(0)
+    quarter(1)
+    stores = [store(0)]
+    quarter(2)
+    stores.append(store(1))
+    quarter(3)
+    stores += [store(2), store(3)]
+    for copy in stores:
+        copy.wait()
 
 
 def gather_self(blocks, feat):
-    count = blocks.shape[1]
+    shape = (blocks.shape[1],) + feat.shape[1:]
     return pl.pallas_call(
         gather_body,
-        out_shape=jax.ShapeDtypeStruct((count,) + feat.shape[1:], feat.dtype),
+        out_shape=jax.ShapeDtypeStruct(shape, feat.dtype),
         grid_spec=pltpu.PrefetchScalarGridSpec(
             num_scalar_prefetch=1,
             grid=(1,),
             in_specs=[pl.BlockSpec(memory_space=pl.ANY)],
-            out_specs=pl.BlockSpec((count,) + feat.shape[1:], lambda i, b: (0, 0, 0)),
-            scratch_shapes=[pltpu.SemaphoreType.DMA(())],
+            out_specs=pl.BlockSpec(memory_space=pl.ANY),
+            scratch_shapes=[
+                pltpu.VMEM(shape, feat.dtype),
+                pltpu.SemaphoreType.DMA((4,)),
+                pltpu.SemaphoreType.DMA((4,)),
+            ],
         ),
         compiler_params=pltpu.CompilerParams(vmem_limit_bytes=56 * MIB),
         name="gather_self",

time: 111 us -> 112 us (level)
  no operation moved by 1% of the time
where the time goes in v8:
time: 112 us; the launch traced here: 111 us
  Pallas kernels  37.2 us (33%)
  waiting for transfers between devices  28.4 us (25%)
  blocking collectives  26.1 us (23%)
  starting transfers between devices  17.5 us (16%)
  other arithmetic  1.33 us (1%)
    all_to_all x1, blocking collectives, per_device(): pieces = lax.all_to_all(pair, ('x', 'y'), 0, 0, tiled=True)  26.1 us
    all_to_all x1, waiting for transfers between devices, per_device(): own_agg = lax.all_to_all(agg, FEAT, 0, 0, tiled=True)  17.3 us
    pallas_call x1, Pallas kernels, aggregate_tiles(): pl.pallas_call(functools.partial(aggregate_body, unroll), out_shape=jax.S...  16.7 us
    all_to_all x1, starting transfers between devices, per_device(): own_self = lax.all_to_all(mine, FEAT, 0, 0, tiled=True)  7.41 us
    pallas_call x1, Pallas kernels, dense_rest(): pl.pallas_call(dense_rest_body, out_shape=(pltpu.HBM((nodes, hid), BF), p...  7.07 us
    all_to_all x1, waiting for transfers between devices, per_device(): own_self = lax.all_to_all(mine, FEAT, 0, 0, tiled=True)  6.41 us
    ppermute x3, starting transfers between devices, shift(): return lax.ppermute(value, axis, [(i, (i + k) % 4) for i in range(4)])  5.98 us
    pallas_call x1, Pallas kernels, dense_self(): pl.pallas_call(dense_self_body, out_shape=(pltpu.HBM((sources * width, ow...  5.78 us
  transfers between devices with their start and end apart: 6, of which 6 were waited for; matrix products, arithmetic and copies ran while one was open for 0% of the time, Pallas kernels for 23%

profile of v8, /device:TPU:0, one launch (start us, length us, event | category | flops | bytes accessed | tf_op | source)
XLA Modules:
  0.0 111.2 jit_solution(550623761954062684)
XLA Ops:
  0.6 4.2 %gather_self.1 = bf16[256,24,128]{2,1,0:T(8,128)(2,1)} custom-call(s32[1,256]{1,0:T(1,128)} %blocks_ref.1, bf16[768,24,128]{2,1,0:T(8,128)(2,1)} %bitcast.10), custom_call_target="tpu_custom_call" | custom-call | tf_op jit(solution)/shard_map/gather_self/pallas_call | solution.py:55
  4.8 7.4 %all-to-all-start.1 = ((bf16[256,24,128]{2,1,0:T(8,128)(2,1)}), bf16[256,24,128]{2,1,0:T(8,128)(2,1)S(1)}, u32[]{:S(2)}, u32[]{:S(2)}) async-start(bf16[256,24,128]{2,1,0:T(8,128)(2,1)} %gather_self.1), calls=%async_computation.1 | async-start | bytes 3145728 | tf_op jit(solution)/shard_map/all_to_all | solution.py:314
  12.3 16.7 %aggregate_tiles.1 = bf16[256,24,128]{2,1,0:T(8,128)(2,1)} custom-call(s32[1,384]{1,0:T(1,128)} %rows_ref.1, s32[1,384]{1,0:T(1,128)} %cols_ref.1, bf16[768,24,128]{2,1,0:T(8,128)(2,1)} %bitcast.11, bf16[384,128,128]{2,1,0:T(8,128)(2,1)} %bitcast.12), custom_call_target="tpu_custom_call" | custom-call | flops 301989888 | bytes 18874368 | tf_op jit(solution)/shard_map/aggregate_tiles/pallas_call | solution.py:113
  29.0 6.4 %all-to-all-done.1 = bf16[256,24,128]{2,1,0:T(8,128)(2,1)S(1)} async-done(((bf16[256,24,128]{2,1,0:T(8,128)(2,1)}), bf16[256,24,128]{2,1,0:T(8,128)(2,1)S(1)}, u32[]{:S(2)}, u32[]{:S(2)}) %all-to-all-start.1) | async-done | bytes 1572896 | tf_op jit(solution)/shard_map/all_to_all | solution.py:314
  35.4 4.0 %all-to-all-start = ((bf16[256,24,128]{2,1,0:T(8,128)(2,1)}), bf16[256,24,128]{2,1,0:T(8,128)(2,1)S(1)}, u32[]{:S(2)}, u32[]{:S(2)}) async-start(bf16[256,24,128]{2,1,0:T(8,128)(2,1)} %aggregate_tiles.1), calls=%async_computation | async-start | bytes 3145728 | tf_op jit(solution)/shard_map/all_to_all | solution.py:316
  39.4 5.8 %dense_self.1 = (bf16[768,1024]{1,0:T(8,128)(2,1)}, f32[1024,1024]{1,0:T(8,128)}) custom-call(bf16[32,8,24,128]{3,2,1,0:T(8,128)(2,1)S(1)} %bitcast.9, bf16[1536,1024]{1,0:T(8,128)(2,1)} %weight_hbm.1, f32[1,1024]{1,0:T(1,128)} %bitcast.14), custom_call_target="tpu_custom_call" | custom-call | tf_op jit(solution)/shard_map/dense_self/pallas_call | solution.py:162
  45.2 17.3 %all-to-all-done = bf16[256,24,128]{2,1,0:T(8,128)(2,1)S(1)} async-done(((bf16[256,24,128]{2,1,0:T(8,128)(2,1)}), bf16[256,24,128]{2,1,0:T(8,128)(2,1)S(1)}, u32[]{:S(2)}, u32[]{:S(2)}) %all-to-all-start) | async-done | bytes 1572896 | tf_op jit(solution)/shard_map/all_to_all | solution.py:316
  62.5 7.1 %dense_rest.1 = (bf16[1024,1024]{1,0:T(8,128)(2,1)}, bf16[768,1024]{1,0:T(8,128)(2,1)S(1)}, bf16[1024,1024]{1,0:T(8,128)(2,1)S(1)}, bf16[16,48,1024]{2,1,0:T(8,128)(2,1)S(1)}) custom-call(s32[1]{0:T(128)} %bitcast.core_ref, bf16[32,8,24,128]{3,2,1,0:T(8,128)(2,1)S(1)} %bitcast.8, bf16[768,1024]{1,0:T(8,128)(2,1)} %get-tuple-element.12.comb_self_hbm, ...), custom_call_target="tpu_custom_call" | custom-call | tf_op jit(solution)/shard_map/dense_rest/pallas_call | solution.py:237
  69.6 0.1 collective-permute-start
  69.6 3.2 %dense_keep.1 = f32[16,48,1024]{2,1,0:T(8,128)S(1)} custom-call(s32[1]{0:T(128)} %bitcast.core_ref, bf16[768,1024]{1,0:T(8,128)(2,1)} %get-tuple-element.12.comb_self_hbm, bf16[768,1024]{1,0:T(8,128)(2,1)S(1)} %get-tuple-element.15.comb_ref, bf16[1024,1024]{1,0:T(8,128)(2,1)S(1)} %get-tuple-element.16.grad_ref), custom_call_target="tpu_custom_call" | custom-call | tf_op jit(solution)/shard_map/dense_keep/pallas_call | solution.py:272
  72.9 0.2 collective-permute-done
  73.0 0.6 add_convert_fusion
  73.6 26.1 %all_to_all.15.pieces_ref = bf16[16,48,1024]{2,1,0:T(8,128)(2,1)S(1)} all-to-all(bf16[16,48,1024]{2,1,0:T(8,128)(2,1)S(1)} %add_convert_fusion), channel_id=1, replica_groups=mesh['grp'=4,'x'=4,'y'=4,'core'=2] {'x','y'}, dimensions={0} | all-to-all | bytes 3145728 | tf_op jit(solution)/shard_map/all_to_all | solution.py:326
  99.8 0.2 sum_pieces.1
  100.0 4.0 %collective-permute-start.3 = (bf16[48,1024]{1,0:T(8,128)(2,1)S(1)}, bf16[48,1024]{1,0:T(8,128)(2,1)S(1)}, u32[]{:S(2)}, u32[]{:S(2)}) collective-permute-start(bf16[48,1024]{1,0:T(8,128)(2,1)S(1)} %sum_pieces.1), channel_id=1, source_target_pairs={{0,64},{32,96},{64,0},{96,32},{1,65},{33,97},{65,1},{97,33},{2,66}... | collective-permute-start | bytes 294920 | tf_op jit(solution)/shard_map/ppermute | solution.py:300
  103.9 0.7 collective-permute-start.2
  104.6 1.3 %collective-permute-start.1 = (bf16[48,1024]{1,0:T(8,128)(2,1)S(1)}, bf16[48,1024]{1,0:T(8,128)(2,1)S(1)}, u32[]{:S(2)}, u32[]{:S(2)}) collective-permute-start(bf16[48,1024]{1,0:T(8,128)(2,1)S(1)} %sum_pieces.1), channel_id=1, source_target_pairs={{0,32},{32,64},{64,96},{96,0},{1,33},{33,65},{65,97},{97,1},{2,34}... | collective-permute-start | bytes 294920 | tf_op jit(solution)/shard_map/ppermute | solution.py:300
  105.9 1.4 %collective-permute-done.3 = bf16[48,1024]{1,0:T(8,128)(2,1)S(1)} collective-permute-done((bf16[48,1024]{1,0:T(8,128)(2,1)S(1)}, bf16[48,1024]{1,0:T(8,128)(2,1)S(1)}, u32[]{:S(2)}, u32[]{:S(2)}) %collective-permute-start.3) | collective-permute-done | bytes 98336 | tf_op jit(solution)/shard_map/ppermute | solution.py:300
  107.4 1.2 %collective-permute-done.2 = bf16[48,1024]{1,0:T(8,128)(2,1)S(1)} collective-permute-done((bf16[48,1024]{1,0:T(8,128)(2,1)S(1)}, bf16[48,1024]{1,0:T(8,128)(2,1)S(1)}, u32[]{:S(2)}, u32[]{:S(2)}) %collective-permute-start.2) | collective-permute-done | bytes 98336 | tf_op jit(solution)/shard_map/ppermute | solution.py:300
  108.6 1.9 %collective-permute-done.1 = bf16[48,1024]{1,0:T(8,128)(2,1)S(1)} collective-permute-done((bf16[48,1024]{1,0:T(8,128)(2,1)S(1)}, bf16[48,1024]{1,0:T(8,128)(2,1)S(1)}, u32[]{:S(2)}, u32[]{:S(2)}) %collective-permute-start.1) | collective-permute-done | bytes 98336 | tf_op jit(solution)/shard_map/ppermute | solution.py:300
  110.5 0.7 fusion.1
Async XLA Ops:
  4.8 30.5 %all-to-all-start.1 = ((bf16[256,24,128]{2,1,0:T(8,128)(2,1)}), bf16[256,24,128]{2,1,0:T(8,128)(2,1)S(1)}, u32[]{:S(2)}, u32[]{:S(2)}) async-start(bf16[256,24,128]{2,1,0:T(8,128)(2,1)} %gather_self.1), calls=%async_computation.1 | async-start | bytes 3145728 | tf_op jit(solution)/shard_map/all_to_all | solution.py:314
  35.4 27.1 %all-to-all-start = ((bf16[256,24,128]{2,1,0:T(8,128)(2,1)}), bf16[256,24,128]{2,1,0:T(8,128)(2,1)S(1)}, u32[]{:S(2)}, u32[]{:S(2)}) async-start(bf16[256,24,128]{2,1,0:T(8,128)(2,1)} %aggregate_tiles.1), calls=%async_computation | async-start | bytes 3145728 | tf_op jit(solution)/shard_map/all_to_all | solution.py:316
  69.6 3.5 %collective-permute-start = (bf16[16,48,1024]{2,1,0:T(8,128)(2,1)S(1)}, bf16[16,48,1024]{2,1,0:T(8,128)(2,1)S(1)}, u32[]{:S(2)}, u32[]{:S(2)}) collective-permute-start(bf16[16,48,1024]{2,1,0:T(8,128)(2,1)S(1)} %get-tuple-element.17), channel_id=1, source_target_pairs={{0,1},{1,0},{2,3},{3,2},{4,5},{5,4},{6,7},{7,6},{8,9},{9,8},{10,11... | collective-permute-start | bytes 4718600 | tf_op jit(solution)/shard_map/ppermute | solution.py:323
  100.0 7.4 %collective-permute-start.3 = (bf16[48,1024]{1,0:T(8,128)(2,1)S(1)}, bf16[48,1024]{1,0:T(8,128)(2,1)S(1)}, u32[]{:S(2)}, u32[]{:S(2)}) collective-permute-start(bf16[48,1024]{1,0:T(8,128)(2,1)S(1)} %sum_pieces.1), channel_id=1, source_target_pairs={{0,64},{32,96},{64,0},{96,32},{1,65},{33,97},{65,1},{97,33},{2,66}... | collective-permute-start | bytes 294920 | tf_op jit(solution)/shard_map/ppermute | solution.py:300
  103.9 4.7 %collective-permute-start.2 = (bf16[48,1024]{1,0:T(8,128)(2,1)S(1)}, bf16[48,1024]{1,0:T(8,128)(2,1)S(1)}, u32[]{:S(2)}, u32[]{:S(2)}) collective-permute-start(bf16[48,1024]{1,0:T(8,128)(2,1)S(1)} %sum_pieces.1), channel_id=1, source_target_pairs={{0,96},{32,0},{64,32},{96,64},{1,97},{33,1},{65,33},{97,65},{2,98}... | collective-permute-start | bytes 294920 | tf_op jit(solution)/shard_map/ppermute | solution.py:300
  104.6 5.8 %collective-permute-start.1 = (bf16[48,1024]{1,0:T(8,128)(2,1)S(1)}, bf16[48,1024]{1,0:T(8,128)(2,1)S(1)}, u32[]{:S(2)}, u32[]{:S(2)}) collective-permute-start(bf16[48,1024]{1,0:T(8,128)(2,1)S(1)} %sum_pieces.1), channel_id=1, source_target_pairs={{0,32},{32,64},{64,96},{96,0},{1,33},{33,65},{65,97},{97,1},{2,34}... | collective-permute-start | bytes 294920 | tf_op jit(solution)/shard_map/ppermute | solution.py:300

commit v9 on v6

--- a/solution.py
+++ b/solution.py
@@ -155,35 +155,31 @@
     comb_self_ref, pre_ref, weight_ref, cot_ref, hidden_ref, sem,
 ):
     half, nodes = comb_ref.shape
-    chunk = nodes // 2
-    chunks = [pl.ds(m * chunk, chunk) for m in range(2)]
-    sources = [(weight_hbm.at[pl.ds(half, half)], weight_ref)]
-    for rows in chunks:
-        sources.append((pre_hbm.at[rows], pre_ref.at[rows]))
-        sources.append((cot_hbm.at[rows], cot_ref.at[rows]))
-    sources.append((comb_self_hbm, comb_self_ref))
+    sources = [
+        (weight_hbm.at[pl.ds(half, half)], weight_ref),
+        (pre_hbm, pre_ref),
+        (cot_hbm, cot_ref),
+        (comb_self_hbm, comb_self_ref),
+    ]
     loads = [pltpu.make_async_copy(a, b, sem.at[i]) for i, (a, b) in enumerate(sources)]
     for load in loads:
         load.start()
     stack_channels(agg_ref, comb_ref)
     loads[0].wait()
-    stores = []
-    for m, rows in enumerate(chunks):
-        part = lax.dot_general(
-            comb_ref[:, rows], weight_ref[...], (((0,), (0,)), ((), ())), preferred_element_type=F32
-        )
-        loads[1 + 2 * m].wait()
-        loads[2 + 2 * m].wait()
-        pre = pre_ref[rows, :] + part
-        decay = jnp.exp(jnp.minimum(pre, 0.0))
-        hidden_ref[rows, :] = jnp.where(pre > 0, pre, decay - 1.0).astype(BF)
-        grad_ref[rows, :] = (cot_ref[rows, :].astype(F32) * decay).astype(BF)
-        stores.append(pltpu.make_async_copy(hidden_ref.at[rows], hidden_hbm.at[rows], sem.at[6 + m]))
-        stores[m].start()
-    loads[5].wait()
+    part = lax.dot_general(
+        comb_ref[...], weight_ref[...], (((0,), (0,)), ((), ())), preferred_element_type=F32
+    )
+    loads[1].wait()
+    loads[2].wait()
+    pre = pre_ref[...] + part
+    decay = jnp.exp(jnp.minimum(pre, 0.0))
+    hidden_ref[...] = jnp.where(pre > 0, pre, decay - 1.0).astype(BF)
+    grad_ref[...] = (cot_ref[...].astype(F32) * decay).astype(BF)
+    store = pltpu.make_async_copy(hidden_ref, hidden_hbm, sem.at[4])
+    store.start()
+    loads[3].wait()
     weight_terms(1 - core_ref[0], comb_self_ref, comb_ref, grad_ref, send_ref)
-    for store in stores:
-        store.wait()
+    store.wait()
 
 
 def weight_terms(dest, comb_self_ref, comb_ref, grad_ref, out_ref):
@@ -228,7 +224,7 @@
             pltpu.VMEM((half, hid), BF),
             pltpu.VMEM((nodes, hid), BF),
             pltpu.VMEM((nodes, hid), BF),
-            pltpu.SemaphoreType.DMA((8,)),
+            pltpu.SemaphoreType.DMA((5,)),
         ],
         compiler_params=pltpu.CompilerParams(vmem_limit_bytes=24 * MIB),
         name="dense_rest",

time: 111 us -> 111 us (level)
  no operation moved by 1% of the time
where the time goes in v9:
time: 111 us; the launch traced here: 110 us
  Pallas kernels  36.1 us (33%)
  waiting for transfers between devices  28.4 us (26%)
  blocking collectives  26.1 us (24%)
  starting transfers between devices  17.5 us (16%)
  other arithmetic  1.33 us (1%)
    all_to_all x1, blocking collectives, per_device(): pieces = lax.all_to_all(pair, ('x', 'y'), 0, 0, tiled=True)  26.1 us
    all_to_all x1, waiting for transfers between devices, per_device(): own_agg = lax.all_to_all(agg, FEAT, 0, 0, tiled=True)  17.3 us
    pallas_call x1, Pallas kernels, aggregate_tiles(): pl.pallas_call(functools.partial(aggregate_body, unroll), out_shape=jax.S...  16.7 us
    all_to_all x1, starting transfers between devices, per_device(): own_self = lax.all_to_all(mine, FEAT, 0, 0, tiled=True)  7.41 us
    pallas_call x1, Pallas kernels, dense_rest(): pl.pallas_call(dense_rest_body, out_shape=(pltpu.HBM((nodes, hid), BF), p...  6.49 us
    all_to_all x1, waiting for transfers between devices, per_device(): own_self = lax.all_to_all(mine, FEAT, 0, 0, tiled=True)  6.41 us
    ppermute x3, starting transfers between devices, shift(): return lax.ppermute(value, axis, [(i, (i + k) % 4) for i in range(4)])  5.98 us
    pallas_call x1, Pallas kernels, dense_self(): pl.pallas_call(dense_self_body, out_shape=(pltpu.HBM((sources * width, ow...  5.78 us
  transfers between devices with their start and end apart: 6, of which 6 were waited for; matrix products, arithmetic and copies ran while one was open for 0% of the time, Pallas kernels for 23%

profile of v9, /device:TPU:0, one launch (start us, length us, event | category | flops | bytes accessed | tf_op | source)
XLA Modules:
  0.0 110.1 jit_solution(1540849005774122719)
XLA Ops:
  0.6 3.7 %gather_self.1 = bf16[256,24,128]{2,1,0:T(8,128)(2,1)} custom-call(s32[1,256]{1,0:T(1,128)} %blocks_ref.1, bf16[768,24,128]{2,1,0:T(8,128)(2,1)} %bitcast.10), custom_call_target="tpu_custom_call" | custom-call | tf_op jit(solution)/shard_map/gather_self/pallas_call | solution.py:36
  4.3 7.4 %all-to-all-start.1 = ((bf16[256,24,128]{2,1,0:T(8,128)(2,1)}), bf16[256,24,128]{2,1,0:T(8,128)(2,1)S(1)}, u32[]{:S(2)}, u32[]{:S(2)}) async-start(bf16[256,24,128]{2,1,0:T(8,128)(2,1)} %gather_self.1), calls=%async_computation.1 | async-start | bytes 3145728 | tf_op jit(solution)/shard_map/all_to_all | solution.py:287
  11.8 16.7 %aggregate_tiles.1 = bf16[256,24,128]{2,1,0:T(8,128)(2,1)} custom-call(s32[1,384]{1,0:T(1,128)} %rows_ref.1, s32[1,384]{1,0:T(1,128)} %cols_ref.1, bf16[768,24,128]{2,1,0:T(8,128)(2,1)} %bitcast.11, bf16[384,128,128]{2,1,0:T(8,128)(2,1)} %bitcast.12), custom_call_target="tpu_custom_call" | custom-call | flops 301989888 | bytes 18874368 | tf_op jit(solution)/shard_map/aggregate_tiles/pallas_call | solution.py:90
  28.5 6.4 %all-to-all-done.1 = bf16[256,24,128]{2,1,0:T(8,128)(2,1)S(1)} async-done(((bf16[256,24,128]{2,1,0:T(8,128)(2,1)}), bf16[256,24,128]{2,1,0:T(8,128)(2,1)S(1)}, u32[]{:S(2)}, u32[]{:S(2)}) %all-to-all-start.1) | async-done | bytes 1572896 | tf_op jit(solution)/shard_map/all_to_all | solution.py:287
  34.9 4.0 %all-to-all-start = ((bf16[256,24,128]{2,1,0:T(8,128)(2,1)}), bf16[256,24,128]{2,1,0:T(8,128)(2,1)S(1)}, u32[]{:S(2)}, u32[]{:S(2)}) async-start(bf16[256,24,128]{2,1,0:T(8,128)(2,1)} %aggregate_tiles.1), calls=%async_computation | async-start | bytes 3145728 | tf_op jit(solution)/shard_map/all_to_all | solution.py:289
  38.9 5.8 %dense_self.1 = (bf16[768,1024]{1,0:T(8,128)(2,1)}, f32[1024,1024]{1,0:T(8,128)}) custom-call(bf16[32,8,24,128]{3,2,1,0:T(8,128)(2,1)S(1)} %bitcast.9, bf16[1536,1024]{1,0:T(8,128)(2,1)} %weight_hbm.1, f32[1,1024]{1,0:T(1,128)} %bitcast.14), custom_call_target="tpu_custom_call" | custom-call | tf_op jit(solution)/shard_map/dense_self/pallas_call | solution.py:139
  44.7 17.3 %all-to-all-done = bf16[256,24,128]{2,1,0:T(8,128)(2,1)S(1)} async-done(((bf16[256,24,128]{2,1,0:T(8,128)(2,1)}), bf16[256,24,128]{2,1,0:T(8,128)(2,1)S(1)}, u32[]{:S(2)}, u32[]{:S(2)}) %all-to-all-start) | async-done | bytes 1572896 | tf_op jit(solution)/shard_map/all_to_all | solution.py:289
  62.0 6.5 %dense_rest.1 = (bf16[1024,1024]{1,0:T(8,128)(2,1)}, bf16[768,1024]{1,0:T(8,128)(2,1)S(1)}, bf16[1024,1024]{1,0:T(8,128)(2,1)S(1)}, bf16[16,48,1024]{2,1,0:T(8,128)(2,1)S(1)}) custom-call(s32[1]{0:T(128)} %bitcast.core_ref, bf16[32,8,24,128]{3,2,1,0:T(8,128)(2,1)S(1)} %bitcast.8, bf16[768,1024]{1,0:T(8,128)(2,1)} %get-tuple-element.12.comb_self_hbm, ...), custom_call_target="tpu_custom_call" | custom-call | tf_op jit(solution)/shard_map/dense_rest/pallas_call | solution.py:210
  68.5 0.1 collective-permute-start
  68.6 3.2 %dense_keep.1 = f32[16,48,1024]{2,1,0:T(8,128)S(1)} custom-call(s32[1]{0:T(128)} %bitcast.core_ref, bf16[768,1024]{1,0:T(8,128)(2,1)} %get-tuple-element.12.comb_self_hbm, bf16[768,1024]{1,0:T(8,128)(2,1)S(1)} %get-tuple-element.15.comb_ref, bf16[1024,1024]{1,0:T(8,128)(2,1)S(1)} %get-tuple-element.16.grad_ref), custom_call_target="tpu_custom_call" | custom-call | tf_op jit(solution)/shard_map/dense_keep/pallas_call | solution.py:245
  71.8 0.2 collective-permute-done
  72.0 0.6 add_convert_fusion
  72.6 26.1 %all_to_all.15.pieces_ref = bf16[16,48,1024]{2,1,0:T(8,128)(2,1)S(1)} all-to-all(bf16[16,48,1024]{2,1,0:T(8,128)(2,1)S(1)} %add_convert_fusion), channel_id=1, replica_groups=mesh['grp'=4,'x'=4,'y'=4,'core'=2] {'x','y'}, dimensions={0} | all-to-all | bytes 3145728 | tf_op jit(solution)/shard_map/all_to_all | solution.py:299
  98.7 0.2 sum_pieces.1
  98.9 4.0 %collective-permute-start.3 = (bf16[48,1024]{1,0:T(8,128)(2,1)S(1)}, bf16[48,1024]{1,0:T(8,128)(2,1)S(1)}, u32[]{:S(2)}, u32[]{:S(2)}) collective-permute-start(bf16[48,1024]{1,0:T(8,128)(2,1)S(1)} %sum_pieces.1), channel_id=1, source_target_pairs={{0,64},{32,96},{64,0},{96,32},{1,65},{33,97},{65,1},{97,33},{2,66}... | collective-permute-start | bytes 294920 | tf_op jit(solution)/shard_map/ppermute | solution.py:273
  102.9 0.7 collective-permute-start.2
  103.6 1.3 %collective-permute-start.1 = (bf16[48,1024]{1,0:T(8,128)(2,1)S(1)}, bf16[48,1024]{1,0:T(8,128)(2,1)S(1)}, u32[]{:S(2)}, u32[]{:S(2)}) collective-permute-start(bf16[48,1024]{1,0:T(8,128)(2,1)S(1)} %sum_pieces.1), channel_id=1, source_target_pairs={{0,32},{32,64},{64,96},{96,0},{1,33},{33,65},{65,97},{97,1},{2,34}... | collective-permute-start | bytes 294920 | tf_op jit(solution)/shard_map/ppermute | solution.py:273
  104.9 1.4 %collective-permute-done.3 = bf16[48,1024]{1,0:T(8,128)(2,1)S(1)} collective-permute-done((bf16[48,1024]{1,0:T(8,128)(2,1)S(1)}, bf16[48,1024]{1,0:T(8,128)(2,1)S(1)}, u32[]{:S(2)}, u32[]{:S(2)}) %collective-permute-start.3) | collective-permute-done | bytes 98336 | tf_op jit(solution)/shard_map/ppermute | solution.py:273
  106.3 1.2 %collective-permute-done.2 = bf16[48,1024]{1,0:T(8,128)(2,1)S(1)} collective-permute-done((bf16[48,1024]{1,0:T(8,128)(2,1)S(1)}, bf16[48,1024]{1,0:T(8,128)(2,1)S(1)}, u32[]{:S(2)}, u32[]{:S(2)}) %collective-permute-start.2) | collective-permute-done | bytes 98336 | tf_op jit(solution)/shard_map/ppermute | solution.py:273
  107.5 1.9 %collective-permute-done.1 = bf16[48,1024]{1,0:T(8,128)(2,1)S(1)} collective-permute-done((bf16[48,1024]{1,0:T(8,128)(2,1)S(1)}, bf16[48,1024]{1,0:T(8,128)(2,1)S(1)}, u32[]{:S(2)}, u32[]{:S(2)}) %collective-permute-start.1) | collective-permute-done | bytes 98336 | tf_op jit(solution)/shard_map/ppermute | solution.py:273
  109.4 0.7 fusion.1
Async XLA Ops:
  4.3 30.5 %all-to-all-start.1 = ((bf16[256,24,128]{2,1,0:T(8,128)(2,1)}), bf16[256,24,128]{2,1,0:T(8,128)(2,1)S(1)}, u32[]{:S(2)}, u32[]{:S(2)}) async-start(bf16[256,24,128]{2,1,0:T(8,128)(2,1)} %gather_self.1), calls=%async_computation.1 | async-start | bytes 3145728 | tf_op jit(solution)/shard_map/all_to_all | solution.py:287
  34.9 27.1 %all-to-all-start = ((bf16[256,24,128]{2,1,0:T(8,128)(2,1)}), bf16[256,24,128]{2,1,0:T(8,128)(2,1)S(1)}, u32[]{:S(2)}, u32[]{:S(2)}) async-start(bf16[256,24,128]{2,1,0:T(8,128)(2,1)} %aggregate_tiles.1), calls=%async_computation | async-start | bytes 3145728 | tf_op jit(solution)/shard_map/all_to_all | solution.py:289
  68.5 3.5 %collective-permute-start = (bf16[16,48,1024]{2,1,0:T(8,128)(2,1)S(1)}, bf16[16,48,1024]{2,1,0:T(8,128)(2,1)S(1)}, u32[]{:S(2)}, u32[]{:S(2)}) collective-permute-start(bf16[16,48,1024]{2,1,0:T(8,128)(2,1)S(1)} %get-tuple-element.17), channel_id=1, source_target_pairs={{0,1},{1,0},{2,3},{3,2},{4,5},{5,4},{6,7},{7,6},{8,9},{9,8},{10,11... | collective-permute-start | bytes 4718600 | tf_op jit(solution)/shard_map/ppermute | solution.py:296
  98.9 7.4 %collective-permute-start.3 = (bf16[48,1024]{1,0:T(8,128)(2,1)S(1)}, bf16[48,1024]{1,0:T(8,128)(2,1)S(1)}, u32[]{:S(2)}, u32[]{:S(2)}) collective-permute-start(bf16[48,1024]{1,0:T(8,128)(2,1)S(1)} %sum_pieces.1), channel_id=1, source_target_pairs={{0,64},{32,96},{64,0},{96,32},{1,65},{33,97},{65,1},{97,33},{2,66}... | collective-permute-start | bytes 294920 | tf_op jit(solution)/shard_map/ppermute | solution.py:273
  102.9 4.7 %collective-permute-start.2 = (bf16[48,1024]{1,0:T(8,128)(2,1)S(1)}, bf16[48,1024]{1,0:T(8,128)(2,1)S(1)}, u32[]{:S(2)}, u32[]{:S(2)}) collective-permute-start(bf16[48,1024]{1,0:T(8,128)(2,1)S(1)} %sum_pieces.1), channel_id=1, source_target_pairs={{0,96},{32,0},{64,32},{96,64},{1,97},{33,1},{65,33},{97,65},{2,98}... | collective-permute-start | bytes 294920 | tf_op jit(solution)/shard_map/ppermute | solution.py:273
  103.6 5.8 %collective-permute-start.1 = (bf16[48,1024]{1,0:T(8,128)(2,1)S(1)}, bf16[48,1024]{1,0:T(8,128)(2,1)S(1)}, u32[]{:S(2)}, u32[]{:S(2)}) collective-permute-start(bf16[48,1024]{1,0:T(8,128)(2,1)S(1)} %sum_pieces.1), channel_id=1, source_target_pairs={{0,32},{32,64},{64,96},{96,0},{1,33},{33,65},{65,97},{97,1},{2,34}... | collective-permute-start | bytes 294920 | tf_op jit(solution)/shard_map/ppermute | solution.py:273

commit v10 on v9

--- a/solution.py
+++ b/solution.py
@@ -152,18 +152,19 @@
 def dense_rest_body(
     core_ref, agg_ref, comb_self_hbm, pre_hbm, weight_hbm, cot_hbm,
     hidden_hbm, comb_ref, grad_ref, send_ref,
-    comb_self_ref, pre_ref, weight_ref, cot_ref, hidden_ref, sem,
+    self_rows_ref, pre_ref, weight_ref, cot_ref, hidden_ref, sem,
 ):
     half, nodes = comb_ref.shape
     sources = [
         (weight_hbm.at[pl.ds(half, half)], weight_ref),
         (pre_hbm, pre_ref),
         (cot_hbm, cot_ref),
-        (comb_self_hbm, comb_self_ref),
     ]
     loads = [pltpu.make_async_copy(a, b, sem.at[i]) for i, (a, b) in enumerate(sources)]
     for load in loads:
         load.start()
+    dest = 1 - core_ref[0]
+    load_rows(dest, comb_self_hbm, self_rows_ref, sem.at[3])
     stack_channels(agg_ref, comb_ref)
     loads[0].wait()
     part = lax.dot_general(
@@ -177,17 +178,24 @@
     grad_ref[...] = (cot_ref[...].astype(F32) * decay).astype(BF)
     store = pltpu.make_async_copy(hidden_ref, hidden_hbm, sem.at[4])
     store.start()
-    loads[3].wait()
-    weight_terms(1 - core_ref[0], comb_self_ref, comb_ref, grad_ref, send_ref)
+    pltpu.make_async_copy(comb_self_hbm.at[pl.ds(0, half // 2)], self_rows_ref, sem.at[3]).wait()
+    weight_terms(dest, self_rows_ref, comb_ref, grad_ref, send_ref)
     store.wait()
 
 
-def weight_terms(dest, comb_self_ref, comb_ref, grad_ref, out_ref):
+def load_rows(dest, comb_hbm, rows_ref, sem):
+    share = comb_hbm.shape[0] // 16
+    for b in range(8):
+        rows = pl.ds(pl.multiple_of((2 * b + dest) * share, share), share)
+        pltpu.make_async_copy(comb_hbm.at[rows], rows_ref.at[pl.ds(b * share, share)], sem).start()
+
+
+def weight_terms(dest, self_rows_ref, comb_ref, grad_ref, out_ref):
     blocks, share, hid = out_ref.shape
     lhs = jnp.concatenate(
-        [
-            source[pl.ds(pl.multiple_of((2 * b + dest) * share, share), share), :]
-            for source in (comb_self_ref, comb_ref)
+        [self_rows_ref[...]]
+        + [
+            comb_ref[pl.ds(pl.multiple_of((2 * b + dest) * share, share), share), :]
             for b in range(blocks // 2)
         ],
         axis=0,
@@ -219,7 +227,7 @@
         + [pl.BlockSpec(memory_space=pl.ANY)] * 4,
         out_specs=(pl.BlockSpec(memory_space=pl.ANY),) + (vmem,) * 3,
         scratch_shapes=[
-            pltpu.VMEM((half, nodes), BF),
+            pltpu.VMEM((half // 2, nodes), BF),
             pltpu.VMEM((nodes, hid), F32),
             pltpu.VMEM((half, hid), BF),
             pltpu.VMEM((nodes, hid), BF),
@@ -231,11 +239,11 @@
     )(core, in_vmem(own_agg), *map(in_hbm, (comb_self, pre, weight, cot)))
 
 
-def dense_keep_body(core_ref, comb_self_hbm, comb_ref, grad_ref, keep_ref, comb_self_ref, sem):
-    load = pltpu.make_async_copy(comb_self_hbm, comb_self_ref, sem)
-    load.start()
-    load.wait()
-    weight_terms(core_ref[0], comb_self_ref, comb_ref, grad_ref, keep_ref)
+def dense_keep_body(core_ref, comb_self_hbm, comb_ref, grad_ref, keep_ref, self_rows_ref, sem):
+    load_rows(core_ref[0], comb_self_hbm, self_rows_ref, sem)
+    count = self_rows_ref.shape[0]
+    pltpu.make_async_copy(comb_self_hbm.at[pl.ds(0, count)], self_rows_ref, sem).wait()
+    weight_terms(core_ref[0], self_rows_ref, comb_ref, grad_ref, keep_ref)
 
 
 def dense_keep(core, comb_self, comb_agg, grad):
@@ -247,7 +255,7 @@
         out_shape=pltpu.VMEM(pieces_of(half, hid), F32),
         in_specs=[pl.BlockSpec(memory_space=pltpu.SMEM), pl.BlockSpec(memory_space=pl.ANY), vmem, vmem],
         out_specs=vmem,
-        scratch_shapes=[pltpu.VMEM((half, nodes), BF), pltpu.SemaphoreType.DMA(())],
+        scratch_shapes=[pltpu.VMEM((half // 2, nodes), BF), pltpu.SemaphoreType.DMA(())],
         compiler_params=pltpu.CompilerParams(vmem_limit_bytes=16 * MIB),
         name="dense_keep",
     )(core, in_hbm(comb_self), in_vmem(comb_agg), in_vmem(grad))

time: 111 us -> 110 us (level)
  no operation moved by 1% of the time
where the time goes in v10:
time: 110 us
  Pallas kernels  35.9 us (33%)
  waiting for transfers between devices  28.6 us (26%)
  blocking collectives  25.9 us (24%)
  starting transfers between devices  17.5 us (16%)
  other arithmetic  1.33 us (1%)
    all_to_all x1, blocking collectives, per_device(): pieces = lax.all_to_all(pair, ('x', 'y'), 0, 0, tiled=True)  25.9 us
    all_to_all x1, waiting for transfers between devices, per_device(): own_agg = lax.all_to_all(agg, FEAT, 0, 0, tiled=True)  17.3 us
    pallas_call x1, Pallas kernels, aggregate_tiles(): pl.pallas_call(functools.partial(aggregate_body, unroll), out_shape=jax.S...  16.7 us
    all_to_all x1, starting transfers between devices, per_device(): own_self = lax.all_to_all(mine, FEAT, 0, 0, tiled=True)  7.41 us
    pallas_call x1, Pallas kernels, dense_rest(): pl.pallas_call(dense_rest_body, out_shape=(pltpu.HBM((nodes, hid), BF), p...  6.49 us
    all_to_all x1, waiting for transfers between devices, per_device(): own_self = lax.all_to_all(mine, FEAT, 0, 0, tiled=True)  6.41 us
    ppermute x3, starting transfers between devices, shift(): return lax.ppermute(value, axis, [(i, (i + k) % 4) for i in range(4)])  5.98 us
    pallas_call x1, Pallas kernels, dense_self(): pl.pallas_call(dense_self_body, out_shape=(pltpu.HBM((sources * width, ow...  5.78 us
  transfers between devices with their start and end apart: 6, of which 6 were waited for; matrix products, arithmetic and copies ran while one was open for 0% of the time, Pallas kernels for 23%

profile of v10, /device:TPU:0, one launch (start us, length us, event | category | flops | bytes accessed | tf_op | source)
XLA Modules:
  0.0 110.0 jit_solution(13942856645259766508)
XLA Ops:
  0.6 3.7 %gather_self.1 = bf16[256,24,128]{2,1,0:T(8,128)(2,1)} custom-call(s32[1,256]{1,0:T(1,128)} %blocks_ref.1, bf16[768,24,128]{2,1,0:T(8,128)(2,1)} %bitcast.10), custom_call_target="tpu_custom_call" | custom-call | tf_op jit(solution)/shard_map/gather_self/pallas_call | solution.py:36
  4.3 7.4 %all-to-all-start.1 = ((bf16[256,24,128]{2,1,0:T(8,128)(2,1)}), bf16[256,24,128]{2,1,0:T(8,128)(2,1)S(1)}, u32[]{:S(2)}, u32[]{:S(2)}) async-start(bf16[256,24,128]{2,1,0:T(8,128)(2,1)} %gather_self.1), calls=%async_computation.1 | async-start | bytes 3145728 | tf_op jit(solution)/shard_map/all_to_all | solution.py:295
  11.8 16.7 %aggregate_tiles.1 = bf16[256,24,128]{2,1,0:T(8,128)(2,1)} custom-call(s32[1,384]{1,0:T(1,128)} %rows_ref.1, s32[1,384]{1,0:T(1,128)} %cols_ref.1, bf16[768,24,128]{2,1,0:T(8,128)(2,1)} %bitcast.11, bf16[384,128,128]{2,1,0:T(8,128)(2,1)} %bitcast.12), custom_call_target="tpu_custom_call" | custom-call | flops 301989888 | bytes 18874368 | tf_op jit(solution)/shard_map/aggregate_tiles/pallas_call | solution.py:90
  28.5 6.4 %all-to-all-done.1 = bf16[256,24,128]{2,1,0:T(8,128)(2,1)S(1)} async-done(((bf16[256,24,128]{2,1,0:T(8,128)(2,1)}), bf16[256,24,128]{2,1,0:T(8,128)(2,1)S(1)}, u32[]{:S(2)}, u32[]{:S(2)}) %all-to-all-start.1) | async-done | bytes 1572896 | tf_op jit(solution)/shard_map/all_to_all | solution.py:295
  34.9 4.0 %all-to-all-start = ((bf16[256,24,128]{2,1,0:T(8,128)(2,1)}), bf16[256,24,128]{2,1,0:T(8,128)(2,1)S(1)}, u32[]{:S(2)}, u32[]{:S(2)}) async-start(bf16[256,24,128]{2,1,0:T(8,128)(2,1)} %aggregate_tiles.1), calls=%async_computation | async-start | bytes 3145728 | tf_op jit(solution)/shard_map/all_to_all | solution.py:297
  38.9 5.8 %dense_self.1 = (bf16[768,1024]{1,0:T(8,128)(2,1)}, f32[1024,1024]{1,0:T(8,128)}) custom-call(bf16[32,8,24,128]{3,2,1,0:T(8,128)(2,1)S(1)} %bitcast.9, bf16[1536,1024]{1,0:T(8,128)(2,1)} %weight_hbm.1, f32[1,1024]{1,0:T(1,128)} %bitcast.14), custom_call_target="tpu_custom_call" | custom-call | tf_op jit(solution)/shard_map/dense_self/pallas_call | solution.py:139
  44.7 17.3 %all-to-all-done = bf16[256,24,128]{2,1,0:T(8,128)(2,1)S(1)} async-done(((bf16[256,24,128]{2,1,0:T(8,128)(2,1)}), bf16[256,24,128]{2,1,0:T(8,128)(2,1)S(1)}, u32[]{:S(2)}, u32[]{:S(2)}) %all-to-all-start) | async-done | bytes 1572896 | tf_op jit(solution)/shard_map/all_to_all | solution.py:297
  62.0 6.5 %dense_rest.1 = (bf16[1024,1024]{1,0:T(8,128)(2,1)}, bf16[768,1024]{1,0:T(8,128)(2,1)S(1)}, bf16[1024,1024]{1,0:T(8,128)(2,1)S(1)}, bf16[16,48,1024]{2,1,0:T(8,128)(2,1)S(1)}) custom-call(s32[1]{0:T(128)} %bitcast.core_ref, bf16[32,8,24,128]{3,2,1,0:T(8,128)(2,1)S(1)} %bitcast.8, bf16[768,1024]{1,0:T(8,128)(2,1)} %get-tuple-element.12.comb_self_hbm, ...), custom_call_target="tpu_custom_call" | custom-call | tf_op jit(solution)/shard_map/dense_rest/pallas_call | solution.py:218
  68.5 0.1 collective-permute-start
  68.6 3.0 %dense_keep.1 = f32[16,48,1024]{2,1,0:T(8,128)S(1)} custom-call(s32[1]{0:T(128)} %bitcast.core_ref, bf16[768,1024]{1,0:T(8,128)(2,1)} %get-tuple-element.12.comb_self_hbm, bf16[768,1024]{1,0:T(8,128)(2,1)S(1)} %get-tuple-element.15.comb_ref, bf16[1024,1024]{1,0:T(8,128)(2,1)S(1)} %get-tuple-element.16.grad_ref), custom_call_target="tpu_custom_call" | custom-call | tf_op jit(solution)/shard_map/dense_keep/pallas_call | solution.py:253
  71.6 0.4 collective-permute-done
  72.0 0.6 add_convert_fusion
  72.6 25.9 %all_to_all.15.pieces_ref = bf16[16,48,1024]{2,1,0:T(8,128)(2,1)S(1)} all-to-all(bf16[16,48,1024]{2,1,0:T(8,128)(2,1)S(1)} %add_convert_fusion), channel_id=1, replica_groups=mesh['grp'=4,'x'=4,'y'=4,'core'=2] {'x','y'}, dimensions={0} | all-to-all | bytes 3145728 | tf_op jit(solution)/shard_map/all_to_all | solution.py:307
  98.5 0.2 sum_pieces.1
  98.7 4.0 %collective-permute-start.3 = (bf16[48,1024]{1,0:T(8,128)(2,1)S(1)}, bf16[48,1024]{1,0:T(8,128)(2,1)S(1)}, u32[]{:S(2)}, u32[]{:S(2)}) collective-permute-start(bf16[48,1024]{1,0:T(8,128)(2,1)S(1)} %sum_pieces.1), channel_id=1, source_target_pairs={{0,64},{32,96},{64,0},{96,32},{1,65},{33,97},{65,1},{97,33},{2,66}... | collective-permute-start | bytes 294920 | tf_op jit(solution)/shard_map/ppermute | solution.py:281
  102.7 0.7 collective-permute-start.2
  103.4 1.3 %collective-permute-start.1 = (bf16[48,1024]{1,0:T(8,128)(2,1)S(1)}, bf16[48,1024]{1,0:T(8,128)(2,1)S(1)}, u32[]{:S(2)}, u32[]{:S(2)}) collective-permute-start(bf16[48,1024]{1,0:T(8,128)(2,1)S(1)} %sum_pieces.1), channel_id=1, source_target_pairs={{0,32},{32,64},{64,96},{96,0},{1,33},{33,65},{65,97},{97,1},{2,34}... | collective-permute-start | bytes 294920 | tf_op jit(solution)/shard_map/ppermute | solution.py:281
  104.7 1.3 %collective-permute-done.3 = bf16[48,1024]{1,0:T(8,128)(2,1)S(1)} collective-permute-done((bf16[48,1024]{1,0:T(8,128)(2,1)S(1)}, bf16[48,1024]{1,0:T(8,128)(2,1)S(1)}, u32[]{:S(2)}, u32[]{:S(2)}) %collective-permute-start.3) | collective-permute-done | bytes 98336 | tf_op jit(solution)/shard_map/ppermute | solution.py:281
  106.0 1.3 %collective-permute-done.2 = bf16[48,1024]{1,0:T(8,128)(2,1)S(1)} collective-permute-done((bf16[48,1024]{1,0:T(8,128)(2,1)S(1)}, bf16[48,1024]{1,0:T(8,128)(2,1)S(1)}, u32[]{:S(2)}, u32[]{:S(2)}) %collective-permute-start.2) | collective-permute-done | bytes 98336 | tf_op jit(solution)/shard_map/ppermute | solution.py:281
  107.3 1.9 %collective-permute-done.1 = bf16[48,1024]{1,0:T(8,128)(2,1)S(1)} collective-permute-done((bf16[48,1024]{1,0:T(8,128)(2,1)S(1)}, bf16[48,1024]{1,0:T(8,128)(2,1)S(1)}, u32[]{:S(2)}, u32[]{:S(2)}) %collective-permute-start.1) | collective-permute-done | bytes 98336 | tf_op jit(solution)/shard_map/ppermute | solution.py:281
  109.2 0.7 fusion.1
Async XLA Ops:
  4.3 30.5 %all-to-all-start.1 = ((bf16[256,24,128]{2,1,0:T(8,128)(2,1)}), bf16[256,24,128]{2,1,0:T(8,128)(2,1)S(1)}, u32[]{:S(2)}, u32[]{:S(2)}) async-start(bf16[256,24,128]{2,1,0:T(8,128)(2,1)} %gather_self.1), calls=%async_computation.1 | async-start | bytes 3145728 | tf_op jit(solution)/shard_map/all_to_all | solution.py:295
  34.9 27.1 %all-to-all-start = ((bf16[256,24,128]{2,1,0:T(8,128)(2,1)}), bf16[256,24,128]{2,1,0:T(8,128)(2,1)S(1)}, u32[]{:S(2)}, u32[]{:S(2)}) async-start(bf16[256,24,128]{2,1,0:T(8,128)(2,1)} %aggregate_tiles.1), calls=%async_computation | async-start | bytes 3145728 | tf_op jit(solution)/shard_map/all_to_all | solution.py:297
  68.5 3.5 %collective-permute-start = (bf16[16,48,1024]{2,1,0:T(8,128)(2,1)S(1)}, bf16[16,48,1024]{2,1,0:T(8,128)(2,1)S(1)}, u32[]{:S(2)}, u32[]{:S(2)}) collective-permute-start(bf16[16,48,1024]{2,1,0:T(8,128)(2,1)S(1)} %get-tuple-element.17), channel_id=1, source_target_pairs={{0,1},{1,0},{2,3},{3,2},{4,5},{5,4},{6,7},{7,6},{8,9},{9,8},{10,11... | collective-permute-start | bytes 4718600 | tf_op jit(solution)/shard_map/ppermute | solution.py:304
  98.7 7.3 %collective-permute-start.3 = (bf16[48,1024]{1,0:T(8,128)(2,1)S(1)}, bf16[48,1024]{1,0:T(8,128)(2,1)S(1)}, u32[]{:S(2)}, u32[]{:S(2)}) collective-permute-start(bf16[48,1024]{1,0:T(8,128)(2,1)S(1)} %sum_pieces.1), channel_id=1, source_target_pairs={{0,64},{32,96},{64,0},{96,32},{1,65},{33,97},{65,1},{97,33},{2,66}... | collective-permute-start | bytes 294920 | tf_op jit(solution)/shard_map/ppermute | solution.py:281
  102.7 4.7 %collective-permute-start.2 = (bf16[48,1024]{1,0:T(8,128)(2,1)S(1)}, bf16[48,1024]{1,0:T(8,128)(2,1)S(1)}, u32[]{:S(2)}, u32[]{:S(2)}) collective-permute-start(bf16[48,1024]{1,0:T(8,128)(2,1)S(1)} %sum_pieces.1), channel_id=1, source_target_pairs={{0,96},{32,0},{64,32},{96,64},{1,97},{33,1},{65,33},{97,65},{2,98}... | collective-permute-start | bytes 294920 | tf_op jit(solution)/shard_map/ppermute | solution.py:281
  103.4 5.8 %collective-permute-start.1 = (bf16[48,1024]{1,0:T(8,128)(2,1)S(1)}, bf16[48,1024]{1,0:T(8,128)(2,1)S(1)}, u32[]{:S(2)}, u32[]{:S(2)}) collective-permute-start(bf16[48,1024]{1,0:T(8,128)(2,1)S(1)} %sum_pieces.1), channel_id=1, source_target_pairs={{0,32},{32,64},{64,96},{96,0},{1,33},{33,65},{65,97},{97,1},{2,34}... | collective-permute-start | bytes 294920 | tf_op jit(solution)/shard_map/ppermute | solution.py:281
